TPU v7x, 128 devices: a whole 4x4x4 slice. The times are simulated.
128 devices in a mesh: rows: 16 (over y, x), cols: 8 (over z, core).
Axes of the slice: x: 4, y: 4, z: 4, core: 2. Of those that a mesh axis runs over, the one named last changes fastest.
Arguments:
- affiliations: float32 [131072, 512], P(('rows', 'cols')), as said below
- tile_block: int32 [128, 240], P(('rows', 'cols')), may hold values from 0 to 1023, as said below
- tile_target: int32 [128, 240], P(('rows', 'cols')), may hold values from 0 to 7
- tile_pattern: int32 [128, 240], P(('rows', 'cols')), may hold values from 0 to 191
- tile_count: int32 [128], P(('rows', 'cols')), may hold values from 15 to 240, as said below
- block_home: int32 [1024], replicated, may hold values from 0 to 1023, as said below
- patterns: int32 [192, 5, 128], replicated, may hold values from 0 to 1073741823, as said below
Outputs:
- updated_affiliations: float32 [131072, 512], P(('rows', 'cols'))
Inputs may be any that keep to these rules, and one draw needn't show every extreme that they name: Live tiles of a device are the first tile_count of its slots, in order of their neighbour's owner row (storage block // 64); some device has exactly 240. `tile_block`: A live tile's neighbour is stored on a device of the same cols index and another rows index; a device's live tiles name at most 4 distinct blocks of one owner row, and in every draw some device names exactly 4 of every other owner row; a (target, neighbour) pair is live at most once on a device; slots past the count hold valid block numbers. `block_home`: A permutation of the node blocks. `patterns`: bits at rows 128 and beyond are zero. `affiliations`: Positive.
All inputs are finite; a program needn't handle non-finite values.
Results may differ from a plain program's by a relative error of at most 0.0003.
Values may be sent and summed in bfloat16 or wider, within the bound.
No kernel may reach another device: no remote copies, remote signals or barrier semaphores. Data moves between devices by JAX's collectives and lax.ppermute only.
A program may use at most 192 MiB of HBM per device.

v0:
```python
import functools

import jax
import jax.numpy as jnp
from jax import lax
from jax.experimental import pallas as pl
from jax.experimental.pallas import tpu as pltpu
from jax.sharding import Mesh
from jax.sharding import PartitionSpec as P

C = 512
BLOCK = 128
STEPS = 2
BPD = 8
SIDE = 4
CAP = 4
N_COLS = 8
NODES = 131072
UNIT = 1572864
PATTERNS = 192
TILES = 240
PARTS = 6
GROUP = (4, 4, 4, 4, 4, 2)
KEYS = PARTS * BPD
SLOTS = TILES + sum(BPD * (g - 1) + 2 * g for g in GROUP) // 16 * 16 + 16
STARTS = SLOTS + SLOTS // 2
LIST = STARTS + 8
EMPTY = PATTERNS * 64
FLOOR = 0.001
STEP_SIZE = 0.3 / NODES
OWN_ROWS = BPD * BLOCK
SENT_ROWS = OWN_ROWS + 16
PICKED = SIDE * CAP
HALF_ROWS = OWN_ROWS // 2

ALL = ("rows_0", "rows_1", "cols_0", "cols_1")
VMEM = pl.BlockSpec(memory_space=pltpu.VMEM)
SMEM = pl.BlockSpec(memory_space=pltpu.SMEM)
HBM = pl.BlockSpec(memory_space=pltpu.HBM)


def pairs(first, second):
    out = []
    for y in range(SIDE):
        for x in range(SIDE):
            for z in range(4):
                for core in range(2):
                    dx, dy = (first, second) if core == 0 else (second, first)
                    sy, sx = (y + dy) % SIDE, (x + dx) % SIDE
                    out.append((((sy * 4 + sx) * 4 + z) * 2 + core, ((y * 4 + x) * 4 + z) * 2 + core))
    return out


def fetch(value, first, second):
    return lax.ppermute(value, ALL, pairs(first, second))


def swap(value, axis, step):
    return lax.ppermute(value, axis, [(i, i ^ step) for i in range(lax.axis_size(axis))])


OWNERS = (
    ((0, 1), (0, 3)),
    ((1, 0), (1, 1), (1, 3), (0, 2)),
    ((3, 0), (3, 1), (3, 3)),
    ((2, 0), (2, 1), (2, 3)),
    ((1, 2), (3, 2)),
    ((2, 2),),
)


def clear(ref, start, size, value):
    def body(i, _):
        for j in range(8):
            ref[start + 8 * i + j] = value
        return 0

    lax.fori_loop(0, size // 8, body, 0)


def ask_kernel(place, blocks, targets, count, home, requests, codes, rank, fill, base):
    first, second, core = place[0], place[1], place[2]
    clear(rank, 0, 128, -1)
    clear(fill, 0, 16, 0)
    clear(requests, 0, 64, 0)
    base[0] = 0
    for part, owners in enumerate(OWNERS):
        for i, (m, k) in enumerate(owners):
            base[m * SIDE + k] = part * 512 + i * CAP

    def note(t, _):
        slot = home[blocks[t]]
        row = slot >> 6
        local = slot & (BPD - 1)
        y, x = row >> 2, row & (SIDE - 1)
        owner_first = jnp.where(core == 0, x, y)
        owner_second = jnp.where(core == 0, y, x)
        k = (owner_first - first) & (SIDE - 1)
        m = (owner_second - second) & (SIDE - 1)
        pair = m * SIDE + k
        seen = rank[pair * BPD + local]
        held = fill[pair]
        mine = jnp.minimum(jnp.where(seen < 0, held, seen), CAP - 1)
        rank[pair * BPD + local] = mine
        fill[pair] = jnp.where(seen < 0, held + 1, held)
        requests[pair * CAP + mine] = local
        codes[t] = base[pair] + mine + targets[t] * 64
        return 0

    lax.fori_loop(0, count[0], note, 0)


def ask(place, blocks, targets, count, home):
    i32 = jnp.int32
    return pl.pallas_call(
        ask_kernel,
        out_shape=(jax.ShapeDtypeStruct((64,), i32), jax.ShapeDtypeStruct((TILES,), i32)),
        in_specs=[SMEM] * 5,
        out_specs=(SMEM,) * 2,
        scratch_shapes=[pltpu.SMEM((128,), i32), pltpu.SMEM((16,), i32), pltpu.SMEM((16,), i32)],
        compiler_params=pltpu.CompilerParams(vmem_limit_bytes=2 << 20),
        name="ask",
    )(place, blocks, targets, count, home)


def sort_kernel(codes, pattern_ids, count, lists, per_key):
    clear(per_key, 0, KEYS, 0)
    clear(lists, 0, SLOTS, EMPTY)
    clear(lists, SLOTS, SLOTS // 2, 0)

    def tally(t, _):
        key = codes[t] >> 6
        per_key[key] = per_key[key] + 1
        return 0

    lax.fori_loop(0, count[0], tally, 0)
    slot = jnp.int32(0)
    for part, size in enumerate(GROUP):
        lists[STARTS + part] = slot
        start = slot
        for target in range(BPD):
            key = part * BPD + target
            tiles = per_key[key]
            per_key[key] = slot
            slot = slot + ((tiles + size - 1) & -size)
        slot = start + jnp.maximum(2 * size, (slot - start + 2 * size - 1) & -(2 * size))
    lists[STARTS + PARTS] = slot

    def put(t, _):
        code = codes[t]
        key = code >> 6
        at = per_key[key]
        per_key[key] = at + 1
        lists[at] = pattern_ids[t] * 64 + (code & 63)
        lists[SLOTS + (at >> 1)] = key & (BPD - 1)
        return 0

    lax.fori_loop(0, count[0], put, 0)


def sort_tiles(codes, pattern_ids, count):
    i32 = jnp.int32
    return pl.pallas_call(
        sort_kernel,
        out_shape=jax.ShapeDtypeStruct((LIST,), i32),
        in_specs=[SMEM] * 3,
        out_specs=SMEM,
        scratch_shapes=[pltpu.SMEM((KEYS,), i32)],
        compiler_params=pltpu.CompilerParams(vmem_limit_bytes=2 << 20),
        name="sort_tiles",
    )(codes, pattern_ids, count)


def sum_rows(total):
    high = total.astype(jnp.bfloat16).astype(jnp.float32)
    rest = total - high
    middle = rest.astype(jnp.bfloat16).astype(jnp.float32)
    low = rest - middle
    row = lax.broadcasted_iota(jnp.int32, (16, C), 0)
    out = jnp.where(row == 0, high, jnp.where(row == 1, middle, jnp.where(row == 2, low, 0.0)))
    return out.astype(jnp.bfloat16)


def first_kernel(current, sent):
    total = jnp.zeros((8, C), jnp.float32)
    for j in range(BPD):
        rows = current[pl.ds(j * BLOCK, BLOCK), :]
        sent[pl.ds(j * BLOCK, BLOCK), :] = rows.astype(jnp.bfloat16)
        total = total + jnp.sum(rows.reshape(BLOCK // 8, 8, C), axis=0)
    sent[pl.ds(OWN_ROWS, 16), :] = sum_rows(jnp.sum(total, axis=0, keepdims=True))


def first(current):
    return pl.pallas_call(
        first_kernel,
        out_shape=jax.ShapeDtypeStruct((SENT_ROWS, C), jnp.bfloat16),
        in_specs=[VMEM],
        out_specs=VMEM,
        compiler_params=pltpu.CompilerParams(vmem_limit_bytes=20 << 20),
        name="first",
    )(current)


def move(table, local, out, at):
    rows = pl.ds(pl.multiple_of(local * BLOCK, BLOCK), BLOCK)
    out[pl.ds(at * BLOCK, BLOCK), :] = table[rows, :]


def pick_early_kernel(asked, wanted, own, far1, far3, near, pass1, pass3, out1, out3):
    pass1[...] = far1[pl.ds(0, HALF_ROWS), :]
    pass3[...] = far3[pl.ds(HALF_ROWS, HALF_ROWS + 16), :]
    for m, out in ((1, out1), (3, out3)):
        for i, (k, table) in enumerate(((0, own), (1, far1), (3, far3))):
            for r in range(CAP):
                move(table, asked[m - 1, k * CAP + r], out, i * CAP + r)
    for r in range(CAP):
        move(far1, wanted[CAP + r], near, r)
        move(far3, wanted[3 * CAP + r], near, CAP + r)


def pick_early(asked, wanted, own, far1, far3):
    b16 = jnp.bfloat16
    out = jax.ShapeDtypeStruct((3 * CAP * BLOCK, C), b16)
    return pl.pallas_call(
        pick_early_kernel,
        out_shape=(
            jax.ShapeDtypeStruct((2 * CAP * BLOCK, C), b16),
            jax.ShapeDtypeStruct((HALF_ROWS, C), b16),
            jax.ShapeDtypeStruct((HALF_ROWS + 16, C), b16),
            out,
            out,
        ),
        in_specs=[SMEM] * 2 + [VMEM] * 3,
        out_specs=(VMEM,) * 5,
        compiler_params=pltpu.CompilerParams(vmem_limit_bytes=20 << 20),
        name="pick_early",
    )(asked, wanted, own, far1, far3)


def pick_late_kernel(asked, wanted, own, far1, far3, low2, high2, near, out1, out3, out2a, out2b, line, far2):
    far2[pl.ds(0, HALF_ROWS), :] = low2[...]
    far2[pl.ds(HALF_ROWS, HALF_ROWS + 16), :] = high2[...]
    tables = ((0, own), (1, far1), (3, far3), (2, far2))
    for r in range(CAP):
        move(far2, asked[0, 2 * CAP + r], out1, r)
        move(far2, asked[2, 2 * CAP + r], out3, r)
        move(far2, wanted[2 * CAP + r], near, r)
    for i, (k, table) in enumerate(tables):
        for r in range(CAP):
            out, at = (out2a, i) if i < 3 else (out2b, 0)
            move(table, asked[1, k * CAP + r], out, at * CAP + r)
    rows = sum(t[pl.ds(OWN_ROWS, 16), :].astype(jnp.float32) for _, t in tables)
    sums = jnp.sum(rows, axis=0, keepdims=True)
    line[...] = jnp.broadcast_to(sums, (8, C))


def pick_late(asked, wanted, own, far1, far3, low2, high2):
    b16 = jnp.bfloat16
    piece = jax.ShapeDtypeStruct((CAP * BLOCK, C), b16)
    return pl.pallas_call(
        pick_late_kernel,
        out_shape=(
            piece,
            piece,
            piece,
            jax.ShapeDtypeStruct((3 * CAP * BLOCK, C), b16),
            piece,
            jax.ShapeDtypeStruct((8, C), jnp.float32),
        ),
        in_specs=[SMEM] * 2 + [VMEM] * 5,
        out_specs=(VMEM,) * 6,
        scratch_shapes=[pltpu.VMEM((SENT_ROWS, C), b16)],
        compiler_params=pltpu.CompilerParams(vmem_limit_bytes=20 << 20),
        name="pick_late",
    )(asked, wanted, own, far1, far3, low2, high2)


def tile_kernel(part, table_count, resume, finish, *refs):
    refs = list(refs)
    lists, words, own = refs[:3]
    tables = refs[3 : 3 + table_count]
    refs = refs[3 + table_count :]
    if resume:
        earlier = refs.pop(0)
    if finish:
        current, all_sums, fresh = refs[:3]
        refs = refs[3:]
        if finish == "more":
            sent = refs.pop(0)
    if finish == "end":
        ready, sems = refs[:2]
        refs = refs[2:]
    total, score_a, score_b, bits = refs[:4]

    row = lax.broadcasted_iota(jnp.int32, (BLOCK, BLOCK), 0)
    bits[...] = lax.shift_left(jnp.ones_like(row), lax.rem(row, 30))
    total[...] = earlier[...] if resume else jnp.zeros_like(total)
    sub = lax.broadcasted_iota(jnp.int32, (8, BLOCK), 0)
    if table_count == 1:
        held = tables[0]
    else:
        held = refs[4]
        at = 0
        for table in tables:
            held[pl.ds(at, table.shape[0]), :] = table[...]
            at += table.shape[0]

    def rows_of(index):
        return pl.ds(pl.multiple_of(index * BLOCK, BLOCK), BLOCK)

    def word_rows(pattern):
        rows = []
        for v in range(BLOCK // 8):
            low, high = 8 * v // 30, (8 * v + 7) // 30
            chunk = jnp.broadcast_to(words[pattern, low : low + 1, :], (8, BLOCK))
            if high != low:
                other = jnp.broadcast_to(words[pattern, high : high + 1, :], (8, BLOCK))
                chunk = jnp.where(sub + 8 * v < 30 * high, chunk, other)
            rows.append(chunk)
        return jnp.concatenate(rows, axis=0)

    size = GROUP[part]

    def target(slot):
        return rows_of(lists[SLOTS + (slot >> 1)])

    def remote(slot, i):
        return held[rows_of(lists[slot + i] & 63), :]

    def score(slot, out):
        mine = own[target(slot), :]
        for i in range(size):
            out[:, i * BLOCK : (i + 1) * BLOCK] = lax.dot_general(
                mine,
                remote(slot, i),
                (((1,), (1,)), ((), ())),
                preferred_element_type=jnp.float32,
            )

    def add(slot, scores):
        weights = []
        for i in range(size):
            packed = word_rows(lists[slot + i] >> 6)
            negative = jnp.minimum(scores[:, i * BLOCK : (i + 1) * BLOCK] * (-1.0 / UNIT), -FLOOR)
            weight = 1.0 / (1.0 - jnp.exp(negative))
            linked = (packed & bits[...]) != 0
            weights.append(jnp.where(linked, weight, 0.0).astype(jnp.bfloat16))
        total[target(slot), :] += jnp.dot(
            jnp.concatenate(weights, axis=1),
            jnp.concatenate([remote(slot, i) for i in range(size)], axis=0),
            preferred_element_type=jnp.float32,
        )

    start, stop = lists[STARTS + part], lists[STARTS + part + 1]
    score(start, score_a)

    def two(i, _):
        slot = pl.multiple_of(start + 2 * size * i, size)
        score(slot + size, score_b)
        add(slot, score_a)
        score(jnp.minimum(slot + 2 * size, stop - size), score_a)
        add(slot + size, score_b)
        return 0

    lax.fori_loop(0, lax.shift_right_logical(stop - start, size.bit_length()), two, 0)

    if not finish:
        return
    col_sums = all_sums[0:1, :]
    moved_sums = jnp.zeros((8, C), jnp.float32)
    copies = []
    for j in range(BPD):
        at = pl.ds(j * BLOCK, BLOCK)
        moved = jnp.maximum(current[at, :] + STEP_SIZE * (total[at, :] - col_sums), 0.0)
        if finish == "more":
            fresh[at, :] = moved
            sent[at, :] = moved.astype(jnp.bfloat16)
            moved_sums = moved_sums + jnp.sum(moved.reshape(BLOCK // 8, 8, C), axis=0)
        else:
            ready[at, :] = moved
            copies.append(pltpu.make_async_copy(ready.at[at, :], fresh.at[at, :], sems.at[j]))
            copies[j].start()
    if finish == "more":
        sent[pl.ds(OWN_ROWS, 16), :] = sum_rows(jnp.sum(moved_sums, axis=0, keepdims=True))
    for copy in copies:
        copy.wait()


def run_tiles(name, part, lists, words, own, tables, earlier=None, current=None, sums=None, finish=""):
    f32 = jnp.float32
    blocks = jax.ShapeDtypeStruct((OWN_ROWS, C), f32)
    args = [lists, words, own, *tables]
    specs = [SMEM] + [VMEM] * (2 + len(tables))
    scratch = []
    out = [blocks]
    if earlier is not None:
        args.append(earlier)
        specs.append(VMEM)
    if finish:
        args += [current, sums]
        specs += [VMEM] * 2
        if finish == "end":
            scratch += [pltpu.VMEM((OWN_ROWS, C), f32), pltpu.SemaphoreType.DMA((BPD,))]
        scratch.append(pltpu.VMEM((OWN_ROWS, C), f32))
        if finish == "more":
            out.append(jax.ShapeDtypeStruct((SENT_ROWS, C), jnp.bfloat16))
    scratch += [
        pltpu.VMEM((BLOCK, GROUP[part] * BLOCK), f32),
        pltpu.VMEM((BLOCK, GROUP[part] * BLOCK), f32),
        pltpu.VMEM((BLOCK, BLOCK), jnp.int32),
    ]
    if len(tables) > 1:
        scratch.append(pltpu.VMEM((sum(t.shape[0] for t in tables), C), jnp.bfloat16))
    return pl.pallas_call(
        functools.partial(tile_kernel, part, len(tables), earlier is not None, finish),
        out_shape=tuple(out),
        in_specs=specs,
        out_specs=(HBM,) if finish == "end" else (VMEM,) * len(out),
        scratch_shapes=scratch,
        compiler_params=pltpu.CompilerParams(vmem_limit_bytes=24 << 20),
        name=name,
    )(*args)


def per_device(affiliations, tile_block, tile_target, tile_pattern, tile_count, block_home, patterns):
    y, x = lax.axis_index("rows_0"), lax.axis_index("rows_1")
    core = lax.axis_index("cols_1")
    place = jnp.stack([jnp.where(core == 0, x, y), jnp.where(core == 0, y, x), core])
    current = affiliations
    own = first(current)
    requests, codes = ask(
        place.astype(jnp.int32), tile_block[0], tile_target[0], tile_count, block_home
    )
    requests = requests.reshape(SIDE, PICKED)
    asked = jnp.stack([fetch(requests[m], 0, SIDE - m) for m in (1, 2, 3)])
    words = jnp.concatenate([patterns, jnp.zeros((1, *patterns.shape[1:]), jnp.int32)], axis=0)

    lists = sort_tiles(codes, tile_pattern[0], tile_count)
    for step in range(STEPS):
        far1, far3 = fetch(own, 1, 0), fetch(own, 3, 0)
        near, pass1, pass3, out1, out3 = pick_early(asked, requests[0], own, far1, far3)
        low2, high2 = fetch(pass1, 1, 0), fetch(pass3, 3, 0)
        side1, side3 = fetch(out1, 0, 1), fetch(out3, 0, 3)
        (total,) = run_tiles("near", 0, lists, words, own, (near,))
        total, low2, high2 = lax.optimization_barrier((total, low2, high2))
        near, out1, out3, out2a, out2b, line = pick_late(asked, requests[0], own, far1, far3, low2, high2)
        lines = tuple(fetch(line, 0, m) for m in (1, 3, 2))
        lines, out2a, out2b, side1, side3 = lax.optimization_barrier(
            (lines, out2a, out2b, side1, side3)
        )
        side2a, side2b = fetch(out2a, 0, 2), fetch(out2b, 0, 2)
        late1, late3 = fetch(out1, 0, 1), fetch(out3, 0, 3)
        sums = line + lines[0] + lines[1] + lines[2]
        other = swap(sums, "cols_1", 1)
        (total,) = run_tiles("sides_1", 1, lists, words, own, (side1, near), total)
        total, other = lax.optimization_barrier((total, other))
        sums = sums + other
        other = swap(sums, "cols_0", 1)
        (total,) = run_tiles("sides_3", 2, lists, words, own, (side3,), total)
        total, other = lax.optimization_barrier((total, other))
        sums = sums + other
        other = swap(sums, "cols_0", 2)
        (total,) = run_tiles("across", 3, lists, words, own, (side2a,), total)
        total, other, late1, late3 = lax.optimization_barrier((total, other, late1, late3))
        col_sums = sums + other
        (total,) = run_tiles("late", 4, lists, words, own, (late1, late3), total)
        total, side2b = lax.optimization_barrier((total, side2b))
        finish = "more" if step < STEPS - 1 else "end"
        current, *own_next = run_tiles(
            "last", 5, lists, words, own, (side2b,), total, current, col_sums, finish
        )
        if own_next:
            (own,) = own_next
    return current


def solution(mesh):
    torus = Mesh(mesh.devices.reshape(4, 4, 4, 2), ALL)
    return jax.shard_map(
        per_device,
        mesh=torus,
        in_specs=(P(ALL, None), P(ALL, None), P(ALL, None), P(ALL, None), P(ALL), P(), P()),
        out_specs=P(ALL, None),
        check_vma=False,
    )
```

profile of v0, /device:TPU:32, one launch (start us, length us, event | category | flops | bytes accessed | tf_op | source)
XLA Modules:
  0.0 166.5 jit_solution(11944182112305481054)
XLA Ops:
  0.0 1.6 copy-done
  1.7 1.6 collective-permute-start.4
  3.3 1.7 %collective-permute-start.3 = (bf16[1040,512]{1,0:T(8,128)(2,1)S(1)}, bf16[1040,512]{1,0:T(8,128)(2,1)S(1)}, u32[]{:S(2)}, u32[]{:S(2)}) collective-permute-start(bf16[1040,512]{1,0:T(8,128)(2,1)S(1)} %first.1.own.refs_2_), channel_id=1, source_target_pairs={{8,0},{33,1},{10,2},{35,3},{12,4},{37,5},{14,6},{39,7},{16,8},{41,... | collective-permute-start | bytes 3194888 | tf_op jit(solution)/shard_map/ppermute | solution.py:55
  5.8 3.3 %ask.1 = (s32[64]{0:T(128)S(1)}, s32[240]{0:T(256)S(1)}) custom-call(s32[3]{0:T(128)S(1)} %pad_add_fusion.1.place, s32[240]{0:T(256)S(1)} %bitcast.9, s32[240]{0:T(256)S(1)} %bitcast.10, s32[1]{0:T(128)S(6)} %copy.9.count, s32[1024]{0:T(1024)S(1)} %copy-done.2), custom_call_target="tpu_custom_call" | custom-call | tf_op jit(solution)/shard_map/ask/pallas_call | solution.py:115
  9.2 3.5 %collective-permute-start.2 = (s32[16]{0:T(128)S(1)}, s32[16]{0:T(128)S(1)}, u32[]{:S(2)}, u32[]{:S(2)}) collective-permute-start(s32[16]{0:T(128)S(1)} %get-tuple-element.138), channel_id=1, source_target_pairs={{32,0},{9,1},{34,2},{11,3},{36,4},{13,5},{38,6},{15,7},{40,8},{17,... | collective-permute-start | bytes 200 | tf_op jit(solution)/shard_map/ppermute | solution.py:55
  12.7 3.4 %collective-permute-start.1 = (s32[16]{0:T(128)S(1)}, s32[16]{0:T(128)S(1)}, u32[]{:S(2)}, u32[]{:S(2)}) collective-permute-start(s32[16]{0:T(128)S(1)} %get-tuple-element.139), channel_id=1, source_target_pairs={{64,0},{17,1},{66,2},{19,3},{68,4},{21,5},{70,6},{23,7},{72,8},{25... | collective-permute-start | bytes 200 | tf_op jit(solution)/shard_map/ppermute | solution.py:55
  16.1 1.7 %collective-permute-done.1 = s32[16]{0:T(128)S(1)} collective-permute-done((s32[16]{0:T(128)S(1)}, s32[16]{0:T(128)S(1)}, u32[]{:S(2)}, u32[]{:S(2)}) %collective-permute-start.1) | collective-permute-done | bytes 96 | tf_op jit(solution)/shard_map/ppermute | solution.py:55
  17.8 3.0 %collective-permute-done = s32[16]{0:T(128)S(1)} collective-permute-done((s32[16]{0:T(128)S(1)}, s32[16]{0:T(128)S(1)}, u32[]{:S(2)}, u32[]{:S(2)}) %collective-permute-start) | collective-permute-done | bytes 96 | tf_op jit(solution)/shard_map/ppermute | solution.py:55
  20.9 0.9 pick_early.2
  21.8 0.5 collective-permute-start.10
  22.3 1.6 collective-permute-start.11
  23.9 3.2 %collective-permute-start.5 = (bf16[512,512]{1,0:T(8,128)(2,1)S(1)}, bf16[512,512]{1,0:T(8,128)(2,1)S(1)}, u32[]{:S(2)}, u32[]{:S(2)}) collective-permute-start(bf16[512,512]{1,0:T(8,128)(2,1)S(1)} %get-tuple-element.74), channel_id=1, source_target_pairs={{8,0},{33,1},{10,2},{35,3},{12,4},{37,5},{14,6},{39,7},{16,8},{41,... | collective-permute-start | bytes 1572872 | tf_op jit(solution)/shard_map/ppermute | solution.py:55
  27.1 0.3 copy.8
  27.5 3.6 %sort_tiles.1.refs_0_ = s32[632]{0:T(1024)S(1)} custom-call(s32[240]{0:T(256)S(1)} %get-tuple-element.71.codes, s32[240]{0:T(256)S(1)} %bitcast.11, s32[1]{0:T(128)S(6)} %copy.9.count), custom_call_target="tpu_custom_call" | custom-call | tf_op jit(solution)/shard_map/sort_tiles/pallas_call | solution.py:163
  31.1 3.4 %near.2.refs_5_ = f32[1024,512]{1,0:T(8,128)S(1)} custom-call(s32[632]{0:T(1024)S(1)} %sort_tiles.1.refs_0_, s32[193,5,128]{2,1,0:T(8,128)S(1)} %concatenate.3.refs_1_, bf16[1040,512]{1,0:T(8,128)(2,1)S(1)} %first.1.own.refs_2_, bf16[1024,512]{1,0:T(8,128)(2,1)S(1)} %get-tuple-element.73.refs_3_), custom_call_target="tpu_custom_call" | custom-call | tf_op jit(solution)/shard_map/near/pallas_call | solution.py:414
  34.5 5.0 %collective-permute-done.5.low2 = bf16[512,512]{1,0:T(8,128)(2,1)S(1)} collective-permute-done((bf16[512,512]{1,0:T(8,128)(2,1)S(1)}, bf16[512,512]{1,0:T(8,128)(2,1)S(1)}, u32[]{:S(2)}, u32[]{:S(2)}) %collective-permute-start.5) | collective-permute-done | bytes 524320 | tf_op jit(solution)/shard_map/ppermute | solution.py:55
  39.5 0.8 collective-permute-done.6.high2
  40.3 0.9 pick_late.2
  41.2 0.7 collective-permute-start.9
  41.9 1.9 %collective-permute-start.8 = (f32[8,512]{1,0:T(8,128)S(1)}, f32[8,512]{1,0:T(8,128)S(1)}, u32[]{:S(2)}, u32[]{:S(2)}) collective-permute-start(f32[8,512]{1,0:T(8,128)S(1)} %get-tuple-element.78), channel_id=1, source_target_pairs={{96,0},{25,1},{98,2},{27,3},{100,4},{29,5},{102,6},{31,7},{104,8},... | collective-permute-start | bytes 49160 | tf_op jit(solution)/shard_map/ppermute | solution.py:55
  43.8 1.3 collective-permute-start.7
  45.1 3.3 %collective-permute-done.9 = f32[8,512]{1,0:T(8,128)S(1)} collective-permute-done((f32[8,512]{1,0:T(8,128)S(1)}, f32[8,512]{1,0:T(8,128)S(1)}, u32[]{:S(2)}, u32[]{:S(2)}) %collective-permute-start.9) | collective-permute-done | bytes 16416 | tf_op jit(solution)/shard_map/ppermute | solution.py:55
  48.4 0.8 collective-permute-start.12
  49.2 2.0 %collective-permute-start.16 = (bf16[512,512]{1,0:T(8,128)(2,1)S(1)}, bf16[512,512]{1,0:T(8,128)(2,1)S(1)}, u32[]{:S(2)}, u32[]{:S(2)}) collective-permute-start(bf16[512,512]{1,0:T(8,128)(2,1)S(1)} %get-tuple-element.95), channel_id=1, source_target_pairs={{32,0},{9,1},{34,2},{11,3},{36,4},{13,5},{38,6},{15,7},{40,8},{17,... | collective-permute-start | bytes 1572872 | tf_op jit(solution)/shard_map/ppermute | solution.py:55
  51.2 2.8 %collective-permute-start.18 = (bf16[512,512]{1,0:T(8,128)(2,1)S(1)}, bf16[512,512]{1,0:T(8,128)(2,1)S(1)}, u32[]{:S(2)}, u32[]{:S(2)}) collective-permute-start(bf16[512,512]{1,0:T(8,128)(2,1)S(1)} %get-tuple-element.100), channel_id=1, source_target_pairs={{64,0},{17,1},{66,2},{19,3},{68,4},{21,5},{70,6},{23,7},{72,8},{25... | collective-permute-start | bytes 1572872 | tf_op jit(solution)/shard_map/ppermute | solution.py:55
  54.1 3.5 %sides_1.2.refs_4_ = f32[1024,512]{1,0:T(8,128)S(1)} custom-call(s32[632]{0:T(1024)S(1)} %sort_tiles.1.refs_0_, s32[193,5,128]{2,1,0:T(8,128)S(1)} %concatenate.3.refs_1_, bf16[1040,512]{1,0:T(8,128)(2,1)S(1)} %first.1.own.refs_2_, bf16[1536,512]{1,0:T(8,128)(2,1)S(1)} %collective-permute-done.10.refs_3_, bf16[512,512]{1,0:T(8,128)(2,1)S(1)} %get-tuple-element.86.refs_4_, ...), custom_call_target="tpu_custom_call" | custom-call | tf_op jit(solution)/shard_map/sides_1/pallas_call | solution.py:414
  57.7 0.8 collective-permute-start.14
  58.4 3.6 %sides_3.2.refs_4_ = f32[1024,512]{1,0:T(8,128)S(1)} custom-call(s32[632]{0:T(1024)S(1)} %sort_tiles.1.refs_0_, s32[193,5,128]{2,1,0:T(8,128)S(1)} %concatenate.3.refs_1_, bf16[1040,512]{1,0:T(8,128)(2,1)S(1)} %first.1.own.refs_2_, bf16[1536,512]{1,0:T(8,128)(2,1)S(1)} %collective-permute-done.11.refs_3_, f32[1024,512]{1,0:T(8,128)S(1)} %sides_1.2.refs_4_), custom_call_target="tpu_custom_call" | custom-call | tf_op jit(solution)/shard_map/sides_3/pallas_call | solution.py:414
  62.0 4.0 %collective-permute-start.15 = (f32[8,512]{1,0:T(8,128)S(1)}, f32[8,512]{1,0:T(8,128)S(1)}, u32[]{:S(2)}, u32[]{:S(2)}) collective-permute-start(f32[8,512]{1,0:T(8,128)S(1)} %add.42), channel_id=1, source_target_pairs={{0,4},{2,6},{4,0},{6,2},{1,5},{3,7},{5,1},{7,3},{8,12},{10,14},{12... | collective-permute-start | bytes 49160 | tf_op jit(solution)/shard_map/ppermute | solution.py:59
  66.0 4.5 %collective-permute-done.12.refs_3_ = bf16[1536,512]{1,0:T(8,128)(2,1)S(1)} collective-permute-done((bf16[1536,512]{1,0:T(8,128)(2,1)S(1)}, bf16[1536,512]{1,0:T(8,128)(2,1)S(1)}, u32[]{:S(2)}, u32[]{:S(2)}) %collective-permute-start.12) | collective-permute-done | bytes 1572896 | tf_op jit(solution)/shard_map/ppermute | solution.py:55
  70.5 3.5 %across.2.refs_5_ = f32[1024,512]{1,0:T(8,128)S(1)} custom-call(s32[632]{0:T(1024)S(1)} %sort_tiles.1.refs_0_, s32[193,5,128]{2,1,0:T(8,128)S(1)} %concatenate.3.refs_1_, bf16[1040,512]{1,0:T(8,128)(2,1)S(1)} %first.1.own.refs_2_, bf16[1536,512]{1,0:T(8,128)(2,1)S(1)} %collective-permute-done.12.refs_3_, f32[1024,512]{1,0:T(8,128)S(1)} %sides_3.2.refs_4_), custom_call_target="tpu_custom_call" | custom-call | tf_op jit(solution)/shard_map/across/pallas_call | solution.py:414
  74.1 0.9 collective-permute-done.16.refs_3_
  75.0 1.0 collective-permute-done.17.refs_4_
  76.1 3.1 %late.2.refs_4_ = f32[1024,512]{1,0:T(8,128)S(1)} custom-call(s32[632]{0:T(1024)S(1)} %sort_tiles.1.refs_0_, s32[193,5,128]{2,1,0:T(8,128)S(1)} %concatenate.3.refs_1_, bf16[1040,512]{1,0:T(8,128)(2,1)S(1)} %first.1.own.refs_2_, bf16[512,512]{1,0:T(8,128)(2,1)S(1)} %collective-permute-done.16.refs_3_, bf16[512,512]{1,0:T(8,128)(2,1)S(1)} %collective-permute-done.17.refs_4_, ...), custom_call_target="tpu_custom_call" | custom-call | tf_op jit(solution)/shard_map/late/pallas_call | solution.py:414
  79.1 2.6 %collective-permute-done.18.refs_3_ = bf16[512,512]{1,0:T(8,128)(2,1)S(1)} collective-permute-done((bf16[512,512]{1,0:T(8,128)(2,1)S(1)}, bf16[512,512]{1,0:T(8,128)(2,1)S(1)}, u32[]{:S(2)}, u32[]{:S(2)}) %collective-permute-start.18) | collective-permute-done | bytes 524320 | tf_op jit(solution)/shard_map/ppermute | solution.py:55
  81.7 2.6 %last.2 = (f32[1024,512]{1,0:T(8,128)S(1)}, bf16[1040,512]{1,0:T(8,128)(2,1)S(1)}) custom-call(s32[632]{0:T(1024)S(1)} %sort_tiles.1.refs_0_, s32[193,5,128]{2,1,0:T(8,128)S(1)} %concatenate.3.refs_1_, bf16[1040,512]{1,0:T(8,128)(2,1)S(1)} %first.1.own.refs_2_, bf16[512,512]{1,0:T(8,128)(2,1)S(1)} %collective-permute-done.18.refs_3_, ...), custom_call_target="tpu_custom_call" | custom-call | tf_op jit(solution)/shard_map/last/pallas_call | solution.py:414
  84.3 0.3 collective-permute-start.20
  84.6 3.6 %collective-permute-start.19 = (bf16[1040,512]{1,0:T(8,128)(2,1)S(1)}, bf16[1040,512]{1,0:T(8,128)(2,1)S(1)}, u32[]{:S(2)}, u32[]{:S(2)}) collective-permute-start(bf16[1040,512]{1,0:T(8,128)(2,1)S(1)} %get-tuple-element.104.own.refs_2_), channel_id=1, source_target_pairs={{8,0},{33,1},{10,2},{35,3},{12,4},{37,5},{14,6},{39,7},{16,8},{41,... | collective-permute-start | bytes 3194888 | tf_op jit(solution)/shard_map/ppermute | solution.py:55
  88.2 12.9 %collective-permute-done.20.far3 = bf16[1040,512]{1,0:T(8,128)(2,1)S(1)} collective-permute-done((bf16[1040,512]{1,0:T(8,128)(2,1)S(1)}, bf16[1040,512]{1,0:T(8,128)(2,1)S(1)}, u32[]{:S(2)}, u32[]{:S(2)}) %collective-permute-start.20) | collective-permute-done | bytes 1064992 | tf_op jit(solution)/shard_map/ppermute | solution.py:55
  101.0 1.2 collective-permute-done.19.far1
  102.2 0.9 pick_early.3
  103.1 0.4 collective-permute-start.26
  103.5 1.7 %collective-permute-start.27 = (bf16[1536,512]{1,0:T(8,128)(2,1)S(1)}, bf16[1536,512]{1,0:T(8,128)(2,1)S(1)}, u32[]{:S(2)}, u32[]{:S(2)}) collective-permute-start(bf16[1536,512]{1,0:T(8,128)(2,1)S(1)} %get-tuple-element.114), channel_id=1, source_target_pairs={{96,0},{25,1},{98,2},{27,3},{100,4},{29,5},{102,6},{31,7},{104,8},... | collective-permute-start | bytes 4718600 | tf_op jit(solution)/shard_map/ppermute | solution.py:55
  105.2 1.6 collective-permute-start.22
  106.8 2.0 %collective-permute-start.21 = (bf16[512,512]{1,0:T(8,128)(2,1)S(1)}, bf16[512,512]{1,0:T(8,128)(2,1)S(1)}, u32[]{:S(2)}, u32[]{:S(2)}) collective-permute-start(bf16[512,512]{1,0:T(8,128)(2,1)S(1)} %get-tuple-element.106), channel_id=1, source_target_pairs={{8,0},{33,1},{10,2},{35,3},{12,4},{37,5},{14,6},{39,7},{16,8},{41,... | collective-permute-start | bytes 1572872 | tf_op jit(solution)/shard_map/ppermute | solution.py:55
  108.9 3.4 %near.3.refs_5_ = f32[1024,512]{1,0:T(8,128)S(1)} custom-call(s32[632]{0:T(1024)S(1)} %sort_tiles.1.refs_0_, s32[193,5,128]{2,1,0:T(8,128)S(1)} %concatenate.3.refs_1_, bf16[1040,512]{1,0:T(8,128)(2,1)S(1)} %get-tuple-element.104.own.refs_2_, bf16[1024,512]{1,0:T(8,128)(2,1)S(1)} %get-tuple-element.105.refs_3_), custom_call_target="tpu_custom_call" | custom-call | tf_op jit(solution)/shard_map/near/pallas_call | solution.py:414
  112.3 10.5 %collective-permute-done.21.low2 = bf16[512,512]{1,0:T(8,128)(2,1)S(1)} collective-permute-done((bf16[512,512]{1,0:T(8,128)(2,1)S(1)}, bf16[512,512]{1,0:T(8,128)(2,1)S(1)}, u32[]{:S(2)}, u32[]{:S(2)}) %collective-permute-start.21) | collective-permute-done | bytes 524320 | tf_op jit(solution)/shard_map/ppermute | solution.py:55
  122.7 0.9 pick_late.3
  123.7 2.1 %collective-permute-start.24 = (f32[8,512]{1,0:T(8,128)S(1)}, f32[8,512]{1,0:T(8,128)S(1)}, u32[]{:S(2)}, u32[]{:S(2)}) collective-permute-start(f32[8,512]{1,0:T(8,128)S(1)} %get-tuple-element.110), channel_id=1, source_target_pairs={{96,0},{25,1},{98,2},{27,3},{100,4},{29,5},{102,6},{31,7},{104,8},... | collective-permute-start | bytes 49160 | tf_op jit(solution)/shard_map/ppermute | solution.py:55
  125.9 1.2 collective-permute-start.23
  127.0 1.9 %collective-permute-done.25 = f32[8,512]{1,0:T(8,128)S(1)} collective-permute-done((f32[8,512]{1,0:T(8,128)S(1)}, f32[8,512]{1,0:T(8,128)S(1)}, u32[]{:S(2)}, u32[]{:S(2)}) %collective-permute-start.25) | collective-permute-done | bytes 16416 | tf_op jit(solution)/shard_map/ppermute | solution.py:55
  129.0 0.6 collective-permute-done.23
  129.6 2.0 %collective-permute-start.28 = (bf16[1536,512]{1,0:T(8,128)(2,1)S(1)}, bf16[1536,512]{1,0:T(8,128)(2,1)S(1)}, u32[]{:S(2)}, u32[]{:S(2)}) collective-permute-start(bf16[1536,512]{1,0:T(8,128)(2,1)S(1)} %get-tuple-element.115), channel_id=1, source_target_pairs={{64,0},{17,1},{66,2},{19,3},{68,4},{21,5},{70,6},{23,7},{72,8},{25... | collective-permute-start | bytes 4718600 | tf_op jit(solution)/shard_map/ppermute | solution.py:55
  131.6 2.0 %collective-permute-start.32 = (bf16[512,512]{1,0:T(8,128)(2,1)S(1)}, bf16[512,512]{1,0:T(8,128)(2,1)S(1)}, u32[]{:S(2)}, u32[]{:S(2)}) collective-permute-start(bf16[512,512]{1,0:T(8,128)(2,1)S(1)} %get-tuple-element.127), channel_id=1, source_target_pairs={{32,0},{9,1},{34,2},{11,3},{36,4},{13,5},{38,6},{15,7},{40,8},{17,... | collective-permute-start | bytes 1572872 | tf_op jit(solution)/shard_map/ppermute | solution.py:55
  133.6 1.5 collective-permute-start.34
  135.2 3.5 %sides_1.3.refs_4_ = f32[1024,512]{1,0:T(8,128)S(1)} custom-call(s32[632]{0:T(1024)S(1)} %sort_tiles.1.refs_0_, s32[193,5,128]{2,1,0:T(8,128)S(1)} %concatenate.3.refs_1_, bf16[1040,512]{1,0:T(8,128)(2,1)S(1)} %get-tuple-element.104.own.refs_2_, bf16[1536,512]{1,0:T(8,128)(2,1)S(1)} %collective-permute-done.26.refs_3_, ...), custom_call_target="tpu_custom_call" | custom-call | tf_op jit(solution)/shard_map/sides_1/pallas_call | solution.py:414
  138.8 3.5 %sides_3.3.refs_4_ = f32[1024,512]{1,0:T(8,128)S(1)} custom-call(s32[632]{0:T(1024)S(1)} %sort_tiles.1.refs_0_, s32[193,5,128]{2,1,0:T(8,128)S(1)} %concatenate.3.refs_1_, bf16[1040,512]{1,0:T(8,128)(2,1)S(1)} %get-tuple-element.104.own.refs_2_, bf16[1536,512]{1,0:T(8,128)(2,1)S(1)} %collective-permute-done.27.refs_3_, f32[1024,512]{1,0:T(8,128)S(1)} %sides_1.3.refs_4_), custom_call_target="tpu_custom_call" | custom-call | tf_op jit(solution)/shard_map/sides_3/pallas_call | solution.py:414
  142.6 3.8 %collective-permute-start.31 = (f32[8,512]{1,0:T(8,128)S(1)}, f32[8,512]{1,0:T(8,128)S(1)}, u32[]{:S(2)}, u32[]{:S(2)}) collective-permute-start(f32[8,512]{1,0:T(8,128)S(1)} %add.48), channel_id=1, source_target_pairs={{0,4},{2,6},{4,0},{6,2},{1,5},{3,7},{5,1},{7,3},{8,12},{10,14},{12... | collective-permute-start | bytes 49160 | tf_op jit(solution)/shard_map/ppermute | solution.py:59
  146.3 5.3 %collective-permute-done.28.refs_3_ = bf16[1536,512]{1,0:T(8,128)(2,1)S(1)} collective-permute-done((bf16[1536,512]{1,0:T(8,128)(2,1)S(1)}, bf16[1536,512]{1,0:T(8,128)(2,1)S(1)}, u32[]{:S(2)}, u32[]{:S(2)}) %collective-permute-start.28) | collective-permute-done | bytes 1572896 | tf_op jit(solution)/shard_map/ppermute | solution.py:55
  151.7 3.4 %across.3.refs_5_ = f32[1024,512]{1,0:T(8,128)S(1)} custom-call(s32[632]{0:T(1024)S(1)} %sort_tiles.1.refs_0_, s32[193,5,128]{2,1,0:T(8,128)S(1)} %concatenate.3.refs_1_, bf16[1040,512]{1,0:T(8,128)(2,1)S(1)} %get-tuple-element.104.own.refs_2_, bf16[1536,512]{1,0:T(8,128)(2,1)S(1)} %collective-permute-done.28.refs_3_, f32[1024,512]{1,0:T(8,128)S(1)} %sides_3.3.refs_4_), custom_call_target="tpu_custom_call" | custom-call | tf_op jit(solution)/shard_map/across/pallas_call | solution.py:414
  155.1 1.8 %collective-permute-done.32.refs_3_ = bf16[512,512]{1,0:T(8,128)(2,1)S(1)} collective-permute-done((bf16[512,512]{1,0:T(8,128)(2,1)S(1)}, bf16[512,512]{1,0:T(8,128)(2,1)S(1)}, u32[]{:S(2)}, u32[]{:S(2)}) %collective-permute-start.32) | collective-permute-done | bytes 524320 | tf_op jit(solution)/shard_map/ppermute | solution.py:55
  157.2 2.8 %late.3.refs_4_ = f32[1024,512]{1,0:T(8,128)S(1)} custom-call(s32[632]{0:T(1024)S(1)} %sort_tiles.1.refs_0_, s32[193,5,128]{2,1,0:T(8,128)S(1)} %concatenate.3.refs_1_, bf16[1040,512]{1,0:T(8,128)(2,1)S(1)} %get-tuple-element.104.own.refs_2_, bf16[512,512]{1,0:T(8,128)(2,1)S(1)} %collective-permute-done.32.refs_3_, ...), custom_call_target="tpu_custom_call" | custom-call | tf_op jit(solution)/shard_map/late/pallas_call | solution.py:414
  160.0 2.8 %collective-permute-done.34.refs_3_ = bf16[512,512]{1,0:T(8,128)(2,1)S(1)} collective-permute-done((bf16[512,512]{1,0:T(8,128)(2,1)S(1)}, bf16[512,512]{1,0:T(8,128)(2,1)S(1)}, u32[]{:S(2)}, u32[]{:S(2)}) %collective-permute-start.34) | collective-permute-done | bytes 524320 | tf_op jit(solution)/shard_map/ppermute | solution.py:55
  162.8 3.5 %last.3 = f32[1024,512]{1,0:T(8,128)} custom-call(s32[632]{0:T(1024)S(1)} %sort_tiles.1.refs_0_, s32[193,5,128]{2,1,0:T(8,128)S(1)} %concatenate.3.refs_1_, bf16[1040,512]{1,0:T(8,128)(2,1)S(1)} %get-tuple-element.104.own.refs_2_, bf16[512,512]{1,0:T(8,128)(2,1)S(1)} %collective-permute-done.34.refs_3_, f32[1024,512]{1,0:T(8,128)S(1)} %late.3.refs_4_, ...), custom_call_target="tpu_custom_call" | custom-call | tf_op jit(solution)/shard_map/last/pallas_call | solution.py:414
  (52 shorter events, 1.1 us)
Async XLA Ops:
  0.0 1.6 copy-start
  1.6 4.2 %copy-start.2 = (s32[1024]{0:T(1024)S(1)}, s32[1024]{0:T(1024)}, u32[]{:S(2)}) copy-start(s32[1024]{0:T(1024)} %home.1) | copy-start | bytes 12292
  1.6 4.2 %copy-start.3 = (s32[1,240]{1,0:T(1,128)S(1)}, s32[1,240]{1,0:T(1,128)}, u32[]{:S(2)}) copy-start(s32[1,240]{1,0:T(1,128)} %param.8) | copy-start | bytes 2884
  1.6 4.2 %copy-start.4 = (s32[1,240]{1,0:T(1,128)S(1)}, s32[1,240]{1,0:T(1,128)}, u32[]{:S(2)}) copy-start(s32[1,240]{1,0:T(1,128)} %param.9) | copy-start | bytes 2884
  1.7 19.1 %collective-permute-start.4 = (bf16[1040,512]{1,0:T(8,128)(2,1)S(1)}, bf16[1040,512]{1,0:T(8,128)(2,1)S(1)}, u32[]{:S(2)}, u32[]{:S(2)}) collective-permute-start(bf16[1040,512]{1,0:T(8,128)(2,1)S(1)} %first.1.own.refs_2_), channel_id=1, source_target_pairs={{24,0},{97,1},{26,2},{99,3},{28,4},{101,5},{30,6},{103,7},{0,8},{1... | collective-permute-start | bytes 3194888 | tf_op jit(solution)/shard_map/ppermute | solution.py:55
  3.3 17.6 %collective-permute-start.3 = (bf16[1040,512]{1,0:T(8,128)(2,1)S(1)}, bf16[1040,512]{1,0:T(8,128)(2,1)S(1)}, u32[]{:S(2)}, u32[]{:S(2)}) collective-permute-start(bf16[1040,512]{1,0:T(8,128)(2,1)S(1)} %first.1.own.refs_2_), channel_id=1, source_target_pairs={{8,0},{33,1},{10,2},{35,3},{12,4},{37,5},{14,6},{39,7},{16,8},{41,... | collective-permute-start | bytes 3194888 | tf_op jit(solution)/shard_map/ppermute | solution.py:55
  9.2 6.9 %collective-permute-start.2 = (s32[16]{0:T(128)S(1)}, s32[16]{0:T(128)S(1)}, u32[]{:S(2)}, u32[]{:S(2)}) collective-permute-start(s32[16]{0:T(128)S(1)} %get-tuple-element.138), channel_id=1, source_target_pairs={{32,0},{9,1},{34,2},{11,3},{36,4},{13,5},{38,6},{15,7},{40,8},{17,... | collective-permute-start | bytes 200 | tf_op jit(solution)/shard_map/ppermute | solution.py:55
  12.7 5.1 %collective-permute-start.1 = (s32[16]{0:T(128)S(1)}, s32[16]{0:T(128)S(1)}, u32[]{:S(2)}, u32[]{:S(2)}) collective-permute-start(s32[16]{0:T(128)S(1)} %get-tuple-element.139), channel_id=1, source_target_pairs={{64,0},{17,1},{66,2},{19,3},{68,4},{21,5},{70,6},{23,7},{72,8},{25... | collective-permute-start | bytes 200 | tf_op jit(solution)/shard_map/ppermute | solution.py:55
  16.1 4.8 %collective-permute-start = (s32[16]{0:T(128)S(1)}, s32[16]{0:T(128)S(1)}, u32[]{:S(2)}, u32[]{:S(2)}) collective-permute-start(s32[16]{0:T(128)S(1)} %get-tuple-element.140), channel_id=1, source_target_pairs={{96,0},{25,1},{98,2},{27,3},{100,4},{29,5},{102,6},{31,7},{104,8},... | collective-permute-start | bytes 200 | tf_op jit(solution)/shard_map/ppermute | solution.py:55
  20.9 6.3 %copy-start.6 = (s32[192,5,128]{2,0,1:T(8,128)S(1)}, s32[192,5,128]{2,0,1:T(8,128)}, u32[]{:S(2)}) copy-start(s32[192,5,128]{2,0,1:T(8,128)} %param.13) | copy-start | bytes 1474564
  21.8 5.7 %copy-start.5 = (s32[1,240]{1,0:T(1,128)S(1)}, s32[1,240]{1,0:T(1,128)}, u32[]{:S(2)}) copy-start(s32[1,240]{1,0:T(1,128)} %param.10) | copy-start | bytes 2884
  21.8 26.6 %collective-permute-start.10 = (bf16[1536,512]{1,0:T(8,128)(2,1)S(1)}, bf16[1536,512]{1,0:T(8,128)(2,1)S(1)}, u32[]{:S(2)}, u32[]{:S(2)}) collective-permute-start(bf16[1536,512]{1,0:T(8,128)(2,1)S(1)} %get-tuple-element.81), channel_id=1, source_target_pairs={{32,0},{9,1},{34,2},{11,3},{36,4},{13,5},{38,6},{15,7},{40,8},{17,... | collective-permute-start | bytes 4718600 | tf_op jit(solution)/shard_map/ppermute | solution.py:55
  22.3 26.1 %collective-permute-start.11 = (bf16[1536,512]{1,0:T(8,128)(2,1)S(1)}, bf16[1536,512]{1,0:T(8,128)(2,1)S(1)}, u32[]{:S(2)}, u32[]{:S(2)}) collective-permute-start(bf16[1536,512]{1,0:T(8,128)(2,1)S(1)} %get-tuple-element.82), channel_id=1, source_target_pairs={{96,0},{25,1},{98,2},{27,3},{100,4},{29,5},{102,6},{31,7},{104,8},... | collective-permute-start | bytes 4718600 | tf_op jit(solution)/shard_map/ppermute | solution.py:55
  23.9 16.4 %collective-permute-start.6 = (bf16[528,512]{1,0:T(8,128)(2,1)S(1)}, bf16[528,512]{1,0:T(8,128)(2,1)S(1)}, u32[]{:S(2)}, u32[]{:S(2)}) collective-permute-start(bf16[528,512]{1,0:T(8,128)(2,1)S(1)} %get-tuple-element.75), channel_id=1, source_target_pairs={{24,0},{97,1},{26,2},{99,3},{28,4},{101,5},{30,6},{103,7},{0,8},{1... | collective-permute-start | bytes 1622024 | tf_op jit(solution)/shard_map/ppermute | solution.py:55
  23.9 15.6 %collective-permute-start.5 = (bf16[512,512]{1,0:T(8,128)(2,1)S(1)}, bf16[512,512]{1,0:T(8,128)(2,1)S(1)}, u32[]{:S(2)}, u32[]{:S(2)}) collective-permute-start(bf16[512,512]{1,0:T(8,128)(2,1)S(1)} %get-tuple-element.74), channel_id=1, source_target_pairs={{8,0},{33,1},{10,2},{35,3},{12,4},{37,5},{14,6},{39,7},{16,8},{41,... | collective-permute-start | bytes 1572872 | tf_op jit(solution)/shard_map/ppermute | solution.py:55
  41.2 7.2 %collective-permute-start.9 = (f32[8,512]{1,0:T(8,128)S(1)}, f32[8,512]{1,0:T(8,128)S(1)}, u32[]{:S(2)}, u32[]{:S(2)}) collective-permute-start(f32[8,512]{1,0:T(8,128)S(1)} %get-tuple-element.78), channel_id=1, source_target_pairs={{64,0},{17,1},{66,2},{19,3},{68,4},{21,5},{70,6},{23,7},{72,8},{25... | collective-permute-start | bytes 49160 | tf_op jit(solution)/shard_map/ppermute | solution.py:55
  41.9 6.5 %collective-permute-start.8 = (f32[8,512]{1,0:T(8,128)S(1)}, f32[8,512]{1,0:T(8,128)S(1)}, u32[]{:S(2)}, u32[]{:S(2)}) collective-permute-start(f32[8,512]{1,0:T(8,128)S(1)} %get-tuple-element.78), channel_id=1, source_target_pairs={{96,0},{25,1},{98,2},{27,3},{100,4},{29,5},{102,6},{31,7},{104,8},... | collective-permute-start | bytes 49160 | tf_op jit(solution)/shard_map/ppermute | solution.py:55
  43.8 4.6 %collective-permute-start.7 = (f32[8,512]{1,0:T(8,128)S(1)}, f32[8,512]{1,0:T(8,128)S(1)}, u32[]{:S(2)}, u32[]{:S(2)}) collective-permute-start(f32[8,512]{1,0:T(8,128)S(1)} %get-tuple-element.78), channel_id=1, source_target_pairs={{32,0},{9,1},{34,2},{11,3},{36,4},{13,5},{38,6},{15,7},{40,8},{17,... | collective-permute-start | bytes 49160 | tf_op jit(solution)/shard_map/ppermute | solution.py:55
  48.4 22.1 %collective-permute-start.12 = (bf16[1536,512]{1,0:T(8,128)(2,1)S(1)}, bf16[1536,512]{1,0:T(8,128)(2,1)S(1)}, u32[]{:S(2)}, u32[]{:S(2)}) collective-permute-start(bf16[1536,512]{1,0:T(8,128)(2,1)S(1)} %get-tuple-element.83), channel_id=1, source_target_pairs={{64,0},{17,1},{66,2},{19,3},{68,4},{21,5},{70,6},{23,7},{72,8},{25... | collective-permute-start | bytes 4718600 | tf_op jit(solution)/shard_map/ppermute | solution.py:55
  49.2 25.8 %collective-permute-start.16 = (bf16[512,512]{1,0:T(8,128)(2,1)S(1)}, bf16[512,512]{1,0:T(8,128)(2,1)S(1)}, u32[]{:S(2)}, u32[]{:S(2)}) collective-permute-start(bf16[512,512]{1,0:T(8,128)(2,1)S(1)} %get-tuple-element.95), channel_id=1, source_target_pairs={{32,0},{9,1},{34,2},{11,3},{36,4},{13,5},{38,6},{15,7},{40,8},{17,... | collective-permute-start | bytes 1572872 | tf_op jit(solution)/shard_map/ppermute | solution.py:55
  51.2 24.8 %collective-permute-start.17 = (bf16[512,512]{1,0:T(8,128)(2,1)S(1)}, bf16[512,512]{1,0:T(8,128)(2,1)S(1)}, u32[]{:S(2)}, u32[]{:S(2)}) collective-permute-start(bf16[512,512]{1,0:T(8,128)(2,1)S(1)} %get-tuple-element.96), channel_id=1, source_target_pairs={{96,0},{25,1},{98,2},{27,3},{100,4},{29,5},{102,6},{31,7},{104,8},... | collective-permute-start | bytes 1572872 | tf_op jit(solution)/shard_map/ppermute | solution.py:55
  51.2 30.5 %collective-permute-start.18 = (bf16[512,512]{1,0:T(8,128)(2,1)S(1)}, bf16[512,512]{1,0:T(8,128)(2,1)S(1)}, u32[]{:S(2)}, u32[]{:S(2)}) collective-permute-start(bf16[512,512]{1,0:T(8,128)(2,1)S(1)} %get-tuple-element.100), channel_id=1, source_target_pairs={{64,0},{17,1},{66,2},{19,3},{68,4},{21,5},{70,6},{23,7},{72,8},{25... | collective-permute-start | bytes 1572872 | tf_op jit(solution)/shard_map/ppermute | solution.py:55
  54.1 3.6 %collective-permute-start.13 = (f32[8,512]{1,0:T(8,128)S(1)}, f32[8,512]{1,0:T(8,128)S(1)}, u32[]{:S(2)}, u32[]{:S(2)}) collective-permute-start(f32[8,512]{1,0:T(8,128)S(1)} %add_add_fusion.1), channel_id=1, source_target_pairs={{0,1},{1,0},{2,3},{3,2},{4,5},{5,4},{6,7},{7,6},{8,9},{9,8},{10,11... | collective-permute-start | bytes 49160 | tf_op jit(solution)/shard_map/ppermute | solution.py:59
  57.7 4.3 %collective-permute-start.14 = (f32[8,512]{1,0:T(8,128)S(1)}, f32[8,512]{1,0:T(8,128)S(1)}, u32[]{:S(2)}, u32[]{:S(2)}) collective-permute-start(f32[8,512]{1,0:T(8,128)S(1)} %add.41), channel_id=1, source_target_pairs={{0,2},{2,0},{4,6},{6,4},{1,3},{3,1},{5,7},{7,5},{8,10},{10,8},{12,... | collective-permute-start | bytes 49160 | tf_op jit(solution)/shard_map/ppermute | solution.py:59
  62.0 14.0 %collective-permute-start.15 = (f32[8,512]{1,0:T(8,128)S(1)}, f32[8,512]{1,0:T(8,128)S(1)}, u32[]{:S(2)}, u32[]{:S(2)}) collective-permute-start(f32[8,512]{1,0:T(8,128)S(1)} %add.42), channel_id=1, source_target_pairs={{0,4},{2,6},{4,0},{6,2},{1,5},{3,7},{5,1},{7,3},{8,12},{10,14},{12... | collective-permute-start | bytes 49160 | tf_op jit(solution)/shard_map/ppermute | solution.py:59
  76.1 5.7 %copy-start.1 = (f32[1024,512]{1,0:T(8,128)S(1)}, f32[1024,512]{1,0:T(8,128)}, u32[]{:S(2)}) copy-start(f32[1024,512]{1,0:T(8,128)} %refs_5_.1) | copy-start | bytes 6291460
  84.3 16.7 %collective-permute-start.20 = (bf16[1040,512]{1,0:T(8,128)(2,1)S(1)}, bf16[1040,512]{1,0:T(8,128)(2,1)S(1)}, u32[]{:S(2)}, u32[]{:S(2)}) collective-permute-start(bf16[1040,512]{1,0:T(8,128)(2,1)S(1)} %get-tuple-element.104.own.refs_2_), channel_id=1, source_target_pairs={{24,0},{97,1},{26,2},{99,3},{28,4},{101,5},{30,6},{103,7},{0,8},{1... | collective-permute-start | bytes 3194888 | tf_op jit(solution)/shard_map/ppermute | solution.py:55
  84.6 17.6 %collective-permute-start.19 = (bf16[1040,512]{1,0:T(8,128)(2,1)S(1)}, bf16[1040,512]{1,0:T(8,128)(2,1)S(1)}, u32[]{:S(2)}, u32[]{:S(2)}) collective-permute-start(bf16[1040,512]{1,0:T(8,128)(2,1)S(1)} %get-tuple-element.104.own.refs_2_), channel_id=1, source_target_pairs={{8,0},{33,1},{10,2},{35,3},{12,4},{37,5},{14,6},{39,7},{16,8},{41,... | collective-permute-start | bytes 3194888 | tf_op jit(solution)/shard_map/ppermute | solution.py:55
  103.1 26.5 %collective-permute-start.26 = (bf16[1536,512]{1,0:T(8,128)(2,1)S(1)}, bf16[1536,512]{1,0:T(8,128)(2,1)S(1)}, u32[]{:S(2)}, u32[]{:S(2)}) collective-permute-start(bf16[1536,512]{1,0:T(8,128)(2,1)S(1)} %get-tuple-element.113), channel_id=1, source_target_pairs={{32,0},{9,1},{34,2},{11,3},{36,4},{13,5},{38,6},{15,7},{40,8},{17,... | collective-permute-start | bytes 4718600 | tf_op jit(solution)/shard_map/ppermute | solution.py:55
  103.5 26.1 %collective-permute-start.27 = (bf16[1536,512]{1,0:T(8,128)(2,1)S(1)}, bf16[1536,512]{1,0:T(8,128)(2,1)S(1)}, u32[]{:S(2)}, u32[]{:S(2)}) collective-permute-start(bf16[1536,512]{1,0:T(8,128)(2,1)S(1)} %get-tuple-element.114), channel_id=1, source_target_pairs={{96,0},{25,1},{98,2},{27,3},{100,4},{29,5},{102,6},{31,7},{104,8},... | collective-permute-start | bytes 4718600 | tf_op jit(solution)/shard_map/ppermute | solution.py:55
  105.2 17.6 %collective-permute-start.22 = (bf16[528,512]{1,0:T(8,128)(2,1)S(1)}, bf16[528,512]{1,0:T(8,128)(2,1)S(1)}, u32[]{:S(2)}, u32[]{:S(2)}) collective-permute-start(bf16[528,512]{1,0:T(8,128)(2,1)S(1)} %get-tuple-element.107), channel_id=1, source_target_pairs={{24,0},{97,1},{26,2},{99,3},{28,4},{101,5},{30,6},{103,7},{0,8},{1... | collective-permute-start | bytes 1622024 | tf_op jit(solution)/shard_map/ppermute | solution.py:55
  106.8 15.9 %collective-permute-start.21 = (bf16[512,512]{1,0:T(8,128)(2,1)S(1)}, bf16[512,512]{1,0:T(8,128)(2,1)S(1)}, u32[]{:S(2)}, u32[]{:S(2)}) collective-permute-start(bf16[512,512]{1,0:T(8,128)(2,1)S(1)} %get-tuple-element.106), channel_id=1, source_target_pairs={{8,0},{33,1},{10,2},{35,3},{12,4},{37,5},{14,6},{39,7},{16,8},{41,... | collective-permute-start | bytes 1572872 | tf_op jit(solution)/shard_map/ppermute | solution.py:55
  123.6 5.3 %collective-permute-start.25 = (f32[8,512]{1,0:T(8,128)S(1)}, f32[8,512]{1,0:T(8,128)S(1)}, u32[]{:S(2)}, u32[]{:S(2)}) collective-permute-start(f32[8,512]{1,0:T(8,128)S(1)} %get-tuple-element.110), channel_id=1, source_target_pairs={{64,0},{17,1},{66,2},{19,3},{68,4},{21,5},{70,6},{23,7},{72,8},{25... | collective-permute-start | bytes 49160 | tf_op jit(solution)/shard_map/ppermute | solution.py:55
  123.7 5.2 %collective-permute-start.24 = (f32[8,512]{1,0:T(8,128)S(1)}, f32[8,512]{1,0:T(8,128)S(1)}, u32[]{:S(2)}, u32[]{:S(2)}) collective-permute-start(f32[8,512]{1,0:T(8,128)S(1)} %get-tuple-element.110), channel_id=1, source_target_pairs={{96,0},{25,1},{98,2},{27,3},{100,4},{29,5},{102,6},{31,7},{104,8},... | collective-permute-start | bytes 49160 | tf_op jit(solution)/shard_map/ppermute | solution.py:55
  125.9 3.7 %collective-permute-start.23 = (f32[8,512]{1,0:T(8,128)S(1)}, f32[8,512]{1,0:T(8,128)S(1)}, u32[]{:S(2)}, u32[]{:S(2)}) collective-permute-start(f32[8,512]{1,0:T(8,128)S(1)} %get-tuple-element.110), channel_id=1, source_target_pairs={{32,0},{9,1},{34,2},{11,3},{36,4},{13,5},{38,6},{15,7},{40,8},{17,... | collective-permute-start | bytes 49160 | tf_op jit(solution)/shard_map/ppermute | solution.py:55
  129.6 22.0 %collective-permute-start.28 = (bf16[1536,512]{1,0:T(8,128)(2,1)S(1)}, bf16[1536,512]{1,0:T(8,128)(2,1)S(1)}, u32[]{:S(2)}, u32[]{:S(2)}) collective-permute-start(bf16[1536,512]{1,0:T(8,128)(2,1)S(1)} %get-tuple-element.115), channel_id=1, source_target_pairs={{64,0},{17,1},{66,2},{19,3},{68,4},{21,5},{70,6},{23,7},{72,8},{25... | collective-permute-start | bytes 4718600 | tf_op jit(solution)/shard_map/ppermute | solution.py:55
  131.6 25.3 %collective-permute-start.32 = (bf16[512,512]{1,0:T(8,128)(2,1)S(1)}, bf16[512,512]{1,0:T(8,128)(2,1)S(1)}, u32[]{:S(2)}, u32[]{:S(2)}) collective-permute-start(bf16[512,512]{1,0:T(8,128)(2,1)S(1)} %get-tuple-element.127), channel_id=1, source_target_pairs={{32,0},{9,1},{34,2},{11,3},{36,4},{13,5},{38,6},{15,7},{40,8},{17,... | collective-permute-start | bytes 1572872 | tf_op jit(solution)/shard_map/ppermute | solution.py:55
  133.6 23.5 %collective-permute-start.33 = (bf16[512,512]{1,0:T(8,128)(2,1)S(1)}, bf16[512,512]{1,0:T(8,128)(2,1)S(1)}, u32[]{:S(2)}, u32[]{:S(2)}) collective-permute-start(bf16[512,512]{1,0:T(8,128)(2,1)S(1)} %get-tuple-element.128), channel_id=1, source_target_pairs={{96,0},{25,1},{98,2},{27,3},{100,4},{29,5},{102,6},{31,7},{104,8},... | collective-permute-start | bytes 1572872 | tf_op jit(solution)/shard_map/ppermute | solution.py:55
  133.6 29.2 %collective-permute-start.34 = (bf16[512,512]{1,0:T(8,128)(2,1)S(1)}, bf16[512,512]{1,0:T(8,128)(2,1)S(1)}, u32[]{:S(2)}, u32[]{:S(2)}) collective-permute-start(bf16[512,512]{1,0:T(8,128)(2,1)S(1)} %get-tuple-element.132), channel_id=1, source_target_pairs={{64,0},{17,1},{66,2},{19,3},{68,4},{21,5},{70,6},{23,7},{72,8},{25... | collective-permute-start | bytes 1572872 | tf_op jit(solution)/shard_map/ppermute | solution.py:55
  135.2 3.5 %collective-permute-start.29 = (f32[8,512]{1,0:T(8,128)S(1)}, f32[8,512]{1,0:T(8,128)S(1)}, u32[]{:S(2)}, u32[]{:S(2)}) collective-permute-start(f32[8,512]{1,0:T(8,128)S(1)} %add_add_fusion), channel_id=1, source_target_pairs={{0,1},{1,0},{2,3},{3,2},{4,5},{5,4},{6,7},{7,6},{8,9},{9,8},{10,11... | collective-permute-start | bytes 49160 | tf_op jit(solution)/shard_map/ppermute | solution.py:59
  138.7 3.8 %collective-permute-start.30 = (f32[8,512]{1,0:T(8,128)S(1)}, f32[8,512]{1,0:T(8,128)S(1)}, u32[]{:S(2)}, u32[]{:S(2)}) collective-permute-start(f32[8,512]{1,0:T(8,128)S(1)} %add.47), channel_id=1, source_target_pairs={{0,2},{2,0},{4,6},{6,4},{1,3},{3,1},{5,7},{7,5},{8,10},{10,8},{12,... | collective-permute-start | bytes 49160 | tf_op jit(solution)/shard_map/ppermute | solution.py:59
  142.6 14.6 %collective-permute-start.31 = (f32[8,512]{1,0:T(8,128)S(1)}, f32[8,512]{1,0:T(8,128)S(1)}, u32[]{:S(2)}, u32[]{:S(2)}) collective-permute-start(f32[8,512]{1,0:T(8,128)S(1)} %add.48), channel_id=1, source_target_pairs={{0,4},{2,6},{4,0},{6,2},{1,5},{3,7},{5,1},{7,3},{8,12},{10,14},{12... | collective-permute-start | bytes 49160 | tf_op jit(solution)/shard_map/ppermute | solution.py:59
where the time goes:
time: 167 us
  waiting for transfers between devices  60.3 us (36%)
  starting transfers between devices  52.3 us (31%)
  Pallas kernels  50.6 us (30%)
  local copies, waits for them, and re-layouts  2.06 us (1%)
    ppermute x29, waiting for transfers between devices, fetch(): return lax.ppermute(value, ALL, pairs(first, second))  60.2 us
    ppermute x29, starting transfers between devices, fetch(): return lax.ppermute(value, ALL, pairs(first, second))  43.7 us
    pallas_call x12, Pallas kernels, run_tiles(): pl.pallas_call(functools.partial(tile_kernel, part, len(tables), earlier...  39.9 us
    ppermute x6, starting transfers between devices, swap(): lax.ppermute(value, axis, [(i, i ^ step) for i in range(lax.axis_size(axi...  8.62 us
    pallas_call x1, Pallas kernels, sort_tiles(): pl.pallas_call(sort_kernel, out_shape=jax.ShapeDtypeStruct((LIST,), i32),...  3.6 us
    pallas_call x1, Pallas kernels, ask(): pl.pallas_call(ask_kernel, out_shape=(jax.ShapeDtypeStruct((64,), i32), j...  3.35 us
  transfers between devices with their start and end apart: 35, of which 19 were waited for; matrix products, arithmetic and copies ran while one was open for 0% of the time, Pallas kernels for 26%

commit v1 on v0

--- a/solution.py
+++ b/solution.py
@@ -206,35 +206,43 @@
     out[pl.ds(at * BLOCK, BLOCK), :] = table[rows, :]
 
 
-def pick_early_kernel(asked, wanted, own, far1, far3, near, pass1, pass3, out1, out3):
-    pass1[...] = far1[pl.ds(0, HALF_ROWS), :]
-    pass3[...] = far3[pl.ds(HALF_ROWS, HALF_ROWS + 16), :]
+def pick_early_kernel(asked, own, far1, far3, out1, out3):
     for m, out in ((1, out1), (3, out3)):
         for i, (k, table) in enumerate(((0, own), (1, far1), (3, far3))):
             for r in range(CAP):
                 move(table, asked[m - 1, k * CAP + r], out, i * CAP + r)
+
+
+def pick_early(asked, own, far1, far3):
+    out = jax.ShapeDtypeStruct((3 * CAP * BLOCK, C), jnp.bfloat16)
+    return pl.pallas_call(
+        pick_early_kernel,
+        out_shape=(out, out),
+        in_specs=[SMEM] + [VMEM] * 3,
+        out_specs=(VMEM,) * 2,
+        compiler_params=pltpu.CompilerParams(vmem_limit_bytes=20 << 20),
+        name="pick_early",
+    )(asked, own, far1, far3)
+
+
+def pick_pass_kernel(wanted, far1, far3, near, pass1, pass3):
+    pass1[...] = far1[pl.ds(0, HALF_ROWS), :]
+    pass3[...] = far3[pl.ds(HALF_ROWS, HALF_ROWS + 16), :]
     for r in range(CAP):
         move(far1, wanted[CAP + r], near, r)
         move(far3, wanted[3 * CAP + r], near, CAP + r)
 
 
-def pick_early(asked, wanted, own, far1, far3):
-    b16 = jnp.bfloat16
-    out = jax.ShapeDtypeStruct((3 * CAP * BLOCK, C), b16)
-    return pl.pallas_call(
-        pick_early_kernel,
-        out_shape=(
-            jax.ShapeDtypeStruct((2 * CAP * BLOCK, C), b16),
-            jax.ShapeDtypeStruct((HALF_ROWS, C), b16),
-            jax.ShapeDtypeStruct((HALF_ROWS + 16, C), b16),
-            out,
-            out,
-        ),
-        in_specs=[SMEM] * 2 + [VMEM] * 3,
-        out_specs=(VMEM,) * 5,
+def pick_pass(wanted, far1, far3):
+    shape = lambda rows: jax.ShapeDtypeStruct((rows, C), jnp.bfloat16)
+    return pl.pallas_call(
+        pick_pass_kernel,
+        out_shape=(shape(2 * CAP * BLOCK), shape(HALF_ROWS), shape(HALF_ROWS + 16)),
+        in_specs=[SMEM] + [VMEM] * 2,
+        out_specs=(VMEM,) * 3,
         compiler_params=pltpu.CompilerParams(vmem_limit_bytes=20 << 20),
-        name="pick_early",
-    )(asked, wanted, own, far1, far3)
+        name="pick_pass",
+    )(wanted, far1, far3)
 
 
 def pick_late_kernel(asked, wanted, own, far1, far3, low2, high2, near, out1, out3, out2a, out2b, line, far2):
@@ -438,7 +446,8 @@
     lists = sort_tiles(codes, tile_pattern[0], tile_count)
     for step in range(STEPS):
         far1, far3 = fetch(own, 1, 0), fetch(own, 3, 0)
-        near, pass1, pass3, out1, out3 = pick_early(asked, requests[0], own, far1, far3)
+        out1, out3 = pick_early(asked, own, far1, far3)
+        near, pass1, pass3 = pick_pass(requests[0], far1, far3)
         low2, high2 = fetch(pass1, 1, 0), fetch(pass3, 3, 0)
         side1, side3 = fetch(out1, 0, 1), fetch(out3, 0, 3)
         (total,) = run_tiles("near", 0, lists, words, own, (near,))

time: 167 us -> 169 us (1.012)
  Pallas kernels: 50.6 us -> 56 us
  waiting for transfers between devices: 60.3 us -> 56.8 us
    ppermute x29, waiting for transfers between devices: 60.2 us -> 56.4 us  [fetch(): return lax.ppermute(value, ALL, pairs(first, second))]
    pallas_call x12, Pallas kernels: 39.9 us -> 43.5 us  [run_tiles(): pl.pallas_call(functools.partial(tile_kernel, part, len(tables), earlier...]
  transfers between devices with their start and end apart: 35 -> 35, of which waited for: 19 -> 23; matrix products, arithmetic and copies ran while one was open for 0% -> 0% of each run, Pallas kernels for 26% -> 29%
where the time goes in v1:
time: 169 us; the launch traced here: 168 us
  waiting for transfers between devices  56.8 us (34%)
  Pallas kernels  56 us (33%)
  starting transfers between devices  52.1 us (31%)
  local copies, waits for them, and re-layouts  2.06 us (1%)
    ppermute x29, waiting for transfers between devices, fetch(): return lax.ppermute(value, ALL, pairs(first, second))  56.4 us
    ppermute x29, starting transfers between devices, fetch(): return lax.ppermute(value, ALL, pairs(first, second))  44.3 us
    pallas_call x12, Pallas kernels, run_tiles(): pl.pallas_call(functools.partial(tile_kernel, part, len(tables), earlier...  43.5 us
    ppermute x6, starting transfers between devices, swap(): lax.ppermute(value, axis, [(i, i ^ step) for i in range(lax.axis_size(axi...  7.75 us
    pallas_call x1, Pallas kernels, sort_tiles(): pl.pallas_call(sort_kernel, out_shape=jax.ShapeDtypeStruct((LIST,), i32),...  3.95 us
    pallas_call x1, Pallas kernels, ask(): pl.pallas_call(ask_kernel, out_shape=(jax.ShapeDtypeStruct((64,), i32), j...  3.77 us
  transfers between devices with their start and end apart: 35, of which 23 were waited for; matrix products, arithmetic and copies ran while one was open for 0% of the time, Pallas kernels for 29%

profile of v1, /device:TPU:32, one launch (start us, length us, event | category | flops | bytes accessed | tf_op | source)
XLA Modules:
  0.0 168.2 jit_solution(4322512830035466630)
XLA Ops:
  0.0 1.6 copy-done
  1.7 1.6 collective-permute-start.4
  3.3 1.7 %collective-permute-start.3 = (bf16[1040,512]{1,0:T(8,128)(2,1)S(1)}, bf16[1040,512]{1,0:T(8,128)(2,1)S(1)}, u32[]{:S(2)}, u32[]{:S(2)}) collective-permute-start(bf16[1040,512]{1,0:T(8,128)(2,1)S(1)} %first.1.refs_2_.own), channel_id=1, source_target_pairs={{8,0},{33,1},{10,2},{35,3},{12,4},{37,5},{14,6},{39,7},{16,8},{41,... | collective-permute-start | bytes 3194888 | tf_op jit(solution)/shard_map/ppermute | solution.py:55
  5.8 3.8 %ask.1 = (s32[64]{0:T(128)S(1)}, s32[240]{0:T(256)S(1)}) custom-call(s32[3]{0:T(128)S(1)} %pad_add_fusion.1.place, s32[240]{0:T(256)S(1)} %bitcast.9, s32[240]{0:T(256)S(1)} %bitcast.10, s32[1]{0:T(128)S(6)} %copy.9.count, s32[1024]{0:T(1024)S(1)} %copy-done.2), custom_call_target="tpu_custom_call" | custom-call | tf_op jit(solution)/shard_map/ask/pallas_call | solution.py:115
  9.6 2.6 %collective-permute-start.2 = (s32[16]{0:T(128)S(1)}, s32[16]{0:T(128)S(1)}, u32[]{:S(2)}, u32[]{:S(2)}) collective-permute-start(s32[16]{0:T(128)S(1)} %get-tuple-element.138), channel_id=1, source_target_pairs={{32,0},{9,1},{34,2},{11,3},{36,4},{13,5},{38,6},{15,7},{40,8},{17,... | collective-permute-start | bytes 200 | tf_op jit(solution)/shard_map/ppermute | solution.py:55
  12.2 0.8 collective-permute-start.1
  13.0 1.1 collective-permute-start
  14.1 3.2 %collective-permute-done.1 = s32[16]{0:T(128)S(1)} collective-permute-done((s32[16]{0:T(128)S(1)}, s32[16]{0:T(128)S(1)}, u32[]{:S(2)}, u32[]{:S(2)}) %collective-permute-start.1) | collective-permute-done | bytes 96 | tf_op jit(solution)/shard_map/ppermute | solution.py:55
  18.3 0.8 pick_early.2
  19.1 3.1 %collective-permute-start.10 = (bf16[1536,512]{1,0:T(8,128)(2,1)S(1)}, bf16[1536,512]{1,0:T(8,128)(2,1)S(1)}, u32[]{:S(2)}, u32[]{:S(2)}) collective-permute-start(bf16[1536,512]{1,0:T(8,128)(2,1)S(1)} %get-tuple-element.81), channel_id=1, source_target_pairs={{32,0},{9,1},{34,2},{11,3},{36,4},{13,5},{38,6},{15,7},{40,8},{17,... | collective-permute-start | bytes 4718600 | tf_op jit(solution)/shard_map/ppermute | solution.py:55
  22.2 0.7 pick_pass.2
  22.9 1.6 collective-permute-start.6
  24.4 1.7 %collective-permute-start.5 = (bf16[512,512]{1,0:T(8,128)(2,1)S(1)}, bf16[512,512]{1,0:T(8,128)(2,1)S(1)}, u32[]{:S(2)}, u32[]{:S(2)}) collective-permute-start(bf16[512,512]{1,0:T(8,128)(2,1)S(1)} %get-tuple-element.74), channel_id=1, source_target_pairs={{8,0},{33,1},{10,2},{35,3},{12,4},{37,5},{14,6},{39,7},{16,8},{41,... | collective-permute-start | bytes 1572872 | tf_op jit(solution)/shard_map/ppermute | solution.py:55
  26.5 4.0 %sort_tiles.1.refs_0_ = s32[632]{0:T(1024)S(1)} custom-call(s32[240]{0:T(256)S(1)} %get-tuple-element.71.codes, s32[240]{0:T(256)S(1)} %bitcast.11, s32[1]{0:T(128)S(6)} %copy.9.count), custom_call_target="tpu_custom_call" | custom-call | tf_op jit(solution)/shard_map/sort_tiles/pallas_call | solution.py:163
  30.5 2.8 %near.2.refs_5_ = f32[1024,512]{1,0:T(8,128)S(1)} custom-call(s32[632]{0:T(1024)S(1)} %sort_tiles.1.refs_0_, s32[193,5,128]{2,1,0:T(8,128)S(1)} %concatenate.3.refs_1_, bf16[1040,512]{1,0:T(8,128)(2,1)S(1)} %first.1.refs_2_.own, bf16[1024,512]{1,0:T(8,128)(2,1)S(1)} %get-tuple-element.73.refs_3_), custom_call_target="tpu_custom_call" | custom-call | tf_op jit(solution)/shard_map/near/pallas_call | solution.py:422
  33.3 6.0 %collective-permute-done.5.low2 = bf16[512,512]{1,0:T(8,128)(2,1)S(1)} collective-permute-done((bf16[512,512]{1,0:T(8,128)(2,1)S(1)}, bf16[512,512]{1,0:T(8,128)(2,1)S(1)}, u32[]{:S(2)}, u32[]{:S(2)}) %collective-permute-start.5) | collective-permute-done | bytes 524320 | tf_op jit(solution)/shard_map/ppermute | solution.py:55
  39.3 0.9 pick_late.2
  40.2 2.3 %collective-permute-start.9 = (f32[8,512]{1,0:T(8,128)S(1)}, f32[8,512]{1,0:T(8,128)S(1)}, u32[]{:S(2)}, u32[]{:S(2)}) collective-permute-start(f32[8,512]{1,0:T(8,128)S(1)} %get-tuple-element.78), channel_id=1, source_target_pairs={{64,0},{17,1},{66,2},{19,3},{68,4},{21,5},{70,6},{23,7},{72,8},{25... | collective-permute-start | bytes 49160 | tf_op jit(solution)/shard_map/ppermute | solution.py:55
  42.5 1.9 %collective-permute-start.8 = (f32[8,512]{1,0:T(8,128)S(1)}, f32[8,512]{1,0:T(8,128)S(1)}, u32[]{:S(2)}, u32[]{:S(2)}) collective-permute-start(f32[8,512]{1,0:T(8,128)S(1)} %get-tuple-element.78), channel_id=1, source_target_pairs={{96,0},{25,1},{98,2},{27,3},{100,4},{29,5},{102,6},{31,7},{104,8},... | collective-permute-start | bytes 49160 | tf_op jit(solution)/shard_map/ppermute | solution.py:55
  44.4 1.3 collective-permute-start.7
  45.8 3.0 %collective-permute-done.9 = f32[8,512]{1,0:T(8,128)S(1)} collective-permute-done((f32[8,512]{1,0:T(8,128)S(1)}, f32[8,512]{1,0:T(8,128)S(1)}, u32[]{:S(2)}, u32[]{:S(2)}) %collective-permute-start.9) | collective-permute-done | bytes 16416 | tf_op jit(solution)/shard_map/ppermute | solution.py:55
  48.7 1.0 collective-permute-start.12
  49.8 1.3 collective-permute-start.16
  51.1 0.7 collective-permute-start.17
  51.8 2.6 %collective-permute-start.18 = (bf16[512,512]{1,0:T(8,128)(2,1)S(1)}, bf16[512,512]{1,0:T(8,128)(2,1)S(1)}, u32[]{:S(2)}, u32[]{:S(2)}) collective-permute-start(bf16[512,512]{1,0:T(8,128)(2,1)S(1)} %get-tuple-element.100), channel_id=1, source_target_pairs={{64,0},{17,1},{66,2},{19,3},{68,4},{21,5},{70,6},{23,7},{72,8},{25... | collective-permute-start | bytes 1572872 | tf_op jit(solution)/shard_map/ppermute | solution.py:55
  54.4 4.1 %sides_1.2.refs_4_ = f32[1024,512]{1,0:T(8,128)S(1)} custom-call(s32[632]{0:T(1024)S(1)} %sort_tiles.1.refs_0_, s32[193,5,128]{2,1,0:T(8,128)S(1)} %concatenate.3.refs_1_, bf16[1040,512]{1,0:T(8,128)(2,1)S(1)} %first.1.refs_2_.own, bf16[1536,512]{1,0:T(8,128)(2,1)S(1)} %collective-permute-done.10.refs_3_, bf16[512,512]{1,0:T(8,128)(2,1)S(1)} %get-tuple-element.86.refs_4_, ...), custom_call_target="tpu_custom_call" | custom-call | tf_op jit(solution)/shard_map/sides_1/pallas_call | solution.py:422
  58.8 3.5 %sides_3.2.refs_4_ = f32[1024,512]{1,0:T(8,128)S(1)} custom-call(s32[632]{0:T(1024)S(1)} %sort_tiles.1.refs_0_, s32[193,5,128]{2,1,0:T(8,128)S(1)} %concatenate.3.refs_1_, bf16[1040,512]{1,0:T(8,128)(2,1)S(1)} %first.1.refs_2_.own, bf16[1536,512]{1,0:T(8,128)(2,1)S(1)} %collective-permute-done.11.refs_3_, f32[1024,512]{1,0:T(8,128)S(1)} %sides_1.2.refs_4_), custom_call_target="tpu_custom_call" | custom-call | tf_op jit(solution)/shard_map/sides_3/pallas_call | solution.py:422
  62.4 3.5 %collective-permute-start.15 = (f32[8,512]{1,0:T(8,128)S(1)}, f32[8,512]{1,0:T(8,128)S(1)}, u32[]{:S(2)}, u32[]{:S(2)}) collective-permute-start(f32[8,512]{1,0:T(8,128)S(1)} %add.42), channel_id=1, source_target_pairs={{0,4},{2,6},{4,0},{6,2},{1,5},{3,7},{5,1},{7,3},{8,12},{10,14},{12... | collective-permute-start | bytes 49160 | tf_op jit(solution)/shard_map/ppermute | solution.py:59
  66.0 4.9 %collective-permute-done.12.refs_3_ = bf16[1536,512]{1,0:T(8,128)(2,1)S(1)} collective-permute-done((bf16[1536,512]{1,0:T(8,128)(2,1)S(1)}, bf16[1536,512]{1,0:T(8,128)(2,1)S(1)}, u32[]{:S(2)}, u32[]{:S(2)}) %collective-permute-start.12) | collective-permute-done | bytes 1572896 | tf_op jit(solution)/shard_map/ppermute | solution.py:55
  70.8 4.2 %across.2.refs_5_ = f32[1024,512]{1,0:T(8,128)S(1)} custom-call(s32[632]{0:T(1024)S(1)} %sort_tiles.1.refs_0_, s32[193,5,128]{2,1,0:T(8,128)S(1)} %concatenate.3.refs_1_, bf16[1040,512]{1,0:T(8,128)(2,1)S(1)} %first.1.refs_2_.own, bf16[1536,512]{1,0:T(8,128)(2,1)S(1)} %collective-permute-done.12.refs_3_, f32[1024,512]{1,0:T(8,128)S(1)} %sides_3.2.refs_4_), custom_call_target="tpu_custom_call" | custom-call | tf_op jit(solution)/shard_map/across/pallas_call | solution.py:422
  75.6 0.7 collective-permute-done.17.refs_4_
  76.4 4.3 %late.2.refs_4_ = f32[1024,512]{1,0:T(8,128)S(1)} custom-call(s32[632]{0:T(1024)S(1)} %sort_tiles.1.refs_0_, s32[193,5,128]{2,1,0:T(8,128)S(1)} %concatenate.3.refs_1_, bf16[1040,512]{1,0:T(8,128)(2,1)S(1)} %first.1.refs_2_.own, bf16[512,512]{1,0:T(8,128)(2,1)S(1)} %collective-permute-done.16.refs_3_, bf16[512,512]{1,0:T(8,128)(2,1)S(1)} %collective-permute-done.17.refs_4_, ...), custom_call_target="tpu_custom_call" | custom-call | tf_op jit(solution)/shard_map/late/pallas_call | solution.py:422
  80.6 1.4 collective-permute-done.18.refs_3_
  82.0 2.6 %last.2 = (f32[1024,512]{1,0:T(8,128)S(1)}, bf16[1040,512]{1,0:T(8,128)(2,1)S(1)}) custom-call(s32[632]{0:T(1024)S(1)} %sort_tiles.1.refs_0_, s32[193,5,128]{2,1,0:T(8,128)S(1)} %concatenate.3.refs_1_, bf16[1040,512]{1,0:T(8,128)(2,1)S(1)} %first.1.refs_2_.own, bf16[512,512]{1,0:T(8,128)(2,1)S(1)} %collective-permute-done.18.refs_3_, ...), custom_call_target="tpu_custom_call" | custom-call | tf_op jit(solution)/shard_map/last/pallas_call | solution.py:422
  84.6 1.0 collective-permute-start.20
  85.6 2.3 %collective-permute-start.19 = (bf16[1040,512]{1,0:T(8,128)(2,1)S(1)}, bf16[1040,512]{1,0:T(8,128)(2,1)S(1)}, u32[]{:S(2)}, u32[]{:S(2)}) collective-permute-start(bf16[1040,512]{1,0:T(8,128)(2,1)S(1)} %get-tuple-element.104.refs_2_.own), channel_id=1, source_target_pairs={{8,0},{33,1},{10,2},{35,3},{12,4},{37,5},{14,6},{39,7},{16,8},{41,... | collective-permute-start | bytes 3194888 | tf_op jit(solution)/shard_map/ppermute | solution.py:55
  87.9 12.9 %collective-permute-done.20.far3 = bf16[1040,512]{1,0:T(8,128)(2,1)S(1)} collective-permute-done((bf16[1040,512]{1,0:T(8,128)(2,1)S(1)}, bf16[1040,512]{1,0:T(8,128)(2,1)S(1)}, u32[]{:S(2)}, u32[]{:S(2)}) %collective-permute-start.20) | collective-permute-done | bytes 1064992 | tf_op jit(solution)/shard_map/ppermute | solution.py:55
  100.8 0.9 collective-permute-done.19.far1
  101.7 0.8 pick_early.3
  102.5 1.7 collective-permute-start.26
  104.6 0.7 pick_pass.3
  105.3 2.3 %collective-permute-start.22 = (bf16[528,512]{1,0:T(8,128)(2,1)S(1)}, bf16[528,512]{1,0:T(8,128)(2,1)S(1)}, u32[]{:S(2)}, u32[]{:S(2)}) collective-permute-start(bf16[528,512]{1,0:T(8,128)(2,1)S(1)} %get-tuple-element.107), channel_id=1, source_target_pairs={{24,0},{97,1},{26,2},{99,3},{28,4},{101,5},{30,6},{103,7},{0,8},{1... | collective-permute-start | bytes 1622024 | tf_op jit(solution)/shard_map/ppermute | solution.py:55
  107.6 1.5 collective-permute-start.21
  109.1 2.8 %near.3.refs_5_ = f32[1024,512]{1,0:T(8,128)S(1)} custom-call(s32[632]{0:T(1024)S(1)} %sort_tiles.1.refs_0_, s32[193,5,128]{2,1,0:T(8,128)S(1)} %concatenate.3.refs_1_, bf16[1040,512]{1,0:T(8,128)(2,1)S(1)} %get-tuple-element.104.refs_2_.own, bf16[1024,512]{1,0:T(8,128)(2,1)S(1)} %get-tuple-element.105.refs_3_), custom_call_target="tpu_custom_call" | custom-call | tf_op jit(solution)/shard_map/near/pallas_call | solution.py:422
  111.9 11.2 %collective-permute-done.21.low2 = bf16[512,512]{1,0:T(8,128)(2,1)S(1)} collective-permute-done((bf16[512,512]{1,0:T(8,128)(2,1)S(1)}, bf16[512,512]{1,0:T(8,128)(2,1)S(1)}, u32[]{:S(2)}, u32[]{:S(2)}) %collective-permute-start.21) | collective-permute-done | bytes 524320 | tf_op jit(solution)/shard_map/ppermute | solution.py:55
  123.1 0.9 pick_late.3
  124.0 1.0 collective-permute-start.25
  125.0 2.5 %collective-permute-start.24 = (f32[8,512]{1,0:T(8,128)S(1)}, f32[8,512]{1,0:T(8,128)S(1)}, u32[]{:S(2)}, u32[]{:S(2)}) collective-permute-start(f32[8,512]{1,0:T(8,128)S(1)} %get-tuple-element.110), channel_id=1, source_target_pairs={{96,0},{25,1},{98,2},{27,3},{100,4},{29,5},{102,6},{31,7},{104,8},... | collective-permute-start | bytes 49160 | tf_op jit(solution)/shard_map/ppermute | solution.py:55
  127.5 0.7 collective-permute-start.23
  128.2 1.1 collective-permute-done.25
  129.9 1.3 collective-permute-done.23
  131.3 0.7 collective-permute-start.28
  132.0 2.1 %collective-permute-start.32 = (bf16[512,512]{1,0:T(8,128)(2,1)S(1)}, bf16[512,512]{1,0:T(8,128)(2,1)S(1)}, u32[]{:S(2)}, u32[]{:S(2)}) collective-permute-start(bf16[512,512]{1,0:T(8,128)(2,1)S(1)} %get-tuple-element.127), channel_id=1, source_target_pairs={{32,0},{9,1},{34,2},{11,3},{36,4},{13,5},{38,6},{15,7},{40,8},{17,... | collective-permute-start | bytes 1572872 | tf_op jit(solution)/shard_map/ppermute | solution.py:55
  134.1 2.8 %collective-permute-start.34 = (bf16[512,512]{1,0:T(8,128)(2,1)S(1)}, bf16[512,512]{1,0:T(8,128)(2,1)S(1)}, u32[]{:S(2)}, u32[]{:S(2)}) collective-permute-start(bf16[512,512]{1,0:T(8,128)(2,1)S(1)} %get-tuple-element.132), channel_id=1, source_target_pairs={{64,0},{17,1},{66,2},{19,3},{68,4},{21,5},{70,6},{23,7},{72,8},{25... | collective-permute-start | bytes 1572872 | tf_op jit(solution)/shard_map/ppermute | solution.py:55
  136.9 4.1 %sides_1.3.refs_4_ = f32[1024,512]{1,0:T(8,128)S(1)} custom-call(s32[632]{0:T(1024)S(1)} %sort_tiles.1.refs_0_, s32[193,5,128]{2,1,0:T(8,128)S(1)} %concatenate.3.refs_1_, bf16[1040,512]{1,0:T(8,128)(2,1)S(1)} %get-tuple-element.104.refs_2_.own, bf16[1536,512]{1,0:T(8,128)(2,1)S(1)} %collective-permute-done.26.refs_3_, ...), custom_call_target="tpu_custom_call" | custom-call | tf_op jit(solution)/shard_map/sides_1/pallas_call | solution.py:422
  141.1 3.5 %sides_3.3.refs_4_ = f32[1024,512]{1,0:T(8,128)S(1)} custom-call(s32[632]{0:T(1024)S(1)} %sort_tiles.1.refs_0_, s32[193,5,128]{2,1,0:T(8,128)S(1)} %concatenate.3.refs_1_, bf16[1040,512]{1,0:T(8,128)(2,1)S(1)} %get-tuple-element.104.refs_2_.own, bf16[1536,512]{1,0:T(8,128)(2,1)S(1)} %collective-permute-done.27.refs_3_, f32[1024,512]{1,0:T(8,128)S(1)} %sides_1.3.refs_4_), custom_call_target="tpu_custom_call" | custom-call | tf_op jit(solution)/shard_map/sides_3/pallas_call | solution.py:422
  144.9 3.9 %collective-permute-start.31 = (f32[8,512]{1,0:T(8,128)S(1)}, f32[8,512]{1,0:T(8,128)S(1)}, u32[]{:S(2)}, u32[]{:S(2)}) collective-permute-start(f32[8,512]{1,0:T(8,128)S(1)} %add.48), channel_id=1, source_target_pairs={{0,4},{2,6},{4,0},{6,2},{1,5},{3,7},{5,1},{7,3},{8,12},{10,14},{12... | collective-permute-start | bytes 49160 | tf_op jit(solution)/shard_map/ppermute | solution.py:59
  148.8 4.5 %collective-permute-done.28.refs_3_ = bf16[1536,512]{1,0:T(8,128)(2,1)S(1)} collective-permute-done((bf16[1536,512]{1,0:T(8,128)(2,1)S(1)}, bf16[1536,512]{1,0:T(8,128)(2,1)S(1)}, u32[]{:S(2)}, u32[]{:S(2)}) %collective-permute-start.28) | collective-permute-done | bytes 1572896 | tf_op jit(solution)/shard_map/ppermute | solution.py:55
  153.3 4.0 %across.3.refs_5_ = f32[1024,512]{1,0:T(8,128)S(1)} custom-call(s32[632]{0:T(1024)S(1)} %sort_tiles.1.refs_0_, s32[193,5,128]{2,1,0:T(8,128)S(1)} %concatenate.3.refs_1_, bf16[1040,512]{1,0:T(8,128)(2,1)S(1)} %get-tuple-element.104.refs_2_.own, bf16[1536,512]{1,0:T(8,128)(2,1)S(1)} %collective-permute-done.28.refs_3_, f32[1024,512]{1,0:T(8,128)S(1)} %sides_3.3.refs_4_), custom_call_target="tpu_custom_call" | custom-call | tf_op jit(solution)/shard_map/across/pallas_call | solution.py:422
  157.3 0.8 collective-permute-done.32.refs_3_
  158.1 0.7 collective-permute-done.33.refs_4_
  158.8 4.0 %late.3.refs_4_ = f32[1024,512]{1,0:T(8,128)S(1)} custom-call(s32[632]{0:T(1024)S(1)} %sort_tiles.1.refs_0_, s32[193,5,128]{2,1,0:T(8,128)S(1)} %concatenate.3.refs_1_, bf16[1040,512]{1,0:T(8,128)(2,1)S(1)} %get-tuple-element.104.refs_2_.own, bf16[512,512]{1,0:T(8,128)(2,1)S(1)} %collective-permute-done.32.refs_3_, ...), custom_call_target="tpu_custom_call" | custom-call | tf_op jit(solution)/shard_map/late/pallas_call | solution.py:422
  162.9 1.6 collective-permute-done.34.refs_3_
  164.5 3.5 %last.3 = f32[1024,512]{1,0:T(8,128)} custom-call(s32[632]{0:T(1024)S(1)} %sort_tiles.1.refs_0_, s32[193,5,128]{2,1,0:T(8,128)S(1)} %concatenate.3.refs_1_, bf16[1040,512]{1,0:T(8,128)(2,1)S(1)} %get-tuple-element.104.refs_2_.own, bf16[512,512]{1,0:T(8,128)(2,1)S(1)} %collective-permute-done.34.refs_3_, f32[1024,512]{1,0:T(8,128)S(1)} %late.3.refs_4_, ...), custom_call_target="tpu_custom_call" | custom-call | tf_op jit(solution)/shard_map/last/pallas_call | solution.py:422
  (54 shorter events, 4.1 us)
Async XLA Ops:
  0.0 1.6 copy-start
  1.6 4.2 %copy-start.2 = (s32[1024]{0:T(1024)S(1)}, s32[1024]{0:T(1024)}, u32[]{:S(2)}) copy-start(s32[1024]{0:T(1024)} %home.1) | copy-start | bytes 12292
  1.6 4.2 %copy-start.3 = (s32[1,240]{1,0:T(1,128)S(1)}, s32[1,240]{1,0:T(1,128)}, u32[]{:S(2)}) copy-start(s32[1,240]{1,0:T(1,128)} %param.8) | copy-start | bytes 2884
  1.6 4.2 %copy-start.4 = (s32[1,240]{1,0:T(1,128)S(1)}, s32[1,240]{1,0:T(1,128)}, u32[]{:S(2)}) copy-start(s32[1,240]{1,0:T(1,128)} %param.9) | copy-start | bytes 2884
  1.7 16.3 %collective-permute-start.4 = (bf16[1040,512]{1,0:T(8,128)(2,1)S(1)}, bf16[1040,512]{1,0:T(8,128)(2,1)S(1)}, u32[]{:S(2)}, u32[]{:S(2)}) collective-permute-start(bf16[1040,512]{1,0:T(8,128)(2,1)S(1)} %first.1.refs_2_.own), channel_id=1, source_target_pairs={{24,0},{97,1},{26,2},{99,3},{28,4},{101,5},{30,6},{103,7},{0,8},{1... | collective-permute-start | bytes 3194888 | tf_op jit(solution)/shard_map/ppermute | solution.py:55
  3.3 15.0 %collective-permute-start.3 = (bf16[1040,512]{1,0:T(8,128)(2,1)S(1)}, bf16[1040,512]{1,0:T(8,128)(2,1)S(1)}, u32[]{:S(2)}, u32[]{:S(2)}) collective-permute-start(bf16[1040,512]{1,0:T(8,128)(2,1)S(1)} %first.1.refs_2_.own), channel_id=1, source_target_pairs={{8,0},{33,1},{10,2},{35,3},{12,4},{37,5},{14,6},{39,7},{16,8},{41,... | collective-permute-start | bytes 3194888 | tf_op jit(solution)/shard_map/ppermute | solution.py:55
  9.6 4.5 %collective-permute-start.2 = (s32[16]{0:T(128)S(1)}, s32[16]{0:T(128)S(1)}, u32[]{:S(2)}, u32[]{:S(2)}) collective-permute-start(s32[16]{0:T(128)S(1)} %get-tuple-element.138), channel_id=1, source_target_pairs={{32,0},{9,1},{34,2},{11,3},{36,4},{13,5},{38,6},{15,7},{40,8},{17,... | collective-permute-start | bytes 200 | tf_op jit(solution)/shard_map/ppermute | solution.py:55
  12.2 5.1 %collective-permute-start.1 = (s32[16]{0:T(128)S(1)}, s32[16]{0:T(128)S(1)}, u32[]{:S(2)}, u32[]{:S(2)}) collective-permute-start(s32[16]{0:T(128)S(1)} %get-tuple-element.139), channel_id=1, source_target_pairs={{64,0},{17,1},{66,2},{19,3},{68,4},{21,5},{70,6},{23,7},{72,8},{25... | collective-permute-start | bytes 200 | tf_op jit(solution)/shard_map/ppermute | solution.py:55
  13.0 4.8 %collective-permute-start = (s32[16]{0:T(128)S(1)}, s32[16]{0:T(128)S(1)}, u32[]{:S(2)}, u32[]{:S(2)}) collective-permute-start(s32[16]{0:T(128)S(1)} %get-tuple-element.140), channel_id=1, source_target_pairs={{96,0},{25,1},{98,2},{27,3},{100,4},{29,5},{102,6},{31,7},{104,8},... | collective-permute-start | bytes 200 | tf_op jit(solution)/shard_map/ppermute | solution.py:55
  19.1 7.1 %copy-start.6 = (s32[192,5,128]{2,0,1:T(8,128)S(1)}, s32[192,5,128]{2,0,1:T(8,128)}, u32[]{:S(2)}) copy-start(s32[192,5,128]{2,0,1:T(8,128)} %param.13) | copy-start | bytes 1474564
  19.1 29.7 %collective-permute-start.10 = (bf16[1536,512]{1,0:T(8,128)(2,1)S(1)}, bf16[1536,512]{1,0:T(8,128)(2,1)S(1)}, u32[]{:S(2)}, u32[]{:S(2)}) collective-permute-start(bf16[1536,512]{1,0:T(8,128)(2,1)S(1)} %get-tuple-element.81), channel_id=1, source_target_pairs={{32,0},{9,1},{34,2},{11,3},{36,4},{13,5},{38,6},{15,7},{40,8},{17,... | collective-permute-start | bytes 4718600 | tf_op jit(solution)/shard_map/ppermute | solution.py:55
  22.2 26.6 %collective-permute-start.11 = (bf16[1536,512]{1,0:T(8,128)(2,1)S(1)}, bf16[1536,512]{1,0:T(8,128)(2,1)S(1)}, u32[]{:S(2)}, u32[]{:S(2)}) collective-permute-start(bf16[1536,512]{1,0:T(8,128)(2,1)S(1)} %get-tuple-element.82), channel_id=1, source_target_pairs={{96,0},{25,1},{98,2},{27,3},{100,4},{29,5},{102,6},{31,7},{104,8},... | collective-permute-start | bytes 4718600 | tf_op jit(solution)/shard_map/ppermute | solution.py:55
  22.8 3.7 %copy-start.5 = (s32[1,240]{1,0:T(1,128)S(1)}, s32[1,240]{1,0:T(1,128)}, u32[]{:S(2)}) copy-start(s32[1,240]{1,0:T(1,128)} %param.10) | copy-start | bytes 2884
  22.9 16.5 %collective-permute-start.6 = (bf16[528,512]{1,0:T(8,128)(2,1)S(1)}, bf16[528,512]{1,0:T(8,128)(2,1)S(1)}, u32[]{:S(2)}, u32[]{:S(2)}) collective-permute-start(bf16[528,512]{1,0:T(8,128)(2,1)S(1)} %get-tuple-element.75), channel_id=1, source_target_pairs={{24,0},{97,1},{26,2},{99,3},{28,4},{101,5},{30,6},{103,7},{0,8},{1... | collective-permute-start | bytes 1622024 | tf_op jit(solution)/shard_map/ppermute | solution.py:55
  24.4 14.9 %collective-permute-start.5 = (bf16[512,512]{1,0:T(8,128)(2,1)S(1)}, bf16[512,512]{1,0:T(8,128)(2,1)S(1)}, u32[]{:S(2)}, u32[]{:S(2)}) collective-permute-start(bf16[512,512]{1,0:T(8,128)(2,1)S(1)} %get-tuple-element.74), channel_id=1, source_target_pairs={{8,0},{33,1},{10,2},{35,3},{12,4},{37,5},{14,6},{39,7},{16,8},{41,... | collective-permute-start | bytes 1572872 | tf_op jit(solution)/shard_map/ppermute | solution.py:55
  40.2 8.5 %collective-permute-start.9 = (f32[8,512]{1,0:T(8,128)S(1)}, f32[8,512]{1,0:T(8,128)S(1)}, u32[]{:S(2)}, u32[]{:S(2)}) collective-permute-start(f32[8,512]{1,0:T(8,128)S(1)} %get-tuple-element.78), channel_id=1, source_target_pairs={{64,0},{17,1},{66,2},{19,3},{68,4},{21,5},{70,6},{23,7},{72,8},{25... | collective-permute-start | bytes 49160 | tf_op jit(solution)/shard_map/ppermute | solution.py:55
  42.5 6.2 %collective-permute-start.8 = (f32[8,512]{1,0:T(8,128)S(1)}, f32[8,512]{1,0:T(8,128)S(1)}, u32[]{:S(2)}, u32[]{:S(2)}) collective-permute-start(f32[8,512]{1,0:T(8,128)S(1)} %get-tuple-element.78), channel_id=1, source_target_pairs={{96,0},{25,1},{98,2},{27,3},{100,4},{29,5},{102,6},{31,7},{104,8},... | collective-permute-start | bytes 49160 | tf_op jit(solution)/shard_map/ppermute | solution.py:55
  44.4 4.3 %collective-permute-start.7 = (f32[8,512]{1,0:T(8,128)S(1)}, f32[8,512]{1,0:T(8,128)S(1)}, u32[]{:S(2)}, u32[]{:S(2)}) collective-permute-start(f32[8,512]{1,0:T(8,128)S(1)} %get-tuple-element.78), channel_id=1, source_target_pairs={{32,0},{9,1},{34,2},{11,3},{36,4},{13,5},{38,6},{15,7},{40,8},{17,... | collective-permute-start | bytes 49160 | tf_op jit(solution)/shard_map/ppermute | solution.py:55
  48.7 22.1 %collective-permute-start.12 = (bf16[1536,512]{1,0:T(8,128)(2,1)S(1)}, bf16[1536,512]{1,0:T(8,128)(2,1)S(1)}, u32[]{:S(2)}, u32[]{:S(2)}) collective-permute-start(bf16[1536,512]{1,0:T(8,128)(2,1)S(1)} %get-tuple-element.83), channel_id=1, source_target_pairs={{64,0},{17,1},{66,2},{19,3},{68,4},{21,5},{70,6},{23,7},{72,8},{25... | collective-permute-start | bytes 4718600 | tf_op jit(solution)/shard_map/ppermute | solution.py:55
  49.8 25.9 %collective-permute-start.16 = (bf16[512,512]{1,0:T(8,128)(2,1)S(1)}, bf16[512,512]{1,0:T(8,128)(2,1)S(1)}, u32[]{:S(2)}, u32[]{:S(2)}) collective-permute-start(bf16[512,512]{1,0:T(8,128)(2,1)S(1)} %get-tuple-element.95), channel_id=1, source_target_pairs={{32,0},{9,1},{34,2},{11,3},{36,4},{13,5},{38,6},{15,7},{40,8},{17,... | collective-permute-start | bytes 1572872 | tf_op jit(solution)/shard_map/ppermute | solution.py:55
  51.1 25.3 %collective-permute-start.17 = (bf16[512,512]{1,0:T(8,128)(2,1)S(1)}, bf16[512,512]{1,0:T(8,128)(2,1)S(1)}, u32[]{:S(2)}, u32[]{:S(2)}) collective-permute-start(bf16[512,512]{1,0:T(8,128)(2,1)S(1)} %get-tuple-element.96), channel_id=1, source_target_pairs={{96,0},{25,1},{98,2},{27,3},{100,4},{29,5},{102,6},{31,7},{104,8},... | collective-permute-start | bytes 1572872 | tf_op jit(solution)/shard_map/ppermute | solution.py:55
  51.8 30.2 %collective-permute-start.18 = (bf16[512,512]{1,0:T(8,128)(2,1)S(1)}, bf16[512,512]{1,0:T(8,128)(2,1)S(1)}, u32[]{:S(2)}, u32[]{:S(2)}) collective-permute-start(bf16[512,512]{1,0:T(8,128)(2,1)S(1)} %get-tuple-element.100), channel_id=1, source_target_pairs={{64,0},{17,1},{66,2},{19,3},{68,4},{21,5},{70,6},{23,7},{72,8},{25... | collective-permute-start | bytes 1572872 | tf_op jit(solution)/shard_map/ppermute | solution.py:55
  54.4 4.2 %collective-permute-start.13 = (f32[8,512]{1,0:T(8,128)S(1)}, f32[8,512]{1,0:T(8,128)S(1)}, u32[]{:S(2)}, u32[]{:S(2)}) collective-permute-start(f32[8,512]{1,0:T(8,128)S(1)} %add_add_fusion.1), channel_id=1, source_target_pairs={{0,1},{1,0},{2,3},{3,2},{4,5},{5,4},{6,7},{7,6},{8,9},{9,8},{10,11... | collective-permute-start | bytes 49160 | tf_op jit(solution)/shard_map/ppermute | solution.py:59
  58.6 3.9 %collective-permute-start.14 = (f32[8,512]{1,0:T(8,128)S(1)}, f32[8,512]{1,0:T(8,128)S(1)}, u32[]{:S(2)}, u32[]{:S(2)}) collective-permute-start(f32[8,512]{1,0:T(8,128)S(1)} %add.41), channel_id=1, source_target_pairs={{0,2},{2,0},{4,6},{6,4},{1,3},{3,1},{5,7},{7,5},{8,10},{10,8},{12,... | collective-permute-start | bytes 49160 | tf_op jit(solution)/shard_map/ppermute | solution.py:59
  62.4 13.9 %collective-permute-start.15 = (f32[8,512]{1,0:T(8,128)S(1)}, f32[8,512]{1,0:T(8,128)S(1)}, u32[]{:S(2)}, u32[]{:S(2)}) collective-permute-start(f32[8,512]{1,0:T(8,128)S(1)} %add.42), channel_id=1, source_target_pairs={{0,4},{2,6},{4,0},{6,2},{1,5},{3,7},{5,1},{7,3},{8,12},{10,14},{12... | collective-permute-start | bytes 49160 | tf_op jit(solution)/shard_map/ppermute | solution.py:59
  76.4 5.7 %copy-start.1 = (f32[1024,512]{1,0:T(8,128)S(1)}, f32[1024,512]{1,0:T(8,128)}, u32[]{:S(2)}) copy-start(f32[1024,512]{1,0:T(8,128)} %refs_5_.1) | copy-start | bytes 6291460
  84.6 16.3 %collective-permute-start.20 = (bf16[1040,512]{1,0:T(8,128)(2,1)S(1)}, bf16[1040,512]{1,0:T(8,128)(2,1)S(1)}, u32[]{:S(2)}, u32[]{:S(2)}) collective-permute-start(bf16[1040,512]{1,0:T(8,128)(2,1)S(1)} %get-tuple-element.104.refs_2_.own), channel_id=1, source_target_pairs={{24,0},{97,1},{26,2},{99,3},{28,4},{101,5},{30,6},{103,7},{0,8},{1... | collective-permute-start | bytes 3194888 | tf_op jit(solution)/shard_map/ppermute | solution.py:55
  85.6 16.2 %collective-permute-start.19 = (bf16[1040,512]{1,0:T(8,128)(2,1)S(1)}, bf16[1040,512]{1,0:T(8,128)(2,1)S(1)}, u32[]{:S(2)}, u32[]{:S(2)}) collective-permute-start(bf16[1040,512]{1,0:T(8,128)(2,1)S(1)} %get-tuple-element.104.refs_2_.own), channel_id=1, source_target_pairs={{8,0},{33,1},{10,2},{35,3},{12,4},{37,5},{14,6},{39,7},{16,8},{41,... | collective-permute-start | bytes 3194888 | tf_op jit(solution)/shard_map/ppermute | solution.py:55
  102.5 28.8 %collective-permute-start.26 = (bf16[1536,512]{1,0:T(8,128)(2,1)S(1)}, bf16[1536,512]{1,0:T(8,128)(2,1)S(1)}, u32[]{:S(2)}, u32[]{:S(2)}) collective-permute-start(bf16[1536,512]{1,0:T(8,128)(2,1)S(1)} %get-tuple-element.113), channel_id=1, source_target_pairs={{32,0},{9,1},{34,2},{11,3},{36,4},{13,5},{38,6},{15,7},{40,8},{17,... | collective-permute-start | bytes 4718600 | tf_op jit(solution)/shard_map/ppermute | solution.py:55
  104.2 27.1 %collective-permute-start.27 = (bf16[1536,512]{1,0:T(8,128)(2,1)S(1)}, bf16[1536,512]{1,0:T(8,128)(2,1)S(1)}, u32[]{:S(2)}, u32[]{:S(2)}) collective-permute-start(bf16[1536,512]{1,0:T(8,128)(2,1)S(1)} %get-tuple-element.114), channel_id=1, source_target_pairs={{96,0},{25,1},{98,2},{27,3},{100,4},{29,5},{102,6},{31,7},{104,8},... | collective-permute-start | bytes 4718600 | tf_op jit(solution)/shard_map/ppermute | solution.py:55
  105.3 17.8 %collective-permute-start.22 = (bf16[528,512]{1,0:T(8,128)(2,1)S(1)}, bf16[528,512]{1,0:T(8,128)(2,1)S(1)}, u32[]{:S(2)}, u32[]{:S(2)}) collective-permute-start(bf16[528,512]{1,0:T(8,128)(2,1)S(1)} %get-tuple-element.107), channel_id=1, source_target_pairs={{24,0},{97,1},{26,2},{99,3},{28,4},{101,5},{30,6},{103,7},{0,8},{1... | collective-permute-start | bytes 1622024 | tf_op jit(solution)/shard_map/ppermute | solution.py:55
  107.6 15.5 %collective-permute-start.21 = (bf16[512,512]{1,0:T(8,128)(2,1)S(1)}, bf16[512,512]{1,0:T(8,128)(2,1)S(1)}, u32[]{:S(2)}, u32[]{:S(2)}) collective-permute-start(bf16[512,512]{1,0:T(8,128)(2,1)S(1)} %get-tuple-element.106), channel_id=1, source_target_pairs={{8,0},{33,1},{10,2},{35,3},{12,4},{37,5},{14,6},{39,7},{16,8},{41,... | collective-permute-start | bytes 1572872 | tf_op jit(solution)/shard_map/ppermute | solution.py:55
  124.0 5.3 %collective-permute-start.25 = (f32[8,512]{1,0:T(8,128)S(1)}, f32[8,512]{1,0:T(8,128)S(1)}, u32[]{:S(2)}, u32[]{:S(2)}) collective-permute-start(f32[8,512]{1,0:T(8,128)S(1)} %get-tuple-element.110), channel_id=1, source_target_pairs={{64,0},{17,1},{66,2},{19,3},{68,4},{21,5},{70,6},{23,7},{72,8},{25... | collective-permute-start | bytes 49160 | tf_op jit(solution)/shard_map/ppermute | solution.py:55
  125.0 4.9 %collective-permute-start.24 = (f32[8,512]{1,0:T(8,128)S(1)}, f32[8,512]{1,0:T(8,128)S(1)}, u32[]{:S(2)}, u32[]{:S(2)}) collective-permute-start(f32[8,512]{1,0:T(8,128)S(1)} %get-tuple-element.110), channel_id=1, source_target_pairs={{96,0},{25,1},{98,2},{27,3},{100,4},{29,5},{102,6},{31,7},{104,8},... | collective-permute-start | bytes 49160 | tf_op jit(solution)/shard_map/ppermute | solution.py:55
  127.5 3.7 %collective-permute-start.23 = (f32[8,512]{1,0:T(8,128)S(1)}, f32[8,512]{1,0:T(8,128)S(1)}, u32[]{:S(2)}, u32[]{:S(2)}) collective-permute-start(f32[8,512]{1,0:T(8,128)S(1)} %get-tuple-element.110), channel_id=1, source_target_pairs={{32,0},{9,1},{34,2},{11,3},{36,4},{13,5},{38,6},{15,7},{40,8},{17,... | collective-permute-start | bytes 49160 | tf_op jit(solution)/shard_map/ppermute | solution.py:55
  131.3 22.0 %collective-permute-start.28 = (bf16[1536,512]{1,0:T(8,128)(2,1)S(1)}, bf16[1536,512]{1,0:T(8,128)(2,1)S(1)}, u32[]{:S(2)}, u32[]{:S(2)}) collective-permute-start(bf16[1536,512]{1,0:T(8,128)(2,1)S(1)} %get-tuple-element.115), channel_id=1, source_target_pairs={{64,0},{17,1},{66,2},{19,3},{68,4},{21,5},{70,6},{23,7},{72,8},{25... | collective-permute-start | bytes 4718600 | tf_op jit(solution)/shard_map/ppermute | solution.py:55
  132.0 26.1 %collective-permute-start.32 = (bf16[512,512]{1,0:T(8,128)(2,1)S(1)}, bf16[512,512]{1,0:T(8,128)(2,1)S(1)}, u32[]{:S(2)}, u32[]{:S(2)}) collective-permute-start(bf16[512,512]{1,0:T(8,128)(2,1)S(1)} %get-tuple-element.127), channel_id=1, source_target_pairs={{32,0},{9,1},{34,2},{11,3},{36,4},{13,5},{38,6},{15,7},{40,8},{17,... | collective-permute-start | bytes 1572872 | tf_op jit(solution)/shard_map/ppermute | solution.py:55
  134.1 24.8 %collective-permute-start.33 = (bf16[512,512]{1,0:T(8,128)(2,1)S(1)}, bf16[512,512]{1,0:T(8,128)(2,1)S(1)}, u32[]{:S(2)}, u32[]{:S(2)}) collective-permute-start(bf16[512,512]{1,0:T(8,128)(2,1)S(1)} %get-tuple-element.128), channel_id=1, source_target_pairs={{96,0},{25,1},{98,2},{27,3},{100,4},{29,5},{102,6},{31,7},{104,8},... | collective-permute-start | bytes 1572872 | tf_op jit(solution)/shard_map/ppermute | solution.py:55
  134.1 30.4 %collective-permute-start.34 = (bf16[512,512]{1,0:T(8,128)(2,1)S(1)}, bf16[512,512]{1,0:T(8,128)(2,1)S(1)}, u32[]{:S(2)}, u32[]{:S(2)}) collective-permute-start(bf16[512,512]{1,0:T(8,128)(2,1)S(1)} %get-tuple-element.132), channel_id=1, source_target_pairs={{64,0},{17,1},{66,2},{19,3},{68,4},{21,5},{70,6},{23,7},{72,8},{25... | collective-permute-start | bytes 1572872 | tf_op jit(solution)/shard_map/ppermute | solution.py:55
  136.8 4.1 %collective-permute-start.29 = (f32[8,512]{1,0:T(8,128)S(1)}, f32[8,512]{1,0:T(8,128)S(1)}, u32[]{:S(2)}, u32[]{:S(2)}) collective-permute-start(f32[8,512]{1,0:T(8,128)S(1)} %add_add_fusion), channel_id=1, source_target_pairs={{0,1},{1,0},{2,3},{3,2},{4,5},{5,4},{6,7},{7,6},{8,9},{9,8},{10,11... | collective-permute-start | bytes 49160 | tf_op jit(solution)/shard_map/ppermute | solution.py:59
  141.0 3.9 %collective-permute-start.30 = (f32[8,512]{1,0:T(8,128)S(1)}, f32[8,512]{1,0:T(8,128)S(1)}, u32[]{:S(2)}, u32[]{:S(2)}) collective-permute-start(f32[8,512]{1,0:T(8,128)S(1)} %add.47), channel_id=1, source_target_pairs={{0,2},{2,0},{4,6},{6,4},{1,3},{3,1},{5,7},{7,5},{8,10},{10,8},{12,... | collective-permute-start | bytes 49160 | tf_op jit(solution)/shard_map/ppermute | solution.py:59
  144.9 14.0 %collective-permute-start.31 = (f32[8,512]{1,0:T(8,128)S(1)}, f32[8,512]{1,0:T(8,128)S(1)}, u32[]{:S(2)}, u32[]{:S(2)}) collective-permute-start(f32[8,512]{1,0:T(8,128)S(1)} %add.48), channel_id=1, source_target_pairs={{0,4},{2,6},{4,0},{6,2},{1,5},{3,7},{5,1},{7,3},{8,12},{10,14},{12... | collective-permute-start | bytes 49160 | tf_op jit(solution)/shard_map/ppermute | solution.py:59

commit v2 on v1

--- a/solution.py
+++ b/solution.py
@@ -206,7 +206,9 @@
     out[pl.ds(at * BLOCK, BLOCK), :] = table[rows, :]
 
 
-def pick_early_kernel(asked, own, far1, far3, out1, out3):
+def pick_early_kernel(asked, own, far1, far3, pass1, pass3, out1, out3):
+    pass1[...] = far1[pl.ds(0, HALF_ROWS), :]
+    pass3[...] = far3[pl.ds(HALF_ROWS, HALF_ROWS + 16), :]
     for m, out in ((1, out1), (3, out3)):
         for i, (k, table) in enumerate(((0, own), (1, far1), (3, far3))):
             for r in range(CAP):
@@ -214,34 +216,37 @@
 
 
 def pick_early(asked, own, far1, far3):
-    out = jax.ShapeDtypeStruct((3 * CAP * BLOCK, C), jnp.bfloat16)
+    b16 = jnp.bfloat16
+    out = jax.ShapeDtypeStruct((3 * CAP * BLOCK, C), b16)
     return pl.pallas_call(
         pick_early_kernel,
-        out_shape=(out, out),
+        out_shape=(
+            jax.ShapeDtypeStruct((HALF_ROWS, C), b16),
+            jax.ShapeDtypeStruct((HALF_ROWS + 16, C), b16),
+            out,
+            out,
+        ),
         in_specs=[SMEM] + [VMEM] * 3,
-        out_specs=(VMEM,) * 2,
+        out_specs=(VMEM,) * 4,
         compiler_params=pltpu.CompilerParams(vmem_limit_bytes=20 << 20),
         name="pick_early",
     )(asked, own, far1, far3)
 
 
-def pick_pass_kernel(wanted, far1, far3, near, pass1, pass3):
-    pass1[...] = far1[pl.ds(0, HALF_ROWS), :]
-    pass3[...] = far3[pl.ds(HALF_ROWS, HALF_ROWS + 16), :]
+def pick_near_kernel(wanted, far1, far3, near):
     for r in range(CAP):
         move(far1, wanted[CAP + r], near, r)
         move(far3, wanted[3 * CAP + r], near, CAP + r)
 
 
-def pick_pass(wanted, far1, far3):
-    shape = lambda rows: jax.ShapeDtypeStruct((rows, C), jnp.bfloat16)
-    return pl.pallas_call(
-        pick_pass_kernel,
-        out_shape=(shape(2 * CAP * BLOCK), shape(HALF_ROWS), shape(HALF_ROWS + 16)),
+def pick_near(wanted, far1, far3):
+    return pl.pallas_call(
+        pick_near_kernel,
+        out_shape=jax.ShapeDtypeStruct((2 * CAP * BLOCK, C), jnp.bfloat16),
         in_specs=[SMEM] + [VMEM] * 2,
-        out_specs=(VMEM,) * 3,
+        out_specs=VMEM,
         compiler_params=pltpu.CompilerParams(vmem_limit_bytes=20 << 20),
-        name="pick_pass",
+        name="pick_near",
     )(wanted, far1, far3)
 
 
@@ -446,8 +451,8 @@
     lists = sort_tiles(codes, tile_pattern[0], tile_count)
     for step in range(STEPS):
         far1, far3 = fetch(own, 1, 0), fetch(own, 3, 0)
-        out1, out3 = pick_early(asked, own, far1, far3)
-        near, pass1, pass3 = pick_pass(requests[0], far1, far3)
+        pass1, pass3, out1, out3 = pick_early(asked, own, far1, far3)
+        near = pick_near(requests[0], far1, far3)
         low2, high2 = fetch(pass1, 1, 0), fetch(pass3, 3, 0)
         side1, side3 = fetch(out1, 0, 1), fetch(out3, 0, 3)
         (total,) = run_tiles("near", 0, lists, words, own, (near,))

time: 169 us -> 166 us (0.982)
  Pallas kernels: 56 us -> 51.9 us
  waiting for transfers between devices: 56.8 us -> 58.5 us
    pallas_call x12, Pallas kernels: 43.5 us -> 40 us  [run_tiles(): pl.pallas_call(functools.partial(tile_kernel, part, len(tables), earlier...]
    ppermute x29, waiting for transfers between devices: 56.4 us -> 58.5 us  [fetch(): return lax.ppermute(value, ALL, pairs(first, second))]
  transfers between devices with their start and end apart: 35 -> 35, of which waited for: 23 -> 19; matrix products, arithmetic and copies ran while one was open for 0% -> 0% of each run, Pallas kernels for 29% -> 27%
where the time goes in v2:
time: 166 us
  waiting for transfers between devices  58.5 us (35%)
  starting transfers between devices  52.1 us (31%)
  Pallas kernels  51.9 us (31%)
  local copies, waits for them, and re-layouts  2.06 us (1%)
    ppermute x29, waiting for transfers between devices, fetch(): return lax.ppermute(value, ALL, pairs(first, second))  58.5 us
    ppermute x29, starting transfers between devices, fetch(): return lax.ppermute(value, ALL, pairs(first, second))  43.9 us
    pallas_call x12, Pallas kernels, run_tiles(): pl.pallas_call(functools.partial(tile_kernel, part, len(tables), earlier...  40 us
    ppermute x6, starting transfers between devices, swap(): lax.ppermute(value, axis, [(i, i ^ step) for i in range(lax.axis_size(axi...  8.24 us
    pallas_call x1, Pallas kernels, sort_tiles(): pl.pallas_call(sort_kernel, out_shape=jax.ShapeDtypeStruct((LIST,), i32),...  3.64 us
    pallas_call x1, Pallas kernels, ask(): pl.pallas_call(ask_kernel, out_shape=(jax.ShapeDtypeStruct((64,), i32), j...  3.39 us
  transfers between devices with their start and end apart: 35, of which 19 were waited for; matrix products, arithmetic and copies ran while one was open for 0% of the time, Pallas kernels for 27%

profile of v2, /device:TPU:32, one launch (start us, length us, event | category | flops | bytes accessed | tf_op | source)
XLA Modules:
  0.0 165.8 jit_solution(17864055960074537851)
XLA Ops:
  0.0 1.6 copy-done
  1.7 1.6 collective-permute-start.4
  3.3 1.7 %collective-permute-start.3 = (bf16[1040,512]{1,0:T(8,128)(2,1)S(1)}, bf16[1040,512]{1,0:T(8,128)(2,1)S(1)}, u32[]{:S(2)}, u32[]{:S(2)}) collective-permute-start(bf16[1040,512]{1,0:T(8,128)(2,1)S(1)} %first.1.refs_2_.own), channel_id=1, source_target_pairs={{8,0},{33,1},{10,2},{35,3},{12,4},{37,5},{14,6},{39,7},{16,8},{41,... | collective-permute-start | bytes 3194888 | tf_op jit(solution)/shard_map/ppermute | solution.py:55
  5.8 3.4 %ask.1 = (s32[64]{0:T(128)S(1)}, s32[240]{0:T(256)S(1)}) custom-call(s32[3]{0:T(128)S(1)} %pad_add_fusion.1.place, s32[240]{0:T(256)S(1)} %bitcast.9, s32[240]{0:T(256)S(1)} %bitcast.10, s32[1]{0:T(128)S(6)} %copy.9.count, s32[1024]{0:T(1024)S(1)} %copy-done.2), custom_call_target="tpu_custom_call" | custom-call | tf_op jit(solution)/shard_map/ask/pallas_call | solution.py:115
  9.3 3.4 %collective-permute-start.2 = (s32[16]{0:T(128)S(1)}, s32[16]{0:T(128)S(1)}, u32[]{:S(2)}, u32[]{:S(2)}) collective-permute-start(s32[16]{0:T(128)S(1)} %get-tuple-element.134), channel_id=1, source_target_pairs={{32,0},{9,1},{34,2},{11,3},{36,4},{13,5},{38,6},{15,7},{40,8},{17,... | collective-permute-start | bytes 200 | tf_op jit(solution)/shard_map/ppermute | solution.py:55
  13.0 0.9 collective-permute-start
  14.0 3.8 %collective-permute-done.1 = s32[16]{0:T(128)S(1)} collective-permute-done((s32[16]{0:T(128)S(1)}, s32[16]{0:T(128)S(1)}, u32[]{:S(2)}, u32[]{:S(2)}) %collective-permute-start.1) | collective-permute-done | bytes 96 | tf_op jit(solution)/shard_map/ppermute | solution.py:55
  18.3 0.8 pick_early.2
  19.1 3.1 %collective-permute-start.10 = (bf16[1536,512]{1,0:T(8,128)(2,1)S(1)}, bf16[1536,512]{1,0:T(8,128)(2,1)S(1)}, u32[]{:S(2)}, u32[]{:S(2)}) collective-permute-start(bf16[1536,512]{1,0:T(8,128)(2,1)S(1)} %get-tuple-element.78), channel_id=1, source_target_pairs={{32,0},{9,1},{34,2},{11,3},{36,4},{13,5},{38,6},{15,7},{40,8},{17,... | collective-permute-start | bytes 4718600 | tf_op jit(solution)/shard_map/ppermute | solution.py:55
  22.2 1.5 collective-permute-start.6
  23.7 1.7 %collective-permute-start.5 = (bf16[512,512]{1,0:T(8,128)(2,1)S(1)}, bf16[512,512]{1,0:T(8,128)(2,1)S(1)}, u32[]{:S(2)}, u32[]{:S(2)}) collective-permute-start(bf16[512,512]{1,0:T(8,128)(2,1)S(1)} %get-tuple-element.71), channel_id=1, source_target_pairs={{8,0},{33,1},{10,2},{35,3},{12,4},{37,5},{14,6},{39,7},{16,8},{41,... | collective-permute-start | bytes 1572872 | tf_op jit(solution)/shard_map/ppermute | solution.py:55
  25.8 3.6 %sort_tiles.1.refs_0_ = s32[632]{0:T(1024)S(1)} custom-call(s32[240]{0:T(256)S(1)} %get-tuple-element.69.codes, s32[240]{0:T(256)S(1)} %bitcast.11, s32[1]{0:T(128)S(6)} %copy.9.count), custom_call_target="tpu_custom_call" | custom-call | tf_op jit(solution)/shard_map/sort_tiles/pallas_call | solution.py:163
  29.5 0.6 pick_near.2.refs_3_
  30.1 3.5 %near.2.refs_5_ = f32[1024,512]{1,0:T(8,128)S(1)} custom-call(s32[632]{0:T(1024)S(1)} %sort_tiles.1.refs_0_, s32[193,5,128]{2,1,0:T(8,128)S(1)} %concatenate.3.refs_1_, bf16[1040,512]{1,0:T(8,128)(2,1)S(1)} %first.1.refs_2_.own, bf16[1024,512]{1,0:T(8,128)(2,1)S(1)} %pick_near.2.refs_3_), custom_call_target="tpu_custom_call" | custom-call | tf_op jit(solution)/shard_map/near/pallas_call | solution.py:427
  33.6 4.9 %collective-permute-done.5.low2 = bf16[512,512]{1,0:T(8,128)(2,1)S(1)} collective-permute-done((bf16[512,512]{1,0:T(8,128)(2,1)S(1)}, bf16[512,512]{1,0:T(8,128)(2,1)S(1)}, u32[]{:S(2)}, u32[]{:S(2)}) %collective-permute-start.5) | collective-permute-done | bytes 524320 | tf_op jit(solution)/shard_map/ppermute | solution.py:55
  38.6 0.9 pick_late.2
  39.5 2.3 %collective-permute-start.9 = (f32[8,512]{1,0:T(8,128)S(1)}, f32[8,512]{1,0:T(8,128)S(1)}, u32[]{:S(2)}, u32[]{:S(2)}) collective-permute-start(f32[8,512]{1,0:T(8,128)S(1)} %get-tuple-element.75), channel_id=1, source_target_pairs={{64,0},{17,1},{66,2},{19,3},{68,4},{21,5},{70,6},{23,7},{72,8},{25... | collective-permute-start | bytes 49160 | tf_op jit(solution)/shard_map/ppermute | solution.py:55
  41.8 1.9 %collective-permute-start.8 = (f32[8,512]{1,0:T(8,128)S(1)}, f32[8,512]{1,0:T(8,128)S(1)}, u32[]{:S(2)}, u32[]{:S(2)}) collective-permute-start(f32[8,512]{1,0:T(8,128)S(1)} %get-tuple-element.75), channel_id=1, source_target_pairs={{96,0},{25,1},{98,2},{27,3},{100,4},{29,5},{102,6},{31,7},{104,8},... | collective-permute-start | bytes 49160 | tf_op jit(solution)/shard_map/ppermute | solution.py:55
  43.7 1.3 collective-permute-start.7
  45.1 3.3 %collective-permute-done.9 = f32[8,512]{1,0:T(8,128)S(1)} collective-permute-done((f32[8,512]{1,0:T(8,128)S(1)}, f32[8,512]{1,0:T(8,128)S(1)}, u32[]{:S(2)}, u32[]{:S(2)}) %collective-permute-start.9) | collective-permute-done | bytes 16416 | tf_op jit(solution)/shard_map/ppermute | solution.py:55
  48.4 0.7 collective-permute-start.12
  49.1 1.7 %collective-permute-start.16 = (bf16[512,512]{1,0:T(8,128)(2,1)S(1)}, bf16[512,512]{1,0:T(8,128)(2,1)S(1)}, u32[]{:S(2)}, u32[]{:S(2)}) collective-permute-start(bf16[512,512]{1,0:T(8,128)(2,1)S(1)} %get-tuple-element.92), channel_id=1, source_target_pairs={{32,0},{9,1},{34,2},{11,3},{36,4},{13,5},{38,6},{15,7},{40,8},{17,... | collective-permute-start | bytes 1572872 | tf_op jit(solution)/shard_map/ppermute | solution.py:55
  51.1 2.9 %collective-permute-start.18 = (bf16[512,512]{1,0:T(8,128)(2,1)S(1)}, bf16[512,512]{1,0:T(8,128)(2,1)S(1)}, u32[]{:S(2)}, u32[]{:S(2)}) collective-permute-start(bf16[512,512]{1,0:T(8,128)(2,1)S(1)} %get-tuple-element.97), channel_id=1, source_target_pairs={{64,0},{17,1},{66,2},{19,3},{68,4},{21,5},{70,6},{23,7},{72,8},{25... | collective-permute-start | bytes 1572872 | tf_op jit(solution)/shard_map/ppermute | solution.py:55
  54.0 3.5 %sides_1.2.refs_4_ = f32[1024,512]{1,0:T(8,128)S(1)} custom-call(s32[632]{0:T(1024)S(1)} %sort_tiles.1.refs_0_, s32[193,5,128]{2,1,0:T(8,128)S(1)} %concatenate.3.refs_1_, bf16[1040,512]{1,0:T(8,128)(2,1)S(1)} %first.1.refs_2_.own, bf16[1536,512]{1,0:T(8,128)(2,1)S(1)} %collective-permute-done.10.refs_3_, bf16[512,512]{1,0:T(8,128)(2,1)S(1)} %get-tuple-element.83.refs_4_, ...), custom_call_target="tpu_custom_call" | custom-call | tf_op jit(solution)/shard_map/sides_1/pallas_call | solution.py:427
  57.6 0.8 collective-permute-start.14
  58.4 3.5 %sides_3.2.refs_4_ = f32[1024,512]{1,0:T(8,128)S(1)} custom-call(s32[632]{0:T(1024)S(1)} %sort_tiles.1.refs_0_, s32[193,5,128]{2,1,0:T(8,128)S(1)} %concatenate.3.refs_1_, bf16[1040,512]{1,0:T(8,128)(2,1)S(1)} %first.1.refs_2_.own, bf16[1536,512]{1,0:T(8,128)(2,1)S(1)} %collective-permute-done.11.refs_3_, f32[1024,512]{1,0:T(8,128)S(1)} %sides_1.2.refs_4_), custom_call_target="tpu_custom_call" | custom-call | tf_op jit(solution)/shard_map/sides_3/pallas_call | solution.py:427
  62.0 3.4 %collective-permute-start.15 = (f32[8,512]{1,0:T(8,128)S(1)}, f32[8,512]{1,0:T(8,128)S(1)}, u32[]{:S(2)}, u32[]{:S(2)}) collective-permute-start(f32[8,512]{1,0:T(8,128)S(1)} %add.42), channel_id=1, source_target_pairs={{0,4},{2,6},{4,0},{6,2},{1,5},{3,7},{5,1},{7,3},{8,12},{10,14},{12... | collective-permute-start | bytes 49160 | tf_op jit(solution)/shard_map/ppermute | solution.py:59
  65.3 5.1 %collective-permute-done.12.refs_3_ = bf16[1536,512]{1,0:T(8,128)(2,1)S(1)} collective-permute-done((bf16[1536,512]{1,0:T(8,128)(2,1)S(1)}, bf16[1536,512]{1,0:T(8,128)(2,1)S(1)}, u32[]{:S(2)}, u32[]{:S(2)}) %collective-permute-start.12) | collective-permute-done | bytes 1572896 | tf_op jit(solution)/shard_map/ppermute | solution.py:55
  70.5 3.5 %across.2.refs_5_ = f32[1024,512]{1,0:T(8,128)S(1)} custom-call(s32[632]{0:T(1024)S(1)} %sort_tiles.1.refs_0_, s32[193,5,128]{2,1,0:T(8,128)S(1)} %concatenate.3.refs_1_, bf16[1040,512]{1,0:T(8,128)(2,1)S(1)} %first.1.refs_2_.own, bf16[1536,512]{1,0:T(8,128)(2,1)S(1)} %collective-permute-done.12.refs_3_, f32[1024,512]{1,0:T(8,128)S(1)} %sides_3.2.refs_4_), custom_call_target="tpu_custom_call" | custom-call | tf_op jit(solution)/shard_map/across/pallas_call | solution.py:427
  74.0 0.9 collective-permute-done.16.refs_3_
  74.9 1.0 collective-permute-done.17.refs_4_
  76.0 3.1 %late.2.refs_4_ = f32[1024,512]{1,0:T(8,128)S(1)} custom-call(s32[632]{0:T(1024)S(1)} %sort_tiles.1.refs_0_, s32[193,5,128]{2,1,0:T(8,128)S(1)} %concatenate.3.refs_1_, bf16[1040,512]{1,0:T(8,128)(2,1)S(1)} %first.1.refs_2_.own, bf16[512,512]{1,0:T(8,128)(2,1)S(1)} %collective-permute-done.16.refs_3_, bf16[512,512]{1,0:T(8,128)(2,1)S(1)} %collective-permute-done.17.refs_4_, ...), custom_call_target="tpu_custom_call" | custom-call | tf_op jit(solution)/shard_map/late/pallas_call | solution.py:427
  79.1 2.6 %collective-permute-done.18.refs_3_ = bf16[512,512]{1,0:T(8,128)(2,1)S(1)} collective-permute-done((bf16[512,512]{1,0:T(8,128)(2,1)S(1)}, bf16[512,512]{1,0:T(8,128)(2,1)S(1)}, u32[]{:S(2)}, u32[]{:S(2)}) %collective-permute-start.18) | collective-permute-done | bytes 524320 | tf_op jit(solution)/shard_map/ppermute | solution.py:55
  81.6 2.6 %last.2 = (f32[1024,512]{1,0:T(8,128)S(1)}, bf16[1040,512]{1,0:T(8,128)(2,1)S(1)}) custom-call(s32[632]{0:T(1024)S(1)} %sort_tiles.1.refs_0_, s32[193,5,128]{2,1,0:T(8,128)S(1)} %concatenate.3.refs_1_, bf16[1040,512]{1,0:T(8,128)(2,1)S(1)} %first.1.refs_2_.own, bf16[512,512]{1,0:T(8,128)(2,1)S(1)} %collective-permute-done.18.refs_3_, ...), custom_call_target="tpu_custom_call" | custom-call | tf_op jit(solution)/shard_map/last/pallas_call | solution.py:427
  84.5 3.0 %collective-permute-start.19 = (bf16[1040,512]{1,0:T(8,128)(2,1)S(1)}, bf16[1040,512]{1,0:T(8,128)(2,1)S(1)}, u32[]{:S(2)}, u32[]{:S(2)}) collective-permute-start(bf16[1040,512]{1,0:T(8,128)(2,1)S(1)} %get-tuple-element.101.refs_2_.own), channel_id=1, source_target_pairs={{8,0},{33,1},{10,2},{35,3},{12,4},{37,5},{14,6},{39,7},{16,8},{41,... | collective-permute-start | bytes 3194888 | tf_op jit(solution)/shard_map/ppermute | solution.py:55
  87.5 12.9 %collective-permute-done.20.far3 = bf16[1040,512]{1,0:T(8,128)(2,1)S(1)} collective-permute-done((bf16[1040,512]{1,0:T(8,128)(2,1)S(1)}, bf16[1040,512]{1,0:T(8,128)(2,1)S(1)}, u32[]{:S(2)}, u32[]{:S(2)}) %collective-permute-start.20) | collective-permute-done | bytes 1064992 | tf_op jit(solution)/shard_map/ppermute | solution.py:55
  100.7 0.8 pick_early.3
  101.5 1.4 collective-permute-start.26
  102.9 0.7 collective-permute-start.27
  103.6 1.7 %collective-permute-start.22 = (bf16[528,512]{1,0:T(8,128)(2,1)S(1)}, bf16[528,512]{1,0:T(8,128)(2,1)S(1)}, u32[]{:S(2)}, u32[]{:S(2)}) collective-permute-start(bf16[528,512]{1,0:T(8,128)(2,1)S(1)} %get-tuple-element.103), channel_id=1, source_target_pairs={{24,0},{97,1},{26,2},{99,3},{28,4},{101,5},{30,6},{103,7},{0,8},{1... | collective-permute-start | bytes 1622024 | tf_op jit(solution)/shard_map/ppermute | solution.py:55
  105.3 2.0 %collective-permute-start.21 = (bf16[512,512]{1,0:T(8,128)(2,1)S(1)}, bf16[512,512]{1,0:T(8,128)(2,1)S(1)}, u32[]{:S(2)}, u32[]{:S(2)}) collective-permute-start(bf16[512,512]{1,0:T(8,128)(2,1)S(1)} %get-tuple-element.102), channel_id=1, source_target_pairs={{8,0},{33,1},{10,2},{35,3},{12,4},{37,5},{14,6},{39,7},{16,8},{41,... | collective-permute-start | bytes 1572872 | tf_op jit(solution)/shard_map/ppermute | solution.py:55
  107.3 0.6 pick_near.3.refs_3_
  107.9 3.4 %near.3.refs_5_ = f32[1024,512]{1,0:T(8,128)S(1)} custom-call(s32[632]{0:T(1024)S(1)} %sort_tiles.1.refs_0_, s32[193,5,128]{2,1,0:T(8,128)S(1)} %concatenate.3.refs_1_, bf16[1040,512]{1,0:T(8,128)(2,1)S(1)} %get-tuple-element.101.refs_2_.own, bf16[1024,512]{1,0:T(8,128)(2,1)S(1)} %pick_near.3.refs_3_), custom_call_target="tpu_custom_call" | custom-call | tf_op jit(solution)/shard_map/near/pallas_call | solution.py:427
  111.3 9.9 %collective-permute-done.21.low2 = bf16[512,512]{1,0:T(8,128)(2,1)S(1)} collective-permute-done((bf16[512,512]{1,0:T(8,128)(2,1)S(1)}, bf16[512,512]{1,0:T(8,128)(2,1)S(1)}, u32[]{:S(2)}, u32[]{:S(2)}) %collective-permute-start.21) | collective-permute-done | bytes 524320 | tf_op jit(solution)/shard_map/ppermute | solution.py:55
  121.2 0.9 pick_late.3
  122.1 0.5 collective-permute-start.25
  122.6 2.5 %collective-permute-start.24 = (f32[8,512]{1,0:T(8,128)S(1)}, f32[8,512]{1,0:T(8,128)S(1)}, u32[]{:S(2)}, u32[]{:S(2)}) collective-permute-start(f32[8,512]{1,0:T(8,128)S(1)} %get-tuple-element.106), channel_id=1, source_target_pairs={{96,0},{25,1},{98,2},{27,3},{100,4},{29,5},{102,6},{31,7},{104,8},... | collective-permute-start | bytes 49160 | tf_op jit(solution)/shard_map/ppermute | solution.py:55
  125.1 0.7 collective-permute-start.23
  125.8 2.4 %collective-permute-done.25 = f32[8,512]{1,0:T(8,128)S(1)} collective-permute-done((f32[8,512]{1,0:T(8,128)S(1)}, f32[8,512]{1,0:T(8,128)S(1)}, u32[]{:S(2)}, u32[]{:S(2)}) %collective-permute-start.25) | collective-permute-done | bytes 16416 | tf_op jit(solution)/shard_map/ppermute | solution.py:55
  128.2 0.6 collective-permute-done.23
  128.9 1.2 collective-permute-start.28
  130.1 2.0 %collective-permute-start.32 = (bf16[512,512]{1,0:T(8,128)(2,1)S(1)}, bf16[512,512]{1,0:T(8,128)(2,1)S(1)}, u32[]{:S(2)}, u32[]{:S(2)}) collective-permute-start(bf16[512,512]{1,0:T(8,128)(2,1)S(1)} %get-tuple-element.123), channel_id=1, source_target_pairs={{32,0},{9,1},{34,2},{11,3},{36,4},{13,5},{38,6},{15,7},{40,8},{17,... | collective-permute-start | bytes 1572872 | tf_op jit(solution)/shard_map/ppermute | solution.py:55
  132.1 2.3 %collective-permute-start.34 = (bf16[512,512]{1,0:T(8,128)(2,1)S(1)}, bf16[512,512]{1,0:T(8,128)(2,1)S(1)}, u32[]{:S(2)}, u32[]{:S(2)}) collective-permute-start(bf16[512,512]{1,0:T(8,128)(2,1)S(1)} %get-tuple-element.128), channel_id=1, source_target_pairs={{64,0},{17,1},{66,2},{19,3},{68,4},{21,5},{70,6},{23,7},{72,8},{25... | collective-permute-start | bytes 1572872 | tf_op jit(solution)/shard_map/ppermute | solution.py:55
  134.4 3.5 %sides_1.3.refs_4_ = f32[1024,512]{1,0:T(8,128)S(1)} custom-call(s32[632]{0:T(1024)S(1)} %sort_tiles.1.refs_0_, s32[193,5,128]{2,1,0:T(8,128)S(1)} %concatenate.3.refs_1_, bf16[1040,512]{1,0:T(8,128)(2,1)S(1)} %get-tuple-element.101.refs_2_.own, bf16[1536,512]{1,0:T(8,128)(2,1)S(1)} %collective-permute-done.26.refs_3_, ...), custom_call_target="tpu_custom_call" | custom-call | tf_op jit(solution)/shard_map/sides_1/pallas_call | solution.py:427
  138.0 0.6 collective-permute-start.30
  138.6 3.5 %sides_3.3.refs_4_ = f32[1024,512]{1,0:T(8,128)S(1)} custom-call(s32[632]{0:T(1024)S(1)} %sort_tiles.1.refs_0_, s32[193,5,128]{2,1,0:T(8,128)S(1)} %concatenate.3.refs_1_, bf16[1040,512]{1,0:T(8,128)(2,1)S(1)} %get-tuple-element.101.refs_2_.own, bf16[1536,512]{1,0:T(8,128)(2,1)S(1)} %collective-permute-done.27.refs_3_, f32[1024,512]{1,0:T(8,128)S(1)} %sides_1.3.refs_4_), custom_call_target="tpu_custom_call" | custom-call | tf_op jit(solution)/shard_map/sides_3/pallas_call | solution.py:427
  142.1 3.5 %collective-permute-start.31 = (f32[8,512]{1,0:T(8,128)S(1)}, f32[8,512]{1,0:T(8,128)S(1)}, u32[]{:S(2)}, u32[]{:S(2)}) collective-permute-start(f32[8,512]{1,0:T(8,128)S(1)} %add.48), channel_id=1, source_target_pairs={{0,4},{2,6},{4,0},{6,2},{1,5},{3,7},{5,1},{7,3},{8,12},{10,14},{12... | collective-permute-start | bytes 49160 | tf_op jit(solution)/shard_map/ppermute | solution.py:59
  145.6 5.3 %collective-permute-done.28.refs_3_ = bf16[1536,512]{1,0:T(8,128)(2,1)S(1)} collective-permute-done((bf16[1536,512]{1,0:T(8,128)(2,1)S(1)}, bf16[1536,512]{1,0:T(8,128)(2,1)S(1)}, u32[]{:S(2)}, u32[]{:S(2)}) %collective-permute-start.28) | collective-permute-done | bytes 1572896 | tf_op jit(solution)/shard_map/ppermute | solution.py:55
  150.9 3.4 %across.3.refs_5_ = f32[1024,512]{1,0:T(8,128)S(1)} custom-call(s32[632]{0:T(1024)S(1)} %sort_tiles.1.refs_0_, s32[193,5,128]{2,1,0:T(8,128)S(1)} %concatenate.3.refs_1_, bf16[1040,512]{1,0:T(8,128)(2,1)S(1)} %get-tuple-element.101.refs_2_.own, bf16[1536,512]{1,0:T(8,128)(2,1)S(1)} %collective-permute-done.28.refs_3_, f32[1024,512]{1,0:T(8,128)S(1)} %sides_3.3.refs_4_), custom_call_target="tpu_custom_call" | custom-call | tf_op jit(solution)/shard_map/across/pallas_call | solution.py:427
  154.3 1.4 collective-permute-done.32.refs_3_
  155.7 0.7 collective-permute-done.33.refs_4_
  156.4 2.9 %late.3.refs_4_ = f32[1024,512]{1,0:T(8,128)S(1)} custom-call(s32[632]{0:T(1024)S(1)} %sort_tiles.1.refs_0_, s32[193,5,128]{2,1,0:T(8,128)S(1)} %concatenate.3.refs_1_, bf16[1040,512]{1,0:T(8,128)(2,1)S(1)} %get-tuple-element.101.refs_2_.own, bf16[512,512]{1,0:T(8,128)(2,1)S(1)} %collective-permute-done.32.refs_3_, ...), custom_call_target="tpu_custom_call" | custom-call | tf_op jit(solution)/shard_map/late/pallas_call | solution.py:427
  159.3 2.8 %collective-permute-done.34.refs_3_ = bf16[512,512]{1,0:T(8,128)(2,1)S(1)} collective-permute-done((bf16[512,512]{1,0:T(8,128)(2,1)S(1)}, bf16[512,512]{1,0:T(8,128)(2,1)S(1)}, u32[]{:S(2)}, u32[]{:S(2)}) %collective-permute-start.34) | collective-permute-done | bytes 524320 | tf_op jit(solution)/shard_map/ppermute | solution.py:55
  162.1 3.5 %last.3 = f32[1024,512]{1,0:T(8,128)} custom-call(s32[632]{0:T(1024)S(1)} %sort_tiles.1.refs_0_, s32[193,5,128]{2,1,0:T(8,128)S(1)} %concatenate.3.refs_1_, bf16[1040,512]{1,0:T(8,128)(2,1)S(1)} %get-tuple-element.101.refs_2_.own, bf16[512,512]{1,0:T(8,128)(2,1)S(1)} %collective-permute-done.34.refs_3_, f32[1024,512]{1,0:T(8,128)S(1)} %late.3.refs_4_, ...), custom_call_target="tpu_custom_call" | custom-call | tf_op jit(solution)/shard_map/last/pallas_call | solution.py:427
  (54 shorter events, 2.5 us)
Async XLA Ops:
  0.0 1.6 copy-start
  1.6 4.2 %copy-start.2 = (s32[1024]{0:T(1024)S(1)}, s32[1024]{0:T(1024)}, u32[]{:S(2)}) copy-start(s32[1024]{0:T(1024)} %home.1) | copy-start | bytes 12292
  1.6 4.2 %copy-start.3 = (s32[1,240]{1,0:T(1,128)S(1)}, s32[1,240]{1,0:T(1,128)}, u32[]{:S(2)}) copy-start(s32[1,240]{1,0:T(1,128)} %param.8) | copy-start | bytes 2884
  1.6 4.2 %copy-start.4 = (s32[1,240]{1,0:T(1,128)S(1)}, s32[1,240]{1,0:T(1,128)}, u32[]{:S(2)}) copy-start(s32[1,240]{1,0:T(1,128)} %param.9) | copy-start | bytes 2884
  1.7 16.3 %collective-permute-start.4 = (bf16[1040,512]{1,0:T(8,128)(2,1)S(1)}, bf16[1040,512]{1,0:T(8,128)(2,1)S(1)}, u32[]{:S(2)}, u32[]{:S(2)}) collective-permute-start(bf16[1040,512]{1,0:T(8,128)(2,1)S(1)} %first.1.refs_2_.own), channel_id=1, source_target_pairs={{24,0},{97,1},{26,2},{99,3},{28,4},{101,5},{30,6},{103,7},{0,8},{1... | collective-permute-start | bytes 3194888 | tf_op jit(solution)/shard_map/ppermute | solution.py:55
  3.3 15.0 %collective-permute-start.3 = (bf16[1040,512]{1,0:T(8,128)(2,1)S(1)}, bf16[1040,512]{1,0:T(8,128)(2,1)S(1)}, u32[]{:S(2)}, u32[]{:S(2)}) collective-permute-start(bf16[1040,512]{1,0:T(8,128)(2,1)S(1)} %first.1.refs_2_.own), channel_id=1, source_target_pairs={{8,0},{33,1},{10,2},{35,3},{12,4},{37,5},{14,6},{39,7},{16,8},{41,... | collective-permute-start | bytes 3194888 | tf_op jit(solution)/shard_map/ppermute | solution.py:55
  9.3 4.7 %collective-permute-start.2 = (s32[16]{0:T(128)S(1)}, s32[16]{0:T(128)S(1)}, u32[]{:S(2)}, u32[]{:S(2)}) collective-permute-start(s32[16]{0:T(128)S(1)} %get-tuple-element.134), channel_id=1, source_target_pairs={{32,0},{9,1},{34,2},{11,3},{36,4},{13,5},{38,6},{15,7},{40,8},{17,... | collective-permute-start | bytes 200 | tf_op jit(solution)/shard_map/ppermute | solution.py:55
  12.7 5.1 %collective-permute-start.1 = (s32[16]{0:T(128)S(1)}, s32[16]{0:T(128)S(1)}, u32[]{:S(2)}, u32[]{:S(2)}) collective-permute-start(s32[16]{0:T(128)S(1)} %get-tuple-element.135), channel_id=1, source_target_pairs={{64,0},{17,1},{66,2},{19,3},{68,4},{21,5},{70,6},{23,7},{72,8},{25... | collective-permute-start | bytes 200 | tf_op jit(solution)/shard_map/ppermute | solution.py:55
  13.0 4.8 %collective-permute-start = (s32[16]{0:T(128)S(1)}, s32[16]{0:T(128)S(1)}, u32[]{:S(2)}, u32[]{:S(2)}) collective-permute-start(s32[16]{0:T(128)S(1)} %get-tuple-element.136), channel_id=1, source_target_pairs={{96,0},{25,1},{98,2},{27,3},{100,4},{29,5},{102,6},{31,7},{104,8},... | collective-permute-start | bytes 200 | tf_op jit(solution)/shard_map/ppermute | solution.py:55
  17.8 7.7 %copy-start.6 = (s32[192,5,128]{2,0,1:T(8,128)S(1)}, s32[192,5,128]{2,0,1:T(8,128)}, u32[]{:S(2)}) copy-start(s32[192,5,128]{2,0,1:T(8,128)} %param.13) | copy-start | bytes 1474564
  19.1 6.7 %copy-start.5 = (s32[1,240]{1,0:T(1,128)S(1)}, s32[1,240]{1,0:T(1,128)}, u32[]{:S(2)}) copy-start(s32[1,240]{1,0:T(1,128)} %param.10) | copy-start | bytes 2884
  19.1 29.2 %collective-permute-start.10 = (bf16[1536,512]{1,0:T(8,128)(2,1)S(1)}, bf16[1536,512]{1,0:T(8,128)(2,1)S(1)}, u32[]{:S(2)}, u32[]{:S(2)}) collective-permute-start(bf16[1536,512]{1,0:T(8,128)(2,1)S(1)} %get-tuple-element.78), channel_id=1, source_target_pairs={{32,0},{9,1},{34,2},{11,3},{36,4},{13,5},{38,6},{15,7},{40,8},{17,... | collective-permute-start | bytes 4718600 | tf_op jit(solution)/shard_map/ppermute | solution.py:55
  22.2 26.1 %collective-permute-start.11 = (bf16[1536,512]{1,0:T(8,128)(2,1)S(1)}, bf16[1536,512]{1,0:T(8,128)(2,1)S(1)}, u32[]{:S(2)}, u32[]{:S(2)}) collective-permute-start(bf16[1536,512]{1,0:T(8,128)(2,1)S(1)} %get-tuple-element.79), channel_id=1, source_target_pairs={{96,0},{25,1},{98,2},{27,3},{100,4},{29,5},{102,6},{31,7},{104,8},... | collective-permute-start | bytes 4718600 | tf_op jit(solution)/shard_map/ppermute | solution.py:55
  22.2 16.4 %collective-permute-start.6 = (bf16[528,512]{1,0:T(8,128)(2,1)S(1)}, bf16[528,512]{1,0:T(8,128)(2,1)S(1)}, u32[]{:S(2)}, u32[]{:S(2)}) collective-permute-start(bf16[528,512]{1,0:T(8,128)(2,1)S(1)} %get-tuple-element.72), channel_id=1, source_target_pairs={{24,0},{97,1},{26,2},{99,3},{28,4},{101,5},{30,6},{103,7},{0,8},{1... | collective-permute-start | bytes 1622024 | tf_op jit(solution)/shard_map/ppermute | solution.py:55
  23.7 14.9 %collective-permute-start.5 = (bf16[512,512]{1,0:T(8,128)(2,1)S(1)}, bf16[512,512]{1,0:T(8,128)(2,1)S(1)}, u32[]{:S(2)}, u32[]{:S(2)}) collective-permute-start(bf16[512,512]{1,0:T(8,128)(2,1)S(1)} %get-tuple-element.71), channel_id=1, source_target_pairs={{8,0},{33,1},{10,2},{35,3},{12,4},{37,5},{14,6},{39,7},{16,8},{41,... | collective-permute-start | bytes 1572872 | tf_op jit(solution)/shard_map/ppermute | solution.py:55
  39.5 8.8 %collective-permute-start.9 = (f32[8,512]{1,0:T(8,128)S(1)}, f32[8,512]{1,0:T(8,128)S(1)}, u32[]{:S(2)}, u32[]{:S(2)}) collective-permute-start(f32[8,512]{1,0:T(8,128)S(1)} %get-tuple-element.75), channel_id=1, source_target_pairs={{64,0},{17,1},{66,2},{19,3},{68,4},{21,5},{70,6},{23,7},{72,8},{25... | collective-permute-start | bytes 49160 | tf_op jit(solution)/shard_map/ppermute | solution.py:55
  41.8 6.5 %collective-permute-start.8 = (f32[8,512]{1,0:T(8,128)S(1)}, f32[8,512]{1,0:T(8,128)S(1)}, u32[]{:S(2)}, u32[]{:S(2)}) collective-permute-start(f32[8,512]{1,0:T(8,128)S(1)} %get-tuple-element.75), channel_id=1, source_target_pairs={{96,0},{25,1},{98,2},{27,3},{100,4},{29,5},{102,6},{31,7},{104,8},... | collective-permute-start | bytes 49160 | tf_op jit(solution)/shard_map/ppermute | solution.py:55
  43.7 4.6 %collective-permute-start.7 = (f32[8,512]{1,0:T(8,128)S(1)}, f32[8,512]{1,0:T(8,128)S(1)}, u32[]{:S(2)}, u32[]{:S(2)}) collective-permute-start(f32[8,512]{1,0:T(8,128)S(1)} %get-tuple-element.75), channel_id=1, source_target_pairs={{32,0},{9,1},{34,2},{11,3},{36,4},{13,5},{38,6},{15,7},{40,8},{17,... | collective-permute-start | bytes 49160 | tf_op jit(solution)/shard_map/ppermute | solution.py:55
  48.4 22.1 %collective-permute-start.12 = (bf16[1536,512]{1,0:T(8,128)(2,1)S(1)}, bf16[1536,512]{1,0:T(8,128)(2,1)S(1)}, u32[]{:S(2)}, u32[]{:S(2)}) collective-permute-start(bf16[1536,512]{1,0:T(8,128)(2,1)S(1)} %get-tuple-element.80), channel_id=1, source_target_pairs={{64,0},{17,1},{66,2},{19,3},{68,4},{21,5},{70,6},{23,7},{72,8},{25... | collective-permute-start | bytes 4718600 | tf_op jit(solution)/shard_map/ppermute | solution.py:55
  49.1 25.9 %collective-permute-start.16 = (bf16[512,512]{1,0:T(8,128)(2,1)S(1)}, bf16[512,512]{1,0:T(8,128)(2,1)S(1)}, u32[]{:S(2)}, u32[]{:S(2)}) collective-permute-start(bf16[512,512]{1,0:T(8,128)(2,1)S(1)} %get-tuple-element.92), channel_id=1, source_target_pairs={{32,0},{9,1},{34,2},{11,3},{36,4},{13,5},{38,6},{15,7},{40,8},{17,... | collective-permute-start | bytes 1572872 | tf_op jit(solution)/shard_map/ppermute | solution.py:55
  50.8 25.2 %collective-permute-start.17 = (bf16[512,512]{1,0:T(8,128)(2,1)S(1)}, bf16[512,512]{1,0:T(8,128)(2,1)S(1)}, u32[]{:S(2)}, u32[]{:S(2)}) collective-permute-start(bf16[512,512]{1,0:T(8,128)(2,1)S(1)} %get-tuple-element.93), channel_id=1, source_target_pairs={{96,0},{25,1},{98,2},{27,3},{100,4},{29,5},{102,6},{31,7},{104,8},... | collective-permute-start | bytes 1572872 | tf_op jit(solution)/shard_map/ppermute | solution.py:55
  51.1 30.5 %collective-permute-start.18 = (bf16[512,512]{1,0:T(8,128)(2,1)S(1)}, bf16[512,512]{1,0:T(8,128)(2,1)S(1)}, u32[]{:S(2)}, u32[]{:S(2)}) collective-permute-start(bf16[512,512]{1,0:T(8,128)(2,1)S(1)} %get-tuple-element.97), channel_id=1, source_target_pairs={{64,0},{17,1},{66,2},{19,3},{68,4},{21,5},{70,6},{23,7},{72,8},{25... | collective-permute-start | bytes 1572872 | tf_op jit(solution)/shard_map/ppermute | solution.py:55
  54.0 3.6 %collective-permute-start.13 = (f32[8,512]{1,0:T(8,128)S(1)}, f32[8,512]{1,0:T(8,128)S(1)}, u32[]{:S(2)}, u32[]{:S(2)}) collective-permute-start(f32[8,512]{1,0:T(8,128)S(1)} %add_add_fusion.1), channel_id=1, source_target_pairs={{0,1},{1,0},{2,3},{3,2},{4,5},{5,4},{6,7},{7,6},{8,9},{9,8},{10,11... | collective-permute-start | bytes 49160 | tf_op jit(solution)/shard_map/ppermute | solution.py:59
  57.6 4.3 %collective-permute-start.14 = (f32[8,512]{1,0:T(8,128)S(1)}, f32[8,512]{1,0:T(8,128)S(1)}, u32[]{:S(2)}, u32[]{:S(2)}) collective-permute-start(f32[8,512]{1,0:T(8,128)S(1)} %add.41), channel_id=1, source_target_pairs={{0,2},{2,0},{4,6},{6,4},{1,3},{3,1},{5,7},{7,5},{8,10},{10,8},{12,... | collective-permute-start | bytes 49160 | tf_op jit(solution)/shard_map/ppermute | solution.py:59
  62.0 14.0 %collective-permute-start.15 = (f32[8,512]{1,0:T(8,128)S(1)}, f32[8,512]{1,0:T(8,128)S(1)}, u32[]{:S(2)}, u32[]{:S(2)}) collective-permute-start(f32[8,512]{1,0:T(8,128)S(1)} %add.42), channel_id=1, source_target_pairs={{0,4},{2,6},{4,0},{6,2},{1,5},{3,7},{5,1},{7,3},{8,12},{10,14},{12... | collective-permute-start | bytes 49160 | tf_op jit(solution)/shard_map/ppermute | solution.py:59
  76.0 5.7 %copy-start.1 = (f32[1024,512]{1,0:T(8,128)S(1)}, f32[1024,512]{1,0:T(8,128)}, u32[]{:S(2)}) copy-start(f32[1024,512]{1,0:T(8,128)} %refs_5_.1) | copy-start | bytes 6291460
  84.2 16.3 %collective-permute-start.20 = (bf16[1040,512]{1,0:T(8,128)(2,1)S(1)}, bf16[1040,512]{1,0:T(8,128)(2,1)S(1)}, u32[]{:S(2)}, u32[]{:S(2)}) collective-permute-start(bf16[1040,512]{1,0:T(8,128)(2,1)S(1)} %get-tuple-element.101.refs_2_.own), channel_id=1, source_target_pairs={{24,0},{97,1},{26,2},{99,3},{28,4},{101,5},{30,6},{103,7},{0,8},{1... | collective-permute-start | bytes 3194888 | tf_op jit(solution)/shard_map/ppermute | solution.py:55
  84.5 16.2 %collective-permute-start.19 = (bf16[1040,512]{1,0:T(8,128)(2,1)S(1)}, bf16[1040,512]{1,0:T(8,128)(2,1)S(1)}, u32[]{:S(2)}, u32[]{:S(2)}) collective-permute-start(bf16[1040,512]{1,0:T(8,128)(2,1)S(1)} %get-tuple-element.101.refs_2_.own), channel_id=1, source_target_pairs={{8,0},{33,1},{10,2},{35,3},{12,4},{37,5},{14,6},{39,7},{16,8},{41,... | collective-permute-start | bytes 3194888 | tf_op jit(solution)/shard_map/ppermute | solution.py:55
  101.5 27.4 %collective-permute-start.26 = (bf16[1536,512]{1,0:T(8,128)(2,1)S(1)}, bf16[1536,512]{1,0:T(8,128)(2,1)S(1)}, u32[]{:S(2)}, u32[]{:S(2)}) collective-permute-start(bf16[1536,512]{1,0:T(8,128)(2,1)S(1)} %get-tuple-element.109), channel_id=1, source_target_pairs={{32,0},{9,1},{34,2},{11,3},{36,4},{13,5},{38,6},{15,7},{40,8},{17,... | collective-permute-start | bytes 4718600 | tf_op jit(solution)/shard_map/ppermute | solution.py:55
  102.9 26.0 %collective-permute-start.27 = (bf16[1536,512]{1,0:T(8,128)(2,1)S(1)}, bf16[1536,512]{1,0:T(8,128)(2,1)S(1)}, u32[]{:S(2)}, u32[]{:S(2)}) collective-permute-start(bf16[1536,512]{1,0:T(8,128)(2,1)S(1)} %get-tuple-element.110), channel_id=1, source_target_pairs={{96,0},{25,1},{98,2},{27,3},{100,4},{29,5},{102,6},{31,7},{104,8},... | collective-permute-start | bytes 4718600 | tf_op jit(solution)/shard_map/ppermute | solution.py:55
  103.6 17.6 %collective-permute-start.22 = (bf16[528,512]{1,0:T(8,128)(2,1)S(1)}, bf16[528,512]{1,0:T(8,128)(2,1)S(1)}, u32[]{:S(2)}, u32[]{:S(2)}) collective-permute-start(bf16[528,512]{1,0:T(8,128)(2,1)S(1)} %get-tuple-element.103), channel_id=1, source_target_pairs={{24,0},{97,1},{26,2},{99,3},{28,4},{101,5},{30,6},{103,7},{0,8},{1... | collective-permute-start | bytes 1622024 | tf_op jit(solution)/shard_map/ppermute | solution.py:55
  105.3 15.9 %collective-permute-start.21 = (bf16[512,512]{1,0:T(8,128)(2,1)S(1)}, bf16[512,512]{1,0:T(8,128)(2,1)S(1)}, u32[]{:S(2)}, u32[]{:S(2)}) collective-permute-start(bf16[512,512]{1,0:T(8,128)(2,1)S(1)} %get-tuple-element.102), channel_id=1, source_target_pairs={{8,0},{33,1},{10,2},{35,3},{12,4},{37,5},{14,6},{39,7},{16,8},{41,... | collective-permute-start | bytes 1572872 | tf_op jit(solution)/shard_map/ppermute | solution.py:55
  122.1 6.1 %collective-permute-start.25 = (f32[8,512]{1,0:T(8,128)S(1)}, f32[8,512]{1,0:T(8,128)S(1)}, u32[]{:S(2)}, u32[]{:S(2)}) collective-permute-start(f32[8,512]{1,0:T(8,128)S(1)} %get-tuple-element.106), channel_id=1, source_target_pairs={{64,0},{17,1},{66,2},{19,3},{68,4},{21,5},{70,6},{23,7},{72,8},{25... | collective-permute-start | bytes 49160 | tf_op jit(solution)/shard_map/ppermute | solution.py:55
  122.6 5.7 %collective-permute-start.24 = (f32[8,512]{1,0:T(8,128)S(1)}, f32[8,512]{1,0:T(8,128)S(1)}, u32[]{:S(2)}, u32[]{:S(2)}) collective-permute-start(f32[8,512]{1,0:T(8,128)S(1)} %get-tuple-element.106), channel_id=1, source_target_pairs={{96,0},{25,1},{98,2},{27,3},{100,4},{29,5},{102,6},{31,7},{104,8},... | collective-permute-start | bytes 49160 | tf_op jit(solution)/shard_map/ppermute | solution.py:55
  125.1 3.7 %collective-permute-start.23 = (f32[8,512]{1,0:T(8,128)S(1)}, f32[8,512]{1,0:T(8,128)S(1)}, u32[]{:S(2)}, u32[]{:S(2)}) collective-permute-start(f32[8,512]{1,0:T(8,128)S(1)} %get-tuple-element.106), channel_id=1, source_target_pairs={{32,0},{9,1},{34,2},{11,3},{36,4},{13,5},{38,6},{15,7},{40,8},{17,... | collective-permute-start | bytes 49160 | tf_op jit(solution)/shard_map/ppermute | solution.py:55
  128.9 22.0 %collective-permute-start.28 = (bf16[1536,512]{1,0:T(8,128)(2,1)S(1)}, bf16[1536,512]{1,0:T(8,128)(2,1)S(1)}, u32[]{:S(2)}, u32[]{:S(2)}) collective-permute-start(bf16[1536,512]{1,0:T(8,128)(2,1)S(1)} %get-tuple-element.111), channel_id=1, source_target_pairs={{64,0},{17,1},{66,2},{19,3},{68,4},{21,5},{70,6},{23,7},{72,8},{25... | collective-permute-start | bytes 4718600 | tf_op jit(solution)/shard_map/ppermute | solution.py:55
  130.1 25.6 %collective-permute-start.32 = (bf16[512,512]{1,0:T(8,128)(2,1)S(1)}, bf16[512,512]{1,0:T(8,128)(2,1)S(1)}, u32[]{:S(2)}, u32[]{:S(2)}) collective-permute-start(bf16[512,512]{1,0:T(8,128)(2,1)S(1)} %get-tuple-element.123), channel_id=1, source_target_pairs={{32,0},{9,1},{34,2},{11,3},{36,4},{13,5},{38,6},{15,7},{40,8},{17,... | collective-permute-start | bytes 1572872 | tf_op jit(solution)/shard_map/ppermute | solution.py:55
  132.1 24.3 %collective-permute-start.33 = (bf16[512,512]{1,0:T(8,128)(2,1)S(1)}, bf16[512,512]{1,0:T(8,128)(2,1)S(1)}, u32[]{:S(2)}, u32[]{:S(2)}) collective-permute-start(bf16[512,512]{1,0:T(8,128)(2,1)S(1)} %get-tuple-element.124), channel_id=1, source_target_pairs={{96,0},{25,1},{98,2},{27,3},{100,4},{29,5},{102,6},{31,7},{104,8},... | collective-permute-start | bytes 1572872 | tf_op jit(solution)/shard_map/ppermute | solution.py:55
  132.1 30.0 %collective-permute-start.34 = (bf16[512,512]{1,0:T(8,128)(2,1)S(1)}, bf16[512,512]{1,0:T(8,128)(2,1)S(1)}, u32[]{:S(2)}, u32[]{:S(2)}) collective-permute-start(bf16[512,512]{1,0:T(8,128)(2,1)S(1)} %get-tuple-element.128), channel_id=1, source_target_pairs={{64,0},{17,1},{66,2},{19,3},{68,4},{21,5},{70,6},{23,7},{72,8},{25... | collective-permute-start | bytes 1572872 | tf_op jit(solution)/shard_map/ppermute | solution.py:55
  134.4 3.5 %collective-permute-start.29 = (f32[8,512]{1,0:T(8,128)S(1)}, f32[8,512]{1,0:T(8,128)S(1)}, u32[]{:S(2)}, u32[]{:S(2)}) collective-permute-start(f32[8,512]{1,0:T(8,128)S(1)} %add_add_fusion), channel_id=1, source_target_pairs={{0,1},{1,0},{2,3},{3,2},{4,5},{5,4},{6,7},{7,6},{8,9},{9,8},{10,11... | collective-permute-start | bytes 49160 | tf_op jit(solution)/shard_map/ppermute | solution.py:59
  138.0 4.1 %collective-permute-start.30 = (f32[8,512]{1,0:T(8,128)S(1)}, f32[8,512]{1,0:T(8,128)S(1)}, u32[]{:S(2)}, u32[]{:S(2)}) collective-permute-start(f32[8,512]{1,0:T(8,128)S(1)} %add.47), channel_id=1, source_target_pairs={{0,2},{2,0},{4,6},{6,4},{1,3},{3,1},{5,7},{7,5},{8,10},{10,8},{12,... | collective-permute-start | bytes 49160 | tf_op jit(solution)/shard_map/ppermute | solution.py:59
  142.1 14.3 %collective-permute-start.31 = (f32[8,512]{1,0:T(8,128)S(1)}, f32[8,512]{1,0:T(8,128)S(1)}, u32[]{:S(2)}, u32[]{:S(2)}) collective-permute-start(f32[8,512]{1,0:T(8,128)S(1)} %add.48), channel_id=1, source_target_pairs={{0,4},{2,6},{4,0},{6,2},{1,5},{3,7},{5,1},{7,3},{8,12},{10,14},{12... | collective-permute-start | bytes 49160 | tf_op jit(solution)/shard_map/ppermute | solution.py:59

commit v3 on v2

--- a/solution.py
+++ b/solution.py
@@ -20,7 +20,7 @@
 PATTERNS = 192
 TILES = 240
 PARTS = 6
-GROUP = (4, 4, 4, 4, 4, 2)
+GROUP = (4, 4, 4, 4, 2, 2)
 KEYS = PARTS * BPD
 SLOTS = TILES + sum(BPD * (g - 1) + 2 * g for g in GROUP) // 16 * 16 + 16
 STARTS = SLOTS + SLOTS // 2

time: 166 us -> 167 us (level)
  Pallas kernels: 51.9 us -> 55.5 us
  starting transfers between devices: 52.1 us -> 49.7 us
    pallas_call x12, Pallas kernels: 40 us -> 43 us  [run_tiles(): pl.pallas_call(functools.partial(tile_kernel, part, len(tables), earlier...]
    ppermute x6, starting transfers between devices: 8.24 us -> 5.71 us  [swap(): lax.ppermute(value, axis, [(i, i ^ step) for i in range(lax.axis_size(axi...]
  transfers between devices with their start and end apart: 35 -> 35, of which waited for: 19 -> 19; matrix products, arithmetic and copies ran while one was open for 0% -> 0% of each run, Pallas kernels for 27% -> 29%
where the time goes in v3:
time: 167 us; the launch traced here: 166 us
  waiting for transfers between devices  57.6 us (34%)
  Pallas kernels  55.5 us (33%)
  starting transfers between devices  49.7 us (30%)
  local copies, waits for them, and re-layouts  2.06 us (1%)
    ppermute x29, waiting for transfers between devices, fetch(): return lax.ppermute(value, ALL, pairs(first, second))  57.5 us
    ppermute x29, starting transfers between devices, fetch(): return lax.ppermute(value, ALL, pairs(first, second))  44 us
    pallas_call x12, Pallas kernels, run_tiles(): pl.pallas_call(functools.partial(tile_kernel, part, len(tables), earlier...  43 us
    ppermute x6, starting transfers between devices, swap(): lax.ppermute(value, axis, [(i, i ^ step) for i in range(lax.axis_size(axi...  5.71 us
    pallas_call x1, Pallas kernels, sort_tiles(): pl.pallas_call(sort_kernel, out_shape=jax.ShapeDtypeStruct((LIST,), i32),...  3.94 us
    pallas_call x1, Pallas kernels, ask(): pl.pallas_call(ask_kernel, out_shape=(jax.ShapeDtypeStruct((64,), i32), j...  3.79 us
  transfers between devices with their start and end apart: 35, of which 19 were waited for; matrix products, arithmetic and copies ran while one was open for 0% of the time, Pallas kernels for 29%

profile of v3, /device:TPU:32, one launch (start us, length us, event | category | flops | bytes accessed | tf_op | source)
XLA Modules:
  0.0 166.1 jit_solution(11208801967360647456)
XLA Ops:
  0.0 1.6 copy-done
  1.7 1.6 collective-permute-start.4
  3.3 1.7 %collective-permute-start.3 = (bf16[1040,512]{1,0:T(8,128)(2,1)S(1)}, bf16[1040,512]{1,0:T(8,128)(2,1)S(1)}, u32[]{:S(2)}, u32[]{:S(2)}) collective-permute-start(bf16[1040,512]{1,0:T(8,128)(2,1)S(1)} %first.1.refs_2_.own), channel_id=1, source_target_pairs={{8,0},{33,1},{10,2},{35,3},{12,4},{37,5},{14,6},{39,7},{16,8},{41,... | collective-permute-start | bytes 3194888 | tf_op jit(solution)/shard_map/ppermute | solution.py:55
  5.8 3.8 %ask.1 = (s32[64]{0:T(128)S(1)}, s32[240]{0:T(256)S(1)}) custom-call(s32[3]{0:T(128)S(1)} %pad_add_fusion.1.place, s32[240]{0:T(256)S(1)} %bitcast.9, s32[240]{0:T(256)S(1)} %bitcast.10, s32[1]{0:T(128)S(6)} %copy.9.count, s32[1024]{0:T(1024)S(1)} %copy-done.2), custom_call_target="tpu_custom_call" | custom-call | tf_op jit(solution)/shard_map/ask/pallas_call | solution.py:115
  9.7 3.4 %collective-permute-start.2 = (s32[16]{0:T(128)S(1)}, s32[16]{0:T(128)S(1)}, u32[]{:S(2)}, u32[]{:S(2)}) collective-permute-start(s32[16]{0:T(128)S(1)} %get-tuple-element.134), channel_id=1, source_target_pairs={{32,0},{9,1},{34,2},{11,3},{36,4},{13,5},{38,6},{15,7},{40,8},{17,... | collective-permute-start | bytes 200 | tf_op jit(solution)/shard_map/ppermute | solution.py:55
  13.0 1.2 collective-permute-start
  14.3 3.7 %collective-permute-done.1 = s32[16]{0:T(128)S(1)} collective-permute-done((s32[16]{0:T(128)S(1)}, s32[16]{0:T(128)S(1)}, u32[]{:S(2)}, u32[]{:S(2)}) %collective-permute-start.1) | collective-permute-done | bytes 96 | tf_op jit(solution)/shard_map/ppermute | solution.py:55
  18.3 0.8 pick_early.2
  19.1 3.1 %collective-permute-start.10 = (bf16[1536,512]{1,0:T(8,128)(2,1)S(1)}, bf16[1536,512]{1,0:T(8,128)(2,1)S(1)}, u32[]{:S(2)}, u32[]{:S(2)}) collective-permute-start(bf16[1536,512]{1,0:T(8,128)(2,1)S(1)} %get-tuple-element.78), channel_id=1, source_target_pairs={{32,0},{9,1},{34,2},{11,3},{36,4},{13,5},{38,6},{15,7},{40,8},{17,... | collective-permute-start | bytes 4718600 | tf_op jit(solution)/shard_map/ppermute | solution.py:55
  22.2 1.5 collective-permute-start.6
  23.7 1.7 %collective-permute-start.5 = (bf16[512,512]{1,0:T(8,128)(2,1)S(1)}, bf16[512,512]{1,0:T(8,128)(2,1)S(1)}, u32[]{:S(2)}, u32[]{:S(2)}) collective-permute-start(bf16[512,512]{1,0:T(8,128)(2,1)S(1)} %get-tuple-element.71), channel_id=1, source_target_pairs={{8,0},{33,1},{10,2},{35,3},{12,4},{37,5},{14,6},{39,7},{16,8},{41,... | collective-permute-start | bytes 1572872 | tf_op jit(solution)/shard_map/ppermute | solution.py:55
  25.5 0.3 copy.8
  25.8 3.9 %sort_tiles.1.refs_0_ = s32[608]{0:T(1024)S(1)} custom-call(s32[240]{0:T(256)S(1)} %get-tuple-element.69.codes, s32[240]{0:T(256)S(1)} %bitcast.11, s32[1]{0:T(128)S(6)} %copy.9.count), custom_call_target="tpu_custom_call" | custom-call | tf_op jit(solution)/shard_map/sort_tiles/pallas_call | solution.py:163
  29.8 0.6 pick_near.2.refs_3_
  30.4 3.5 %near.2.refs_5_ = f32[1024,512]{1,0:T(8,128)S(1)} custom-call(s32[608]{0:T(1024)S(1)} %sort_tiles.1.refs_0_, s32[193,5,128]{2,1,0:T(8,128)S(1)} %concatenate.3.refs_1_, bf16[1040,512]{1,0:T(8,128)(2,1)S(1)} %first.1.refs_2_.own, bf16[1024,512]{1,0:T(8,128)(2,1)S(1)} %pick_near.2.refs_3_), custom_call_target="tpu_custom_call" | custom-call | tf_op jit(solution)/shard_map/near/pallas_call | solution.py:427
  34.0 4.6 %collective-permute-done.5.low2 = bf16[512,512]{1,0:T(8,128)(2,1)S(1)} collective-permute-done((bf16[512,512]{1,0:T(8,128)(2,1)S(1)}, bf16[512,512]{1,0:T(8,128)(2,1)S(1)}, u32[]{:S(2)}, u32[]{:S(2)}) %collective-permute-start.5) | collective-permute-done | bytes 524320 | tf_op jit(solution)/shard_map/ppermute | solution.py:55
  38.6 0.9 pick_late.2
  39.5 2.3 %collective-permute-start.9 = (f32[8,512]{1,0:T(8,128)S(1)}, f32[8,512]{1,0:T(8,128)S(1)}, u32[]{:S(2)}, u32[]{:S(2)}) collective-permute-start(f32[8,512]{1,0:T(8,128)S(1)} %get-tuple-element.75), channel_id=1, source_target_pairs={{64,0},{17,1},{66,2},{19,3},{68,4},{21,5},{70,6},{23,7},{72,8},{25... | collective-permute-start | bytes 49160 | tf_op jit(solution)/shard_map/ppermute | solution.py:55
  41.8 1.9 %collective-permute-start.8 = (f32[8,512]{1,0:T(8,128)S(1)}, f32[8,512]{1,0:T(8,128)S(1)}, u32[]{:S(2)}, u32[]{:S(2)}) collective-permute-start(f32[8,512]{1,0:T(8,128)S(1)} %get-tuple-element.75), channel_id=1, source_target_pairs={{96,0},{25,1},{98,2},{27,3},{100,4},{29,5},{102,6},{31,7},{104,8},... | collective-permute-start | bytes 49160 | tf_op jit(solution)/shard_map/ppermute | solution.py:55
  43.7 1.3 collective-permute-start.7
  45.1 3.3 %collective-permute-done.9 = f32[8,512]{1,0:T(8,128)S(1)} collective-permute-done((f32[8,512]{1,0:T(8,128)S(1)}, f32[8,512]{1,0:T(8,128)S(1)}, u32[]{:S(2)}, u32[]{:S(2)}) %collective-permute-start.9) | collective-permute-done | bytes 16416 | tf_op jit(solution)/shard_map/ppermute | solution.py:55
  48.4 0.7 collective-permute-start.12
  49.1 1.7 %collective-permute-start.16 = (bf16[512,512]{1,0:T(8,128)(2,1)S(1)}, bf16[512,512]{1,0:T(8,128)(2,1)S(1)}, u32[]{:S(2)}, u32[]{:S(2)}) collective-permute-start(bf16[512,512]{1,0:T(8,128)(2,1)S(1)} %get-tuple-element.92), channel_id=1, source_target_pairs={{32,0},{9,1},{34,2},{11,3},{36,4},{13,5},{38,6},{15,7},{40,8},{17,... | collective-permute-start | bytes 1572872 | tf_op jit(solution)/shard_map/ppermute | solution.py:55
  50.8 0.3 collective-permute-start.17
  51.1 2.9 %collective-permute-start.18 = (bf16[512,512]{1,0:T(8,128)(2,1)S(1)}, bf16[512,512]{1,0:T(8,128)(2,1)S(1)}, u32[]{:S(2)}, u32[]{:S(2)}) collective-permute-start(bf16[512,512]{1,0:T(8,128)(2,1)S(1)} %get-tuple-element.97), channel_id=1, source_target_pairs={{64,0},{17,1},{66,2},{19,3},{68,4},{21,5},{70,6},{23,7},{72,8},{25... | collective-permute-start | bytes 1572872 | tf_op jit(solution)/shard_map/ppermute | solution.py:55
  54.0 4.7 %sides_1.2.refs_4_ = f32[1024,512]{1,0:T(8,128)S(1)} custom-call(s32[608]{0:T(1024)S(1)} %sort_tiles.1.refs_0_, s32[193,5,128]{2,1,0:T(8,128)S(1)} %concatenate.3.refs_1_, bf16[1040,512]{1,0:T(8,128)(2,1)S(1)} %first.1.refs_2_.own, bf16[1536,512]{1,0:T(8,128)(2,1)S(1)} %collective-permute-done.10.refs_3_, bf16[512,512]{1,0:T(8,128)(2,1)S(1)} %get-tuple-element.83.refs_4_, ...), custom_call_target="tpu_custom_call" | custom-call | tf_op jit(solution)/shard_map/sides_1/pallas_call | solution.py:427
  58.9 4.2 %sides_3.2.refs_4_ = f32[1024,512]{1,0:T(8,128)S(1)} custom-call(s32[608]{0:T(1024)S(1)} %sort_tiles.1.refs_0_, s32[193,5,128]{2,1,0:T(8,128)S(1)} %concatenate.3.refs_1_, bf16[1040,512]{1,0:T(8,128)(2,1)S(1)} %first.1.refs_2_.own, bf16[1536,512]{1,0:T(8,128)(2,1)S(1)} %collective-permute-done.11.refs_3_, f32[1024,512]{1,0:T(8,128)S(1)} %sides_1.2.refs_4_), custom_call_target="tpu_custom_call" | custom-call | tf_op jit(solution)/shard_map/sides_3/pallas_call | solution.py:427
  63.1 3.1 %collective-permute-start.15 = (f32[8,512]{1,0:T(8,128)S(1)}, f32[8,512]{1,0:T(8,128)S(1)}, u32[]{:S(2)}, u32[]{:S(2)}) collective-permute-start(f32[8,512]{1,0:T(8,128)S(1)} %add.42), channel_id=1, source_target_pairs={{0,4},{2,6},{4,0},{6,2},{1,5},{3,7},{5,1},{7,3},{8,12},{10,14},{12... | collective-permute-start | bytes 49160 | tf_op jit(solution)/shard_map/ppermute | solution.py:59
  66.2 4.3 %collective-permute-done.12.refs_3_ = bf16[1536,512]{1,0:T(8,128)(2,1)S(1)} collective-permute-done((bf16[1536,512]{1,0:T(8,128)(2,1)S(1)}, bf16[1536,512]{1,0:T(8,128)(2,1)S(1)}, u32[]{:S(2)}, u32[]{:S(2)}) %collective-permute-start.12) | collective-permute-done | bytes 1572896 | tf_op jit(solution)/shard_map/ppermute | solution.py:55
  70.5 3.5 %across.2.refs_5_ = f32[1024,512]{1,0:T(8,128)S(1)} custom-call(s32[608]{0:T(1024)S(1)} %sort_tiles.1.refs_0_, s32[193,5,128]{2,1,0:T(8,128)S(1)} %concatenate.3.refs_1_, bf16[1040,512]{1,0:T(8,128)(2,1)S(1)} %first.1.refs_2_.own, bf16[1536,512]{1,0:T(8,128)(2,1)S(1)} %collective-permute-done.12.refs_3_, f32[1024,512]{1,0:T(8,128)S(1)} %sides_3.2.refs_4_), custom_call_target="tpu_custom_call" | custom-call | tf_op jit(solution)/shard_map/across/pallas_call | solution.py:427
  74.0 0.9 collective-permute-done.16.refs_3_
  74.9 1.0 collective-permute-done.17.refs_4_
  76.0 2.7 %late.2.refs_4_ = f32[1024,512]{1,0:T(8,128)S(1)} custom-call(s32[608]{0:T(1024)S(1)} %sort_tiles.1.refs_0_, s32[193,5,128]{2,1,0:T(8,128)S(1)} %concatenate.3.refs_1_, bf16[1040,512]{1,0:T(8,128)(2,1)S(1)} %first.1.refs_2_.own, bf16[512,512]{1,0:T(8,128)(2,1)S(1)} %collective-permute-done.16.refs_3_, bf16[512,512]{1,0:T(8,128)(2,1)S(1)} %collective-permute-done.17.refs_4_, ...), custom_call_target="tpu_custom_call" | custom-call | tf_op jit(solution)/shard_map/late/pallas_call | solution.py:427
  78.7 2.9 %collective-permute-done.18.refs_3_ = bf16[512,512]{1,0:T(8,128)(2,1)S(1)} collective-permute-done((bf16[512,512]{1,0:T(8,128)(2,1)S(1)}, bf16[512,512]{1,0:T(8,128)(2,1)S(1)}, u32[]{:S(2)}, u32[]{:S(2)}) %collective-permute-start.18) | collective-permute-done | bytes 524320 | tf_op jit(solution)/shard_map/ppermute | solution.py:55
  81.6 2.6 %last.2 = (f32[1024,512]{1,0:T(8,128)S(1)}, bf16[1040,512]{1,0:T(8,128)(2,1)S(1)}) custom-call(s32[608]{0:T(1024)S(1)} %sort_tiles.1.refs_0_, s32[193,5,128]{2,1,0:T(8,128)S(1)} %concatenate.3.refs_1_, bf16[1040,512]{1,0:T(8,128)(2,1)S(1)} %first.1.refs_2_.own, bf16[512,512]{1,0:T(8,128)(2,1)S(1)} %collective-permute-done.18.refs_3_, ...), custom_call_target="tpu_custom_call" | custom-call | tf_op jit(solution)/shard_map/last/pallas_call | solution.py:427
  84.3 3.8 %collective-permute-start.19 = (bf16[1040,512]{1,0:T(8,128)(2,1)S(1)}, bf16[1040,512]{1,0:T(8,128)(2,1)S(1)}, u32[]{:S(2)}, u32[]{:S(2)}) collective-permute-start(bf16[1040,512]{1,0:T(8,128)(2,1)S(1)} %get-tuple-element.101.refs_2_.own), channel_id=1, source_target_pairs={{8,0},{33,1},{10,2},{35,3},{12,4},{37,5},{14,6},{39,7},{16,8},{41,... | collective-permute-start | bytes 3194888 | tf_op jit(solution)/shard_map/ppermute | solution.py:55
  88.1 12.9 %collective-permute-done.20.far3 = bf16[1040,512]{1,0:T(8,128)(2,1)S(1)} collective-permute-done((bf16[1040,512]{1,0:T(8,128)(2,1)S(1)}, bf16[1040,512]{1,0:T(8,128)(2,1)S(1)}, u32[]{:S(2)}, u32[]{:S(2)}) %collective-permute-start.20) | collective-permute-done | bytes 1064992 | tf_op jit(solution)/shard_map/ppermute | solution.py:55
  100.9 0.8 collective-permute-done.19.far1
  101.8 0.8 pick_early.3
  102.6 0.4 collective-permute-start.26
  103.0 1.7 %collective-permute-start.27 = (bf16[1536,512]{1,0:T(8,128)(2,1)S(1)}, bf16[1536,512]{1,0:T(8,128)(2,1)S(1)}, u32[]{:S(2)}, u32[]{:S(2)}) collective-permute-start(bf16[1536,512]{1,0:T(8,128)(2,1)S(1)} %get-tuple-element.110), channel_id=1, source_target_pairs={{96,0},{25,1},{98,2},{27,3},{100,4},{29,5},{102,6},{31,7},{104,8},... | collective-permute-start | bytes 4718600 | tf_op jit(solution)/shard_map/ppermute | solution.py:55
  104.7 2.5 %collective-permute-start.22 = (bf16[528,512]{1,0:T(8,128)(2,1)S(1)}, bf16[528,512]{1,0:T(8,128)(2,1)S(1)}, u32[]{:S(2)}, u32[]{:S(2)}) collective-permute-start(bf16[528,512]{1,0:T(8,128)(2,1)S(1)} %get-tuple-element.103), channel_id=1, source_target_pairs={{24,0},{97,1},{26,2},{99,3},{28,4},{101,5},{30,6},{103,7},{0,8},{1... | collective-permute-start | bytes 1622024 | tf_op jit(solution)/shard_map/ppermute | solution.py:55
  107.2 1.2 collective-permute-start.21
  108.4 0.6 pick_near.3.refs_3_
  109.0 3.4 %near.3.refs_5_ = f32[1024,512]{1,0:T(8,128)S(1)} custom-call(s32[608]{0:T(1024)S(1)} %sort_tiles.1.refs_0_, s32[193,5,128]{2,1,0:T(8,128)S(1)} %concatenate.3.refs_1_, bf16[1040,512]{1,0:T(8,128)(2,1)S(1)} %get-tuple-element.101.refs_2_.own, bf16[1024,512]{1,0:T(8,128)(2,1)S(1)} %pick_near.3.refs_3_), custom_call_target="tpu_custom_call" | custom-call | tf_op jit(solution)/shard_map/near/pallas_call | solution.py:427
  112.4 9.9 %collective-permute-done.21.low2 = bf16[512,512]{1,0:T(8,128)(2,1)S(1)} collective-permute-done((bf16[512,512]{1,0:T(8,128)(2,1)S(1)}, bf16[512,512]{1,0:T(8,128)(2,1)S(1)}, u32[]{:S(2)}, u32[]{:S(2)}) %collective-permute-start.21) | collective-permute-done | bytes 524320 | tf_op jit(solution)/shard_map/ppermute | solution.py:55
  122.4 0.9 pick_late.3
  123.3 2.1 %collective-permute-start.24 = (f32[8,512]{1,0:T(8,128)S(1)}, f32[8,512]{1,0:T(8,128)S(1)}, u32[]{:S(2)}, u32[]{:S(2)}) collective-permute-start(f32[8,512]{1,0:T(8,128)S(1)} %get-tuple-element.106), channel_id=1, source_target_pairs={{96,0},{25,1},{98,2},{27,3},{100,4},{29,5},{102,6},{31,7},{104,8},... | collective-permute-start | bytes 49160 | tf_op jit(solution)/shard_map/ppermute | solution.py:55
  125.5 1.2 collective-permute-start.23
  126.7 1.9 %collective-permute-done.25 = f32[8,512]{1,0:T(8,128)S(1)} collective-permute-done((f32[8,512]{1,0:T(8,128)S(1)}, f32[8,512]{1,0:T(8,128)S(1)}, u32[]{:S(2)}, u32[]{:S(2)}) %collective-permute-start.25) | collective-permute-done | bytes 16416 | tf_op jit(solution)/shard_map/ppermute | solution.py:55
  128.6 0.6 collective-permute-done.23
  129.2 2.0 %collective-permute-start.28 = (bf16[1536,512]{1,0:T(8,128)(2,1)S(1)}, bf16[1536,512]{1,0:T(8,128)(2,1)S(1)}, u32[]{:S(2)}, u32[]{:S(2)}) collective-permute-start(bf16[1536,512]{1,0:T(8,128)(2,1)S(1)} %get-tuple-element.111), channel_id=1, source_target_pairs={{64,0},{17,1},{66,2},{19,3},{68,4},{21,5},{70,6},{23,7},{72,8},{25... | collective-permute-start | bytes 4718600 | tf_op jit(solution)/shard_map/ppermute | solution.py:55
  131.2 2.0 %collective-permute-start.32 = (bf16[512,512]{1,0:T(8,128)(2,1)S(1)}, bf16[512,512]{1,0:T(8,128)(2,1)S(1)}, u32[]{:S(2)}, u32[]{:S(2)}) collective-permute-start(bf16[512,512]{1,0:T(8,128)(2,1)S(1)} %get-tuple-element.123), channel_id=1, source_target_pairs={{32,0},{9,1},{34,2},{11,3},{36,4},{13,5},{38,6},{15,7},{40,8},{17,... | collective-permute-start | bytes 1572872 | tf_op jit(solution)/shard_map/ppermute | solution.py:55
  133.3 1.5 collective-permute-start.34
  134.8 4.7 %sides_1.3.refs_4_ = f32[1024,512]{1,0:T(8,128)S(1)} custom-call(s32[608]{0:T(1024)S(1)} %sort_tiles.1.refs_0_, s32[193,5,128]{2,1,0:T(8,128)S(1)} %concatenate.3.refs_1_, bf16[1040,512]{1,0:T(8,128)(2,1)S(1)} %get-tuple-element.101.refs_2_.own, bf16[1536,512]{1,0:T(8,128)(2,1)S(1)} %collective-permute-done.26.refs_3_, ...), custom_call_target="tpu_custom_call" | custom-call | tf_op jit(solution)/shard_map/sides_1/pallas_call | solution.py:427
  139.6 4.2 %sides_3.3.refs_4_ = f32[1024,512]{1,0:T(8,128)S(1)} custom-call(s32[608]{0:T(1024)S(1)} %sort_tiles.1.refs_0_, s32[193,5,128]{2,1,0:T(8,128)S(1)} %concatenate.3.refs_1_, bf16[1040,512]{1,0:T(8,128)(2,1)S(1)} %get-tuple-element.101.refs_2_.own, bf16[1536,512]{1,0:T(8,128)(2,1)S(1)} %collective-permute-done.27.refs_3_, f32[1024,512]{1,0:T(8,128)S(1)} %sides_1.3.refs_4_), custom_call_target="tpu_custom_call" | custom-call | tf_op jit(solution)/shard_map/sides_3/pallas_call | solution.py:427
  143.8 2.5 %collective-permute-start.31 = (f32[8,512]{1,0:T(8,128)S(1)}, f32[8,512]{1,0:T(8,128)S(1)}, u32[]{:S(2)}, u32[]{:S(2)}) collective-permute-start(f32[8,512]{1,0:T(8,128)S(1)} %add.48), channel_id=1, source_target_pairs={{0,4},{2,6},{4,0},{6,2},{1,5},{3,7},{5,1},{7,3},{8,12},{10,14},{12... | collective-permute-start | bytes 49160 | tf_op jit(solution)/shard_map/ppermute | solution.py:59
  146.3 5.0 %collective-permute-done.28.refs_3_ = bf16[1536,512]{1,0:T(8,128)(2,1)S(1)} collective-permute-done((bf16[1536,512]{1,0:T(8,128)(2,1)S(1)}, bf16[1536,512]{1,0:T(8,128)(2,1)S(1)}, u32[]{:S(2)}, u32[]{:S(2)}) %collective-permute-start.28) | collective-permute-done | bytes 1572896 | tf_op jit(solution)/shard_map/ppermute | solution.py:55
  151.3 3.4 %across.3.refs_5_ = f32[1024,512]{1,0:T(8,128)S(1)} custom-call(s32[608]{0:T(1024)S(1)} %sort_tiles.1.refs_0_, s32[193,5,128]{2,1,0:T(8,128)S(1)} %concatenate.3.refs_1_, bf16[1040,512]{1,0:T(8,128)(2,1)S(1)} %get-tuple-element.101.refs_2_.own, bf16[1536,512]{1,0:T(8,128)(2,1)S(1)} %collective-permute-done.28.refs_3_, f32[1024,512]{1,0:T(8,128)S(1)} %sides_3.3.refs_4_), custom_call_target="tpu_custom_call" | custom-call | tf_op jit(solution)/shard_map/across/pallas_call | solution.py:427
  154.7 1.8 %collective-permute-done.32.refs_3_ = bf16[512,512]{1,0:T(8,128)(2,1)S(1)} collective-permute-done((bf16[512,512]{1,0:T(8,128)(2,1)S(1)}, bf16[512,512]{1,0:T(8,128)(2,1)S(1)}, u32[]{:S(2)}, u32[]{:S(2)}) %collective-permute-start.32) | collective-permute-done | bytes 524320 | tf_op jit(solution)/shard_map/ppermute | solution.py:55
  156.5 0.3 collective-permute-done.33.refs_4_
  156.8 2.5 %late.3.refs_4_ = f32[1024,512]{1,0:T(8,128)S(1)} custom-call(s32[608]{0:T(1024)S(1)} %sort_tiles.1.refs_0_, s32[193,5,128]{2,1,0:T(8,128)S(1)} %concatenate.3.refs_1_, bf16[1040,512]{1,0:T(8,128)(2,1)S(1)} %get-tuple-element.101.refs_2_.own, bf16[512,512]{1,0:T(8,128)(2,1)S(1)} %collective-permute-done.32.refs_3_, ...), custom_call_target="tpu_custom_call" | custom-call | tf_op jit(solution)/shard_map/late/pallas_call | solution.py:427
  159.3 3.1 %collective-permute-done.34.refs_3_ = bf16[512,512]{1,0:T(8,128)(2,1)S(1)} collective-permute-done((bf16[512,512]{1,0:T(8,128)(2,1)S(1)}, bf16[512,512]{1,0:T(8,128)(2,1)S(1)}, u32[]{:S(2)}, u32[]{:S(2)}) %collective-permute-start.34) | collective-permute-done | bytes 524320 | tf_op jit(solution)/shard_map/ppermute | solution.py:55
  162.4 3.5 %last.3 = f32[1024,512]{1,0:T(8,128)} custom-call(s32[608]{0:T(1024)S(1)} %sort_tiles.1.refs_0_, s32[193,5,128]{2,1,0:T(8,128)S(1)} %concatenate.3.refs_1_, bf16[1040,512]{1,0:T(8,128)(2,1)S(1)} %get-tuple-element.101.refs_2_.own, bf16[512,512]{1,0:T(8,128)(2,1)S(1)} %collective-permute-done.34.refs_3_, f32[1024,512]{1,0:T(8,128)S(1)} %late.3.refs_4_, ...), custom_call_target="tpu_custom_call" | custom-call | tf_op jit(solution)/shard_map/last/pallas_call | solution.py:427
  (54 shorter events, 1.1 us)
Async XLA Ops:
  0.0 1.6 copy-start
  1.6 4.2 %copy-start.2 = (s32[1024]{0:T(1024)S(1)}, s32[1024]{0:T(1024)}, u32[]{:S(2)}) copy-start(s32[1024]{0:T(1024)} %home.1) | copy-start | bytes 12292
  1.6 4.2 %copy-start.3 = (s32[1,240]{1,0:T(1,128)S(1)}, s32[1,240]{1,0:T(1,128)}, u32[]{:S(2)}) copy-start(s32[1,240]{1,0:T(1,128)} %param.8) | copy-start | bytes 2884
  1.6 4.2 %copy-start.4 = (s32[1,240]{1,0:T(1,128)S(1)}, s32[1,240]{1,0:T(1,128)}, u32[]{:S(2)}) copy-start(s32[1,240]{1,0:T(1,128)} %param.9) | copy-start | bytes 2884
  1.7 16.4 %collective-permute-start.4 = (bf16[1040,512]{1,0:T(8,128)(2,1)S(1)}, bf16[1040,512]{1,0:T(8,128)(2,1)S(1)}, u32[]{:S(2)}, u32[]{:S(2)}) collective-permute-start(bf16[1040,512]{1,0:T(8,128)(2,1)S(1)} %first.1.refs_2_.own), channel_id=1, source_target_pairs={{24,0},{97,1},{26,2},{99,3},{28,4},{101,5},{30,6},{103,7},{0,8},{1... | collective-permute-start | bytes 3194888 | tf_op jit(solution)/shard_map/ppermute | solution.py:55
  3.3 15.0 %collective-permute-start.3 = (bf16[1040,512]{1,0:T(8,128)(2,1)S(1)}, bf16[1040,512]{1,0:T(8,128)(2,1)S(1)}, u32[]{:S(2)}, u32[]{:S(2)}) collective-permute-start(bf16[1040,512]{1,0:T(8,128)(2,1)S(1)} %first.1.refs_2_.own), channel_id=1, source_target_pairs={{8,0},{33,1},{10,2},{35,3},{12,4},{37,5},{14,6},{39,7},{16,8},{41,... | collective-permute-start | bytes 3194888 | tf_op jit(solution)/shard_map/ppermute | solution.py:55
  9.7 4.7 %collective-permute-start.2 = (s32[16]{0:T(128)S(1)}, s32[16]{0:T(128)S(1)}, u32[]{:S(2)}, u32[]{:S(2)}) collective-permute-start(s32[16]{0:T(128)S(1)} %get-tuple-element.134), channel_id=1, source_target_pairs={{32,0},{9,1},{34,2},{11,3},{36,4},{13,5},{38,6},{15,7},{40,8},{17,... | collective-permute-start | bytes 200 | tf_op jit(solution)/shard_map/ppermute | solution.py:55
  13.0 5.0 %collective-permute-start.1 = (s32[16]{0:T(128)S(1)}, s32[16]{0:T(128)S(1)}, u32[]{:S(2)}, u32[]{:S(2)}) collective-permute-start(s32[16]{0:T(128)S(1)} %get-tuple-element.135), channel_id=1, source_target_pairs={{64,0},{17,1},{66,2},{19,3},{68,4},{21,5},{70,6},{23,7},{72,8},{25... | collective-permute-start | bytes 200 | tf_op jit(solution)/shard_map/ppermute | solution.py:55
  13.0 5.0 %collective-permute-start = (s32[16]{0:T(128)S(1)}, s32[16]{0:T(128)S(1)}, u32[]{:S(2)}, u32[]{:S(2)}) collective-permute-start(s32[16]{0:T(128)S(1)} %get-tuple-element.136), channel_id=1, source_target_pairs={{96,0},{25,1},{98,2},{27,3},{100,4},{29,5},{102,6},{31,7},{104,8},... | collective-permute-start | bytes 200 | tf_op jit(solution)/shard_map/ppermute | solution.py:55
  18.1 7.4 %copy-start.6 = (s32[192,5,128]{2,0,1:T(8,128)S(1)}, s32[192,5,128]{2,0,1:T(8,128)}, u32[]{:S(2)}) copy-start(s32[192,5,128]{2,0,1:T(8,128)} %param.13) | copy-start | bytes 1474564
  19.1 6.7 %copy-start.5 = (s32[1,240]{1,0:T(1,128)S(1)}, s32[1,240]{1,0:T(1,128)}, u32[]{:S(2)}) copy-start(s32[1,240]{1,0:T(1,128)} %param.10) | copy-start | bytes 2884
  19.1 29.2 %collective-permute-start.10 = (bf16[1536,512]{1,0:T(8,128)(2,1)S(1)}, bf16[1536,512]{1,0:T(8,128)(2,1)S(1)}, u32[]{:S(2)}, u32[]{:S(2)}) collective-permute-start(bf16[1536,512]{1,0:T(8,128)(2,1)S(1)} %get-tuple-element.78), channel_id=1, source_target_pairs={{32,0},{9,1},{34,2},{11,3},{36,4},{13,5},{38,6},{15,7},{40,8},{17,... | collective-permute-start | bytes 4718600 | tf_op jit(solution)/shard_map/ppermute | solution.py:55
  22.2 26.1 %collective-permute-start.11 = (bf16[1536,512]{1,0:T(8,128)(2,1)S(1)}, bf16[1536,512]{1,0:T(8,128)(2,1)S(1)}, u32[]{:S(2)}, u32[]{:S(2)}) collective-permute-start(bf16[1536,512]{1,0:T(8,128)(2,1)S(1)} %get-tuple-element.79), channel_id=1, source_target_pairs={{96,0},{25,1},{98,2},{27,3},{100,4},{29,5},{102,6},{31,7},{104,8},... | collective-permute-start | bytes 4718600 | tf_op jit(solution)/shard_map/ppermute | solution.py:55
  22.2 16.4 %collective-permute-start.6 = (bf16[528,512]{1,0:T(8,128)(2,1)S(1)}, bf16[528,512]{1,0:T(8,128)(2,1)S(1)}, u32[]{:S(2)}, u32[]{:S(2)}) collective-permute-start(bf16[528,512]{1,0:T(8,128)(2,1)S(1)} %get-tuple-element.72), channel_id=1, source_target_pairs={{24,0},{97,1},{26,2},{99,3},{28,4},{101,5},{30,6},{103,7},{0,8},{1... | collective-permute-start | bytes 1622024 | tf_op jit(solution)/shard_map/ppermute | solution.py:55
  23.7 14.9 %collective-permute-start.5 = (bf16[512,512]{1,0:T(8,128)(2,1)S(1)}, bf16[512,512]{1,0:T(8,128)(2,1)S(1)}, u32[]{:S(2)}, u32[]{:S(2)}) collective-permute-start(bf16[512,512]{1,0:T(8,128)(2,1)S(1)} %get-tuple-element.71), channel_id=1, source_target_pairs={{8,0},{33,1},{10,2},{35,3},{12,4},{37,5},{14,6},{39,7},{16,8},{41,... | collective-permute-start | bytes 1572872 | tf_op jit(solution)/shard_map/ppermute | solution.py:55
  39.5 8.8 %collective-permute-start.9 = (f32[8,512]{1,0:T(8,128)S(1)}, f32[8,512]{1,0:T(8,128)S(1)}, u32[]{:S(2)}, u32[]{:S(2)}) collective-permute-start(f32[8,512]{1,0:T(8,128)S(1)} %get-tuple-element.75), channel_id=1, source_target_pairs={{64,0},{17,1},{66,2},{19,3},{68,4},{21,5},{70,6},{23,7},{72,8},{25... | collective-permute-start | bytes 49160 | tf_op jit(solution)/shard_map/ppermute | solution.py:55
  41.8 6.5 %collective-permute-start.8 = (f32[8,512]{1,0:T(8,128)S(1)}, f32[8,512]{1,0:T(8,128)S(1)}, u32[]{:S(2)}, u32[]{:S(2)}) collective-permute-start(f32[8,512]{1,0:T(8,128)S(1)} %get-tuple-element.75), channel_id=1, source_target_pairs={{96,0},{25,1},{98,2},{27,3},{100,4},{29,5},{102,6},{31,7},{104,8},... | collective-permute-start | bytes 49160 | tf_op jit(solution)/shard_map/ppermute | solution.py:55
  43.7 4.6 %collective-permute-start.7 = (f32[8,512]{1,0:T(8,128)S(1)}, f32[8,512]{1,0:T(8,128)S(1)}, u32[]{:S(2)}, u32[]{:S(2)}) collective-permute-start(f32[8,512]{1,0:T(8,128)S(1)} %get-tuple-element.75), channel_id=1, source_target_pairs={{32,0},{9,1},{34,2},{11,3},{36,4},{13,5},{38,6},{15,7},{40,8},{17,... | collective-permute-start | bytes 49160 | tf_op jit(solution)/shard_map/ppermute | solution.py:55
  48.4 22.1 %collective-permute-start.12 = (bf16[1536,512]{1,0:T(8,128)(2,1)S(1)}, bf16[1536,512]{1,0:T(8,128)(2,1)S(1)}, u32[]{:S(2)}, u32[]{:S(2)}) collective-permute-start(bf16[1536,512]{1,0:T(8,128)(2,1)S(1)} %get-tuple-element.80), channel_id=1, source_target_pairs={{64,0},{17,1},{66,2},{19,3},{68,4},{21,5},{70,6},{23,7},{72,8},{25... | collective-permute-start | bytes 4718600 | tf_op jit(solution)/shard_map/ppermute | solution.py:55
  49.1 25.9 %collective-permute-start.16 = (bf16[512,512]{1,0:T(8,128)(2,1)S(1)}, bf16[512,512]{1,0:T(8,128)(2,1)S(1)}, u32[]{:S(2)}, u32[]{:S(2)}) collective-permute-start(bf16[512,512]{1,0:T(8,128)(2,1)S(1)} %get-tuple-element.92), channel_id=1, source_target_pairs={{32,0},{9,1},{34,2},{11,3},{36,4},{13,5},{38,6},{15,7},{40,8},{17,... | collective-permute-start | bytes 1572872 | tf_op jit(solution)/shard_map/ppermute | solution.py:55
  50.8 25.2 %collective-permute-start.17 = (bf16[512,512]{1,0:T(8,128)(2,1)S(1)}, bf16[512,512]{1,0:T(8,128)(2,1)S(1)}, u32[]{:S(2)}, u32[]{:S(2)}) collective-permute-start(bf16[512,512]{1,0:T(8,128)(2,1)S(1)} %get-tuple-element.93), channel_id=1, source_target_pairs={{96,0},{25,1},{98,2},{27,3},{100,4},{29,5},{102,6},{31,7},{104,8},... | collective-permute-start | bytes 1572872 | tf_op jit(solution)/shard_map/ppermute | solution.py:55
  51.1 30.5 %collective-permute-start.18 = (bf16[512,512]{1,0:T(8,128)(2,1)S(1)}, bf16[512,512]{1,0:T(8,128)(2,1)S(1)}, u32[]{:S(2)}, u32[]{:S(2)}) collective-permute-start(bf16[512,512]{1,0:T(8,128)(2,1)S(1)} %get-tuple-element.97), channel_id=1, source_target_pairs={{64,0},{17,1},{66,2},{19,3},{68,4},{21,5},{70,6},{23,7},{72,8},{25... | collective-permute-start | bytes 1572872 | tf_op jit(solution)/shard_map/ppermute | solution.py:55
  54.0 4.8 %collective-permute-start.13 = (f32[8,512]{1,0:T(8,128)S(1)}, f32[8,512]{1,0:T(8,128)S(1)}, u32[]{:S(2)}, u32[]{:S(2)}) collective-permute-start(f32[8,512]{1,0:T(8,128)S(1)} %add_add_fusion.1), channel_id=1, source_target_pairs={{0,1},{1,0},{2,3},{3,2},{4,5},{5,4},{6,7},{7,6},{8,9},{9,8},{10,11... | collective-permute-start | bytes 49160 | tf_op jit(solution)/shard_map/ppermute | solution.py:59
  58.8 4.3 %collective-permute-start.14 = (f32[8,512]{1,0:T(8,128)S(1)}, f32[8,512]{1,0:T(8,128)S(1)}, u32[]{:S(2)}, u32[]{:S(2)}) collective-permute-start(f32[8,512]{1,0:T(8,128)S(1)} %add.41), channel_id=1, source_target_pairs={{0,2},{2,0},{4,6},{6,4},{1,3},{3,1},{5,7},{7,5},{8,10},{10,8},{12,... | collective-permute-start | bytes 49160 | tf_op jit(solution)/shard_map/ppermute | solution.py:59
  63.1 12.9 %collective-permute-start.15 = (f32[8,512]{1,0:T(8,128)S(1)}, f32[8,512]{1,0:T(8,128)S(1)}, u32[]{:S(2)}, u32[]{:S(2)}) collective-permute-start(f32[8,512]{1,0:T(8,128)S(1)} %add.42), channel_id=1, source_target_pairs={{0,4},{2,6},{4,0},{6,2},{1,5},{3,7},{5,1},{7,3},{8,12},{10,14},{12... | collective-permute-start | bytes 49160 | tf_op jit(solution)/shard_map/ppermute | solution.py:59
  76.0 5.7 %copy-start.1 = (f32[1024,512]{1,0:T(8,128)S(1)}, f32[1024,512]{1,0:T(8,128)}, u32[]{:S(2)}) copy-start(f32[1024,512]{1,0:T(8,128)} %refs_5_.1) | copy-start | bytes 6291460
  84.2 16.7 %collective-permute-start.20 = (bf16[1040,512]{1,0:T(8,128)(2,1)S(1)}, bf16[1040,512]{1,0:T(8,128)(2,1)S(1)}, u32[]{:S(2)}, u32[]{:S(2)}) collective-permute-start(bf16[1040,512]{1,0:T(8,128)(2,1)S(1)} %get-tuple-element.101.refs_2_.own), channel_id=1, source_target_pairs={{24,0},{97,1},{26,2},{99,3},{28,4},{101,5},{30,6},{103,7},{0,8},{1... | collective-permute-start | bytes 3194888 | tf_op jit(solution)/shard_map/ppermute | solution.py:55
  84.3 17.5 %collective-permute-start.19 = (bf16[1040,512]{1,0:T(8,128)(2,1)S(1)}, bf16[1040,512]{1,0:T(8,128)(2,1)S(1)}, u32[]{:S(2)}, u32[]{:S(2)}) collective-permute-start(bf16[1040,512]{1,0:T(8,128)(2,1)S(1)} %get-tuple-element.101.refs_2_.own), channel_id=1, source_target_pairs={{8,0},{33,1},{10,2},{35,3},{12,4},{37,5},{14,6},{39,7},{16,8},{41,... | collective-permute-start | bytes 3194888 | tf_op jit(solution)/shard_map/ppermute | solution.py:55
  102.6 26.6 %collective-permute-start.26 = (bf16[1536,512]{1,0:T(8,128)(2,1)S(1)}, bf16[1536,512]{1,0:T(8,128)(2,1)S(1)}, u32[]{:S(2)}, u32[]{:S(2)}) collective-permute-start(bf16[1536,512]{1,0:T(8,128)(2,1)S(1)} %get-tuple-element.109), channel_id=1, source_target_pairs={{32,0},{9,1},{34,2},{11,3},{36,4},{13,5},{38,6},{15,7},{40,8},{17,... | collective-permute-start | bytes 4718600 | tf_op jit(solution)/shard_map/ppermute | solution.py:55
  103.0 26.2 %collective-permute-start.27 = (bf16[1536,512]{1,0:T(8,128)(2,1)S(1)}, bf16[1536,512]{1,0:T(8,128)(2,1)S(1)}, u32[]{:S(2)}, u32[]{:S(2)}) collective-permute-start(bf16[1536,512]{1,0:T(8,128)(2,1)S(1)} %get-tuple-element.110), channel_id=1, source_target_pairs={{96,0},{25,1},{98,2},{27,3},{100,4},{29,5},{102,6},{31,7},{104,8},... | collective-permute-start | bytes 4718600 | tf_op jit(solution)/shard_map/ppermute | solution.py:55
  104.7 17.6 %collective-permute-start.22 = (bf16[528,512]{1,0:T(8,128)(2,1)S(1)}, bf16[528,512]{1,0:T(8,128)(2,1)S(1)}, u32[]{:S(2)}, u32[]{:S(2)}) collective-permute-start(bf16[528,512]{1,0:T(8,128)(2,1)S(1)} %get-tuple-element.103), channel_id=1, source_target_pairs={{24,0},{97,1},{26,2},{99,3},{28,4},{101,5},{30,6},{103,7},{0,8},{1... | collective-permute-start | bytes 1622024 | tf_op jit(solution)/shard_map/ppermute | solution.py:55
  107.2 15.1 %collective-permute-start.21 = (bf16[512,512]{1,0:T(8,128)(2,1)S(1)}, bf16[512,512]{1,0:T(8,128)(2,1)S(1)}, u32[]{:S(2)}, u32[]{:S(2)}) collective-permute-start(bf16[512,512]{1,0:T(8,128)(2,1)S(1)} %get-tuple-element.102), channel_id=1, source_target_pairs={{8,0},{33,1},{10,2},{35,3},{12,4},{37,5},{14,6},{39,7},{16,8},{41,... | collective-permute-start | bytes 1572872 | tf_op jit(solution)/shard_map/ppermute | solution.py:55
  123.3 5.3 %collective-permute-start.25 = (f32[8,512]{1,0:T(8,128)S(1)}, f32[8,512]{1,0:T(8,128)S(1)}, u32[]{:S(2)}, u32[]{:S(2)}) collective-permute-start(f32[8,512]{1,0:T(8,128)S(1)} %get-tuple-element.106), channel_id=1, source_target_pairs={{64,0},{17,1},{66,2},{19,3},{68,4},{21,5},{70,6},{23,7},{72,8},{25... | collective-permute-start | bytes 49160 | tf_op jit(solution)/shard_map/ppermute | solution.py:55
  123.3 5.2 %collective-permute-start.24 = (f32[8,512]{1,0:T(8,128)S(1)}, f32[8,512]{1,0:T(8,128)S(1)}, u32[]{:S(2)}, u32[]{:S(2)}) collective-permute-start(f32[8,512]{1,0:T(8,128)S(1)} %get-tuple-element.106), channel_id=1, source_target_pairs={{96,0},{25,1},{98,2},{27,3},{100,4},{29,5},{102,6},{31,7},{104,8},... | collective-permute-start | bytes 49160 | tf_op jit(solution)/shard_map/ppermute | solution.py:55
  125.5 3.7 %collective-permute-start.23 = (f32[8,512]{1,0:T(8,128)S(1)}, f32[8,512]{1,0:T(8,128)S(1)}, u32[]{:S(2)}, u32[]{:S(2)}) collective-permute-start(f32[8,512]{1,0:T(8,128)S(1)} %get-tuple-element.106), channel_id=1, source_target_pairs={{32,0},{9,1},{34,2},{11,3},{36,4},{13,5},{38,6},{15,7},{40,8},{17,... | collective-permute-start | bytes 49160 | tf_op jit(solution)/shard_map/ppermute | solution.py:55
  129.2 22.0 %collective-permute-start.28 = (bf16[1536,512]{1,0:T(8,128)(2,1)S(1)}, bf16[1536,512]{1,0:T(8,128)(2,1)S(1)}, u32[]{:S(2)}, u32[]{:S(2)}) collective-permute-start(bf16[1536,512]{1,0:T(8,128)(2,1)S(1)} %get-tuple-element.111), channel_id=1, source_target_pairs={{64,0},{17,1},{66,2},{19,3},{68,4},{21,5},{70,6},{23,7},{72,8},{25... | collective-permute-start | bytes 4718600 | tf_op jit(solution)/shard_map/ppermute | solution.py:55
  131.2 25.3 %collective-permute-start.32 = (bf16[512,512]{1,0:T(8,128)(2,1)S(1)}, bf16[512,512]{1,0:T(8,128)(2,1)S(1)}, u32[]{:S(2)}, u32[]{:S(2)}) collective-permute-start(bf16[512,512]{1,0:T(8,128)(2,1)S(1)} %get-tuple-element.123), channel_id=1, source_target_pairs={{32,0},{9,1},{34,2},{11,3},{36,4},{13,5},{38,6},{15,7},{40,8},{17,... | collective-permute-start | bytes 1572872 | tf_op jit(solution)/shard_map/ppermute | solution.py:55
  133.2 23.5 %collective-permute-start.33 = (bf16[512,512]{1,0:T(8,128)(2,1)S(1)}, bf16[512,512]{1,0:T(8,128)(2,1)S(1)}, u32[]{:S(2)}, u32[]{:S(2)}) collective-permute-start(bf16[512,512]{1,0:T(8,128)(2,1)S(1)} %get-tuple-element.124), channel_id=1, source_target_pairs={{96,0},{25,1},{98,2},{27,3},{100,4},{29,5},{102,6},{31,7},{104,8},... | collective-permute-start | bytes 1572872 | tf_op jit(solution)/shard_map/ppermute | solution.py:55
  133.3 29.2 %collective-permute-start.34 = (bf16[512,512]{1,0:T(8,128)(2,1)S(1)}, bf16[512,512]{1,0:T(8,128)(2,1)S(1)}, u32[]{:S(2)}, u32[]{:S(2)}) collective-permute-start(bf16[512,512]{1,0:T(8,128)(2,1)S(1)} %get-tuple-element.128), channel_id=1, source_target_pairs={{64,0},{17,1},{66,2},{19,3},{68,4},{21,5},{70,6},{23,7},{72,8},{25... | collective-permute-start | bytes 1572872 | tf_op jit(solution)/shard_map/ppermute | solution.py:55
  134.8 4.7 %collective-permute-start.29 = (f32[8,512]{1,0:T(8,128)S(1)}, f32[8,512]{1,0:T(8,128)S(1)}, u32[]{:S(2)}, u32[]{:S(2)}) collective-permute-start(f32[8,512]{1,0:T(8,128)S(1)} %add_add_fusion), channel_id=1, source_target_pairs={{0,1},{1,0},{2,3},{3,2},{4,5},{5,4},{6,7},{7,6},{8,9},{9,8},{10,11... | collective-permute-start | bytes 49160 | tf_op jit(solution)/shard_map/ppermute | solution.py:59
  139.5 4.3 %collective-permute-start.30 = (f32[8,512]{1,0:T(8,128)S(1)}, f32[8,512]{1,0:T(8,128)S(1)}, u32[]{:S(2)}, u32[]{:S(2)}) collective-permute-start(f32[8,512]{1,0:T(8,128)S(1)} %add.47), channel_id=1, source_target_pairs={{0,2},{2,0},{4,6},{6,4},{1,3},{3,1},{5,7},{7,5},{8,10},{10,8},{12,... | collective-permute-start | bytes 49160 | tf_op jit(solution)/shard_map/ppermute | solution.py:59
  143.8 12.9 %collective-permute-start.31 = (f32[8,512]{1,0:T(8,128)S(1)}, f32[8,512]{1,0:T(8,128)S(1)}, u32[]{:S(2)}, u32[]{:S(2)}) collective-permute-start(f32[8,512]{1,0:T(8,128)S(1)} %add.48), channel_id=1, source_target_pairs={{0,4},{2,6},{4,0},{6,2},{1,5},{3,7},{5,1},{7,3},{8,12},{10,14},{12... | collective-permute-start | bytes 49160 | tf_op jit(solution)/shard_map/ppermute | solution.py:59
